TPU v7x, 128 devices: a whole 4x4x4 slice. The times are simulated.
128 devices in a mesh: replica: 8 (over z_hi, y), tensor: 16 (over x, z_lo, core).
Axes of the slice: x: 4, y: 4, z: 4 (z_hi: 2, z_lo: 2; z = z_hi * 2 + z_lo), core: 2. Of those that a mesh axis runs over, the one named last changes fastest.
Arguments:
- queries: bfloat16 [1024, 8192], P('replica', 'tensor'), may hold values from -200 to 200
- new_kv: bfloat16 [1024, 1024], P('replica'), may hold values from -8 to 8
- kv_pool: bfloat16 [1024, 64, 1024], P(('replica', 'tensor')), may hold values from -6 to 6
- anchor: int32 [8, 8], replicated, may hold values from 0 to 7, as said below
- page_table: int32 [64, 16], replicated, may hold values from 0 to 7, as said below
- prefix_len: int32 [64], replicated, may hold values from 1 to 1024, 32768 in all
- turn_rows: int32 [8, 8], replicated, may hold values from 1 to 32, 128 in all within a row
- out_weight: bfloat16 [8192, 16384], P('tensor', 'replica'), may hold values from -0.5 to 0.5
- residual: bfloat16 [1024, 16384], P(None, 'replica'), may hold values from -400 to 400
- norm_gain: bfloat16 [16384], P('replica'), may hold values from 0.099609375 to 1.8984375
- gate_up: bfloat16 [16384, 2, 26624], P('replica', None, 'tensor'), may hold values from -0.046875 to 0.046875
Outputs:
- hidden: bfloat16 [1024, 26624], P('replica', 'tensor')
Inputs may be any that keep to these rules, and one draw needn't show every extreme that they name: Slot j of new replica d holds session anchor[d, j] of old replica j; for each old replica, the 8 slots that come from it name each of its 8 sessions exactly once. `page_table`: row o * 8 + s lists the pages of session s of old replica o: entry k is a local page index on device k of that replica's 16 tensor devices, whose pages are numbered (o * 16 + k) * 8 + index in kv_pool; on each device the 8 sessions use distinct pages. `prefix_len`: indexed by d * 8 + j for slot j of new replica d. `turn_rows`: each replica's entries sum to 128.
All inputs are finite; a program needn't handle non-finite values.
Results may differ from a plain program's by a relative error of at most 0.0064.
Values may be sent and summed in bfloat16 or wider, within the bound.
A program may use at most 128 MiB of HBM per device.

v0:
```python
import jax
import jax.numpy as jnp
import numpy as np
from jax import lax
from jax.sharding import PartitionSpec as P

D = 16384
HD = 128
HEADS = 64
KVH = 4
PAGE = 64
SHARE = 1
ROWS = 128
GROUP = 16


EPSILON = 1e-05


def per_device(
    queries,
    new_kv,
    kv_pool,
    anchor,
    page_table,
    prefix_len,
    turn_rows,
    out_weight,
    residual,
    norm_gain,
    gate_up,
):
    replicas = lax.axis_size("replica")
    tensors = lax.axis_size("tensor")
    replica_idx = lax.axis_index("replica")
    tensor_idx = lax.axis_index("tensor")
    sessions = SHARE * replicas
    heads_local = HEADS // tensors
    pair_width = 2 * HD
    cached_len = tensors * PAGE
    owner_head = np.arange(tensors) * heads_local // GROUP
    from_here = lax.dynamic_slice_in_dim(anchor, replica_idx * SHARE, SHARE, 1)
    table_rows = lax.dynamic_slice_in_dim(page_table, replica_idx * sessions, sessions, 0)
    my_column = lax.dynamic_slice_in_dim(table_rows, tensor_idx, 1, 1)[:, 0]
    page_index = jnp.take(my_column, from_here.reshape(-1), axis=0)
    chosen = jnp.take(kv_pool, page_index, axis=0).reshape(replicas, SHARE, PAGE, KVH, pair_width)
    outgoing = jnp.take(chosen, owner_head, axis=3)
    outgoing = jnp.transpose(outgoing, (0, 3, 1, 2, 4)).reshape(
        replicas * tensors, SHARE, PAGE, pair_width
    )
    arrived = lax.all_to_all(
        outgoing, ("replica", "tensor"), split_axis=0, concat_axis=0, tiled=True
    )
    arrived = arrived.reshape(replicas, tensors, SHARE, PAGE, pair_width)
    prefix_blocks = jnp.transpose(arrived, (0, 2, 1, 3, 4)).reshape(
        sessions, cached_len, pair_width
    )
    kv_group = tensor_idx * heads_local // GROUP
    fresh_pair = lax.dynamic_slice_in_dim(new_kv, kv_group * pair_width, pair_width, 1)
    rows_here = queries.shape[0]
    slot_rows = ROWS // 4
    query_heads = queries.reshape(rows_here, heads_local, HD)
    counts = lax.dynamic_slice_in_dim(turn_rows, replica_idx, 1, 0)[0]
    bounds = jnp.cumsum(counts, dtype=jnp.int32)
    starts = bounds - counts
    row_ids = jnp.arange(rows_here, dtype=jnp.int32)
    row_slot = jnp.sum(
        (row_ids[:, None] >= bounds[None, :]).astype(jnp.int32), axis=1, dtype=jnp.int32
    )
    offsets = jnp.arange(slot_rows, dtype=jnp.int32)
    padded_index = jnp.minimum(starts[:, None] + offsets[None, :], rows_here - 1).reshape(-1)
    slot_queries = jnp.take(query_heads, padded_index, axis=0).reshape(
        sessions, slot_rows, heads_local, HD
    )
    slot_fresh = jnp.take(fresh_pair, padded_index, axis=0).reshape(sessions, slot_rows, pair_width)
    lengths = lax.dynamic_slice_in_dim(prefix_len, replica_idx * sessions, sessions, 0)
    key_pos = jnp.arange(cached_len, dtype=jnp.int32)
    prefix_mask = (key_pos[None, :] < lengths[:, None])[:, None, :]
    fresh_mask = (offsets[None, None, :] <= offsets[None, :, None]) & (
        offsets[None, None, :] < counts[:, None, None]
    )
    score_scale = HD ** (-0.5)
    prefix_scores = (
        jnp.einsum(
            "smhd,skd->hsmk",
            slot_queries,
            prefix_blocks[:, :, :HD],
            preferred_element_type=jnp.float32,
        )
        * score_scale
    )
    fresh_scores = (
        jnp.einsum(
            "smhd,snd->hsmn",
            slot_queries,
            slot_fresh[:, :, :HD],
            preferred_element_type=jnp.float32,
        )
        * score_scale
    )
    prefix_scores = jnp.where(prefix_mask[None], prefix_scores, -jnp.inf)
    fresh_scores = jnp.where(fresh_mask[None], fresh_scores, -jnp.inf)
    row_peak = jnp.maximum(jnp.max(prefix_scores, axis=3), jnp.max(fresh_scores, axis=3))
    prefix_weights = jnp.exp(prefix_scores - row_peak[..., None])
    fresh_weights = jnp.exp(fresh_scores - row_peak[..., None])
    denominator = jnp.sum(prefix_weights, axis=3) + jnp.sum(fresh_weights, axis=3)
    mixed_values = jnp.einsum(
        "hsmk,skd->smhd",
        prefix_weights.astype(jnp.bfloat16),
        prefix_blocks[:, :, HD:],
        preferred_element_type=jnp.float32,
    )
    mixed_values = mixed_values + jnp.einsum(
        "hsmn,snd->smhd",
        fresh_weights.astype(jnp.bfloat16),
        slot_fresh[:, :, HD:],
        preferred_element_type=jnp.float32,
    )
    slot_attended = (mixed_values / jnp.transpose(denominator, (1, 2, 0))[..., None]).astype(
        jnp.bfloat16
    )
    slot_attended = slot_attended.reshape(sessions * slot_rows, heads_local * HD)
    back_index = row_slot * slot_rows + row_ids - jnp.take(starts, row_slot, axis=0)
    attended = jnp.take(slot_attended, back_index, axis=0)
    partial_out = jnp.dot(
        lax.all_gather(attended, "replica", axis=0, tiled=True),
        out_weight,
        preferred_element_type=jnp.float32,
    )
    weights_local = gate_up.reshape(gate_up.shape[0], 2 * gate_up.shape[2])
    gain_row = norm_gain.astype(jnp.float32)
    carried = residual.astype(jnp.float32) + lax.psum(partial_out, "tensor")
    squares = lax.psum(jnp.sum(carried * carried, axis=1), "replica")
    normed = (carried * lax.rsqrt(squares / D + EPSILON)[:, None] * gain_row[None, :]).astype(
        jnp.bfloat16
    )
    summed = lax.psum_scatter(
        jnp.dot(normed, weights_local, preferred_element_type=jnp.float32),
        "replica",
        scatter_dimension=0,
        tiled=True,
    )
    paired = summed.reshape(rows_here, 2, gate_up.shape[2])
    return (jax.nn.silu(paired[:, 0, :]) * paired[:, 1, :]).astype(jnp.bfloat16)


def solution(mesh):
    placed = (
        P("replica", "tensor"),
        P("replica", None),
        P(("replica", "tensor"), None, None),
        P(),
        P(),
        P(),
        P(),
        P("tensor", "replica"),
        P(None, "replica"),
        P("replica"),
        P("replica", None, "tensor"),
    )
    return jax.shard_map(
        per_device, mesh=mesh, in_specs=placed, out_specs=P("replica", "tensor"), check_vma=False
    )
```

profile of v0, /device:TPU:1, one launch (start us, length us, event | category | flops | bytes accessed | tf_op | source)
XLA Modules:
  0.0 568.2 jit_solution(5678871009920733186)
XLA Ops:
  6.5 0.9 constant_dynamic-slice_fusion
  7.6 0.8 dynamic-slice_bitcast_fusion
  9.7 1.8 gather_fusion.1
  11.5 1.6 gather.42
  13.1 1.4 fusion.18
  14.5 2.8 gather_fusion.2
  17.3 4.7 copy.48
  22.0 11.9 %all-to-all-start = ((bf16[128,1,64,256]{3,2,1,0:T(8,128)(2,1)}), bf16[128,1,64,256]{3,2,1,0:T(8,128)(2,1)}, u32[]{:S(2)}, u32[]{:S(2)}) async-start(bf16[128,1,64,256]{3,2,1,0:T(8,128)(2,1)} %bitcast.135), calls=%async_computation | async-start | bytes 8388608 | tf_op jit(solution)/shard_map/all_to_all | solution.py:51
  34.1 0.7 fusion.33
  35.0 0.7 bitcast_subtract_fusion.1
  35.9 0.9 constant_dynamic-slice_fusion.1
  36.7 1.1 gather_fusion.4
  37.9 1.0 gather_fusion.3
  38.9 0.7 fusion.39
  39.7 4.9 compare_and_fusion.1
  45.7 40.2 %all-to-all-done = bf16[128,1,64,256]{3,2,1,0:T(8,128)(2,1)} async-done(((bf16[128,1,64,256]{3,2,1,0:T(8,128)(2,1)}), bf16[128,1,64,256]{3,2,1,0:T(8,128)(2,1)}, u32[]{:S(2)}, u32[]{:S(2)}) %all-to-all-start) | async-done | bytes 4194336 | tf_op jit(solution)/shard_map/all_to_all | solution.py:51
  85.8 2.4 bitcast_reduce_fusion
  88.3 2.7 fusion.6
  90.9 1.0 fusion.4
  92.7 0.8 gather_fusion.5
  93.5 0.7 broadcast_select_fusion.1
  94.3 46.5 %all-gather.2.cloned.1.call-done = bf16[1024,512]{1,0:T(8,128)(2,1)} async-done(((bf16[128,512]{1,0:T(8,128)(2,1)}), bf16[1024,512]{1,0:T(8,128)(2,1)}) %all-gather.2.cloned.1.call-update) | async-done | bytes 1048592 | tf_op jit(solution)/shard_map/all_gather | solution.py:126
  140.8 6.8 %fusion.41 = f32[1024,2048]{1,0:T(8,128)} fusion(bf16[1024,512]{1,0:T(8,128)(2,1)} %all-gather.2.cloned.1.call-done, bf16[512,2048]{1,0:T(8,128)(2,1)S(1)} %copy-done), kind=kOutput, calls=%fused_computation.105 | convolution fusion | flops 2147483648 | bytes 11534336 | tf_op jit(solution)/shard_map/dot_general | solution.py:125
  148.4 14.3 %copy.66 = bf16[256,8,2,1664]{3,1,2,0:T(8,128)(2,1)} copy(bf16[256,8,2,1664]{3,2,1,0:T(2,128)(2,1)} %bitcast.137) | data formatting | bytes 27262976
  162.7 180.5 %all-reduce.2.cloned.1.call-done = f32[1024,2048]{1,0:T(8,128)} async-done(((f32[1024,2048]{1,0:T(8,128)}), f32[1024,2048]{1,0:T(8,128)}) %all-reduce.2.cloned.1.call-update) | async-done | bytes 8388624 | tf_op jit(solution)/shard_map/psum | solution.py:132
  343.1 5.7 %multiply_reduce_fusion = f32[1024]{0:T(1024)S(1)} fusion(f32[1024,2048]{1,0:T(8,128)} %all-reduce.2.cloned.1.call-done, bf16[1024,2048]{1,0:T(8,128)(2,1)} %param.20), kind=kLoop, calls=%fused_computation.7 | loop fusion | flops 8387584 | bytes 12587008 | tf_op jit(solution)/shard_map/reduce_sum | solution.py:133
  348.9 20.7 %psum.15 = f32[1024]{0:T(1024)S(1)} all-reduce(f32[1024]{0:T(1024)S(1)} %multiply_reduce_fusion), channel_id=1, replica_groups=mesh['replica'=8,'tensor'=16] {'replica'}, use_global_device_ids=true, to_apply=%region_8.9 | all-reduce | flops 1024 | bytes 8192 | tf_op jit(solution)/shard_map/psum | solution.py:133
  369.6 24.2 %fusion = f32[1024,3328]{1,0:T(8,128)} fusion(bf16[2048,3328]{1,0:T(8,128)(2,1)} %bitcast.138, f32[1024,2048]{1,0:T(8,128)} %all-reduce.2.cloned.1.call-done, bf16[1024,2048]{1,0:T(8,128)(2,1)} %param.20, f32[2048]{0:T(1024)S(1)} %convert_element_type.29, f32[1024]{0:T(1024)S(1)} %add_rsqrt_fusion), kind=kOutput, calls=%fused_computation.9 | convolution fusion | flops 13969129472 | bytes 39858176 | tf_op jit(solution)/shard_map/dot_general | solution.py:138
  393.8 160.3 %reduce-scatter.2.cloned.1.call-done = f32[128,3328]{1,0:T(8,128)} async-done(((f32[1024,3328]{1,0:T(8,128)}), f32[128,3328]{1,0:T(8,128)}) %reduce-scatter.2.cloned.1.call-update) | async-done | bytes 1703952 | tf_op jit(solution)/shard_map/reduce_scatter | solution.py:137
  554.1 3.1 reshape.267
  557.2 3.4 fusion.38
  560.7 1.0 fusion.20
  (49 shorter events, 4.5 us)
Async XLA Ops:
  6.5 134.3 %copy-start = (bf16[512,2048]{1,0:T(8,128)(2,1)S(1)}, bf16[512,2048]{1,0:T(8,128)(2,1)}, u32[]{:S(2)}) copy-start(bf16[512,2048]{1,0:T(8,128)(2,1)} %param.19) | copy-start | bytes 6291460
  22.0 12.0 %copy-start.4 = (s32[64]{0:T(128)S(1)}, s32[64]{0:T(128)}, u32[]{:S(2)}) copy-start(s32[64]{0:T(128)} %param.17) | copy-start | bytes 772
  22.0 13.8 %copy-start.2 = (bf16[128,512]{1,0:T(8,128)(2,1)S(1)}, bf16[128,512]{1,0:T(8,128)(2,1)}, u32[]{:S(2)}) copy-start(bf16[128,512]{1,0:T(8,128)(2,1)} %param.12) | copy-start | bytes 393220
  22.0 63.8 %all-to-all-start = ((bf16[128,1,64,256]{3,2,1,0:T(8,128)(2,1)}), bf16[128,1,64,256]{3,2,1,0:T(8,128)(2,1)}, u32[]{:S(2)}, u32[]{:S(2)}) async-start(bf16[128,1,64,256]{3,2,1,0:T(8,128)(2,1)} %bitcast.135), calls=%async_computation | async-start | bytes 8388608 | tf_op jit(solution)/shard_map/all_to_all | solution.py:51
  33.9 106.9 %all-gather.2.cloned.1.call-start = ((), (), s32[]{:S(2)}) async-start(), calls=%async_computation.2 | async-start | bytes 1179648 | tf_op jit(solution)/shard_map/all_gather | solution.py:126
  94.3 248.8 %all-reduce.2.cloned.1.call-start = ((), (), s32[]{:S(2)}) async-start(), calls=%async_computation.3 | async-start | bytes 16777216 | tf_op jit(solution)/shard_map/psum | solution.py:132
  147.7 0.7 copy-start.3
  147.7 406.4 %reduce-scatter.2.cloned.1.call-start = ((), (), s32[]{:S(2)}) async-start(), calls=%async_computation.4 | async-start | bytes 15335424 | tf_op jit(solution)/shard_map/reduce_scatter | solution.py:137
  393.8 167.9 %copy-start.1 = (bf16[512,2048]{1,0:T(8,128)(2,1)S(1)}, bf16[512,2048]{1,0:T(8,128)(2,1)}, u32[]{:S(2)}) copy-start(bf16[512,2048]{1,0:T(8,128)(2,1)} %param.19) | copy-start | bytes 6291460
Sparse Core Ops, SparseCore 0:
  94.4 46.4 all-gather.1
  147.8 195.2 all-reduce.1
  393.9 160.1 reduce-scatter.1
where the time goes:
time: 569 us; the launch traced here: 568 us
  waiting for transfers between devices  427 us (75%)
  local copies, waits for them, and re-layouts  40.4 us (7%)
  matrix products  37.1 us (7%)
  blocking collectives  20.7 us (4%)
  other arithmetic  17.1 us (3%)
  between operations  13.3 us (2%)
  starting transfers between devices  12.1 us (2%)
    psum x1, waiting for transfers between devices, per_device(): carried = residual.astype(jnp.float32) + lax.psum(partial_out, 'tensor')  180 us
    reduce_scatter x1, waiting for transfers between devices, per_device(): lax.psum_scatter(jnp.dot(normed, weights_local, preferred_element_type=jn...  160 us
    all_gather x1, waiting for transfers between devices, per_device(): lax.all_gather(attended, 'replica', axis=0, tiled=True)  46.5 us
    all_to_all x1, waiting for transfers between devices, per_device(): lax.all_to_all(outgoing, ('replica', 'tensor'), split_axis=0, concat_axis...  40.2 us
    dot_general x1, matrix products, per_device(): jnp.dot(normed, weights_local, preferred_element_type=jnp.float32)  24.2 us
    psum x1, blocking collectives, per_device(): squares = lax.psum(jnp.sum(carried * carried, axis=1), 'replica')  20.7 us
    unnamed x13, local copies, waits for them, and re-layouts  15.1 us
    all_to_all x1, starting transfers between devices, per_device(): lax.all_to_all(outgoing, ('replica', 'tensor'), split_axis=0, concat_axis...  11.9 us
  transfers between devices with their start and end apart: 4, of which 4 were waited for; matrix products, arithmetic and copies ran while one was open for 5% of the time, Pallas kernels for 0%

commit v1 on v0

--- a/solution.py
+++ b/solution.py
@@ -127,19 +127,35 @@
         out_weight,
         preferred_element_type=jnp.float32,
     )
-    weights_local = gate_up.reshape(gate_up.shape[0], 2 * gate_up.shape[2])
-    gain_row = norm_gain.astype(jnp.float32)
-    carried = residual.astype(jnp.float32) + lax.psum(partial_out, "tensor")
-    squares = lax.psum(jnp.sum(carried * carried, axis=1), "replica")
-    normed = (carried * lax.rsqrt(squares / D + EPSILON)[:, None] * gain_row[None, :]).astype(
-        jnp.bfloat16
-    )
-    summed = lax.psum_scatter(
-        jnp.dot(normed, weights_local, preferred_element_type=jnp.float32),
-        "replica",
-        scatter_dimension=0,
+    all_rows = partial_out.shape[0]
+    width = partial_out.shape[1]
+    part_rows = all_rows // tensors
+    head_parts = lax.all_to_all(
+        partial_out.astype(jnp.bfloat16).reshape(tensors, part_rows, width),
+        "tensor",
+        split_axis=0,
+        concat_axis=0,
         tiled=True,
     )
+    head_sum = jnp.sum(head_parts.astype(jnp.float32), axis=0)
+    my_residual = lax.dynamic_slice_in_dim(residual, tensor_idx * part_rows, part_rows, 0)
+    carried = my_residual.astype(jnp.float32) + head_sum
+    gain_row = norm_gain.astype(jnp.float32)
+    squares = lax.psum(jnp.sum(carried * carried, axis=1), "replica")
+    normed_part = (
+        carried * lax.rsqrt(squares / D + EPSILON)[:, None] * gain_row[None, :]
+    ).astype(jnp.bfloat16)
+    normed = lax.all_gather(normed_part, "tensor", axis=0, tiled=True)
+    weights_local = gate_up.reshape(gate_up.shape[0], 2 * gate_up.shape[2])
+    slab = jnp.dot(normed, weights_local, preferred_element_type=jnp.float32)
+    slab_parts = lax.all_to_all(
+        slab.astype(jnp.bfloat16).reshape(replicas, rows_here, slab.shape[1]),
+        "replica",
+        split_axis=0,
+        concat_axis=0,
+        tiled=True,
+    )
+    summed = jnp.sum(slab_parts.astype(jnp.float32), axis=0)
     paired = summed.reshape(rows_here, 2, gate_up.shape[2])
     return (jax.nn.silu(paired[:, 0, :]) * paired[:, 1, :]).astype(jnp.bfloat16)
 

time: 569 us -> 397 us (0.70)
  waiting for transfers between devices: 427 us -> 171 us
  blocking collectives: 20.7 us -> 104 us
  starting transfers between devices: 12.1 us -> 18.8 us
  matrix products: 37.1 us -> 31.2 us
    psum x1 -> x0, waiting for transfers between devices: 180 us -> none  [per_device(): carried = residual.astype(jnp.float32) + lax.psum(partial_out, 'tensor')]
    reduce_scatter x1 -> x0, waiting for transfers between devices: 160 us -> none  [per_device(): lax.psum_scatter(jnp.dot(normed, weights_local, preferred_element_type=jn...]
    all_to_all x0 -> x1, blocking collectives: none -> 85.2 us  [per_device(): lax.all_to_all(slab.astype(jnp.bfloat16).reshape(replicas, rows_here, sla...]
    all_to_all x0 -> x1, waiting for transfers between devices: none -> 53 us  [per_device(): lax.all_to_all(partial_out.astype(jnp.bfloat16).reshape(tensors, part_row...]
    all_gather x0 -> x1, waiting for transfers between devices: none -> 31.2 us  [per_device(): normed = lax.all_gather(normed_part, 'tensor', axis=0, tiled=True)]
    all_to_all x0 -> x1, starting transfers between devices: none -> 6.75 us  [per_device(): lax.all_to_all(partial_out.astype(jnp.bfloat16).reshape(tensors, part_row...]
  transfers between devices with their start and end apart: 4 -> 4, of which waited for: 4 -> 4; matrix products, arithmetic and copies ran while one was open for 5% -> 7% of each run, Pallas kernels for 0% -> 0%
where the time goes in v1:
time: 397 us; the launch traced here: 396 us
  waiting for transfers between devices  171 us (43%)
  blocking collectives  104 us (26%)
  local copies, waits for them, and re-layouts  36.8 us (9%)
  matrix products  31.2 us (8%)
  other arithmetic  20.1 us (5%)
  starting transfers between devices  18.8 us (5%)
  between operations  13.7 us (3%)
    all_to_all x1, blocking collectives, per_device(): lax.all_to_all(slab.astype(jnp.bfloat16).reshape(replicas, rows_here, sla...  85.2 us
    all_to_all x1, waiting for transfers between devices, per_device(): lax.all_to_all(partial_out.astype(jnp.bfloat16).reshape(tensors, part_row...  53 us
    all_gather x1, waiting for transfers between devices, per_device(): lax.all_gather(attended, 'replica', axis=0, tiled=True)  46.6 us
    all_to_all x1, waiting for transfers between devices, per_device(): lax.all_to_all(outgoing, ('replica', 'tensor'), split_axis=0, concat_axis...  40.2 us
    all_gather x1, waiting for transfers between devices, per_device(): normed = lax.all_gather(normed_part, 'tensor', axis=0, tiled=True)  31.2 us
    dot_general x1, matrix products, per_device(): slab = jnp.dot(normed, weights_local, preferred_element_type=jnp.float32)  19.7 us
    psum x1, blocking collectives, per_device(): squares = lax.psum(jnp.sum(carried * carried, axis=1), 'replica')  19.3 us
    unnamed x13, local copies, waits for them, and re-layouts  14.4 us
  transfers between devices with their start and end apart: 4, of which 4 were waited for; matrix products, arithmetic and copies ran while one was open for 7% of the time, Pallas kernels for 0%

profile of v1, /device:TPU:1, one launch (start us, length us, event | category | flops | bytes accessed | tf_op | source)
XLA Modules:
  0.0 396.0 jit_solution(17759787468812746814)
XLA Ops:
  6.5 0.9 constant_dynamic-slice_fusion
  9.7 1.8 gather_fusion.1
  11.5 1.6 gather.42
  13.1 1.4 fusion.15
  14.5 2.8 gather_fusion.2
  17.3 4.7 %copy.44 = bf16[8,16,1,64,256]{4,3,1,0,2:T(8,128)(2,1)} copy(bf16[8,16,1,64,256]{4,3,0,1,2:T(8,128)(2,1)} %bitcast.140) | data formatting | bytes 8388608 | tf_op jit(solution)/shard_map/transpose | solution.py:48
  22.0 11.9 %all-to-all-start = ((bf16[128,1,64,256]{3,2,1,0:T(8,128)(2,1)}), bf16[128,1,64,256]{3,2,1,0:T(8,128)(2,1)}, u32[]{:S(2)}, u32[]{:S(2)}) async-start(bf16[128,1,64,256]{3,2,1,0:T(8,128)(2,1)} %bitcast.139), calls=%async_computation | async-start | bytes 8388608 | tf_op jit(solution)/shard_map/all_to_all | solution.py:51
  35.9 0.9 constant_dynamic-slice_fusion.1
  36.7 1.1 gather_fusion.4
  37.9 1.0 gather_fusion.3
  39.7 4.9 %compare_and_fusion.1 = (pred[128]{0:T(512)(128)(4,1)S(1)}, s32[128]{0:T(128)S(1)}) fusion(s32[128]{0:T(128)S(1)} %convert_reduce_fusion.2, s32[]{:T(128)} %bitcast.12, s32[]{:T(128)} %bitcast.11, s32[]{:T(128)} %bitcast.10, s32[]{:T(128)} %bitcast.9, s32[]{:T(128)} %bitcast.8, s32[]{:T(128)} %bitcast.7, s32[]{:T(128)} %bitcast.6, s32[]{:T(128)} %bitcast.5), kind=kLoop, calls=%fused_computation.84 | loop fusion | flops 4224 | bytes 1184 | tf_op jit(solution)/shard_map/jit(_take)/and | solution.py:124
  45.7 40.2 %all-to-all-done = bf16[128,1,64,256]{3,2,1,0:T(8,128)(2,1)} async-done(((bf16[128,1,64,256]{3,2,1,0:T(8,128)(2,1)}), bf16[128,1,64,256]{3,2,1,0:T(8,128)(2,1)}, u32[]{:S(2)}, u32[]{:S(2)}) %all-to-all-start) | async-done | bytes 4194336 | tf_op jit(solution)/shard_map/all_to_all | solution.py:51
  85.8 2.4 bitcast_reduce_fusion
  88.3 2.7 fusion.3
  90.9 1.0 fusion.1
  92.7 0.8 gather_fusion.5
  94.3 46.6 %all-gather.3.cloned.1.call-done = bf16[1024,512]{1,0:T(8,128)(2,1)} async-done(((bf16[128,512]{1,0:T(8,128)(2,1)}), bf16[1024,512]{1,0:T(8,128)(2,1)}) %all-gather.3.cloned.1.call-update) | async-done | bytes 1048592 | tf_op jit(solution)/shard_map/all_gather | solution.py:126
  140.8 5.5 %convolution_convert_fusion.1 = bf16[1024,2048]{1,0:T(8,128)(2,1)} fusion(bf16[1024,512]{1,0:T(8,128)(2,1)} %all-gather.3.cloned.1.call-done, bf16[512,2048]{1,0:T(8,128)(2,1)S(1)} %copy-done), kind=kOutput, calls=%fused_computation.13 | convolution fusion | flops 2149580800 | bytes 7340032 | tf_op jit(solution)/shard_map/dot_general | solution.py:125
  146.3 6.8 %all-to-all-start.1 = ((bf16[16,64,2048]{2,1,0:T(8,128)(2,1)}), bf16[16,64,2048]{2,1,0:T(8,128)(2,1)}, u32[]{:S(2)}, u32[]{:S(2)}) async-start(bf16[16,64,2048]{2,1,0:T(8,128)(2,1)} %bitcast.146), calls=%async_computation.1 | async-start | bytes 8388608 | tf_op jit(solution)/shard_map/all_to_all | solution.py:133
  153.1 53.0 %all-to-all-done.1 = bf16[16,64,2048]{2,1,0:T(8,128)(2,1)} async-done(((bf16[16,64,2048]{2,1,0:T(8,128)(2,1)}), bf16[16,64,2048]{2,1,0:T(8,128)(2,1)}, u32[]{:S(2)}, u32[]{:S(2)}) %all-to-all-start.1) | async-done | bytes 4194336 | tf_op jit(solution)/shard_map/all_to_all | solution.py:133
  206.2 3.0 convert_reduce_fusion.1
  209.2 1.1 multiply_reduce_fusion
  210.3 19.3 %psum.7 = f32[64]{0:T(128)S(1)} all-reduce(f32[64]{0:T(128)S(1)} %multiply_reduce_fusion), channel_id=1, replica_groups=mesh['replica'=8,'tensor'=16] {'replica'}, use_global_device_ids=true, to_apply=%region_8.9 | all-reduce | flops 64 | bytes 512 | tf_op jit(solution)/shard_map/psum | solution.py:144
  229.6 1.8 multiply_convert_fusion
  231.4 14.2 %copy.60 = bf16[256,8,2,1664]{3,1,2,0:T(8,128)(2,1)} copy(bf16[256,8,2,1664]{3,2,1,0:T(2,128)(2,1)} %bitcast.141) | data formatting | bytes 27262976
  245.6 31.2 %all-gather.5.cloned.1.call-done = bf16[1024,2048]{1,0:T(8,128)(2,1)} async-done(((bf16[64,2048]{1,0:T(8,128)(2,1)}), bf16[1024,2048]{1,0:T(8,128)(2,1)}) %all-gather.5.cloned.1.call-update) | async-done | bytes 4194320 | tf_op jit(solution)/shard_map/all_gather | solution.py:148
  276.8 19.7 %convolution_convert_fusion = bf16[1024,3328]{1,0:T(8,128)(2,1)S(1)} fusion(bf16[1024,2048]{1,0:T(8,128)(2,1)} %all-gather.5.cloned.1.call-done, bf16[2048,3328]{1,0:T(8,128)(2,1)} %bitcast.142), kind=kOutput, calls=%fused_computation.8 | convolution fusion | flops 13962051584 | bytes 24641536 | tf_op jit(solution)/shard_map/dot_general | solution.py:150
  296.5 85.2 %all_to_all.15 = bf16[8,128,3328]{2,1,0:T(8,128)(2,1)S(1)} all-to-all(bf16[8,128,3328]{2,1,0:T(8,128)(2,1)S(1)} %bitcast.143), channel_id=1, replica_groups=mesh['replica'=8,'tensor'=16] {'replica'}, dimensions={0} | all-to-all | bytes 13631488 | tf_op jit(solution)/shard_map/all_to_all | solution.py:151
  381.7 2.1 convert_reduce_fusion
  383.8 2.7 copy.51
  386.5 1.6 fusion.17
  388.1 1.0 copy.52
  (52 shorter events, 7.4 us)
Async XLA Ops:
  6.5 134.3 %copy-start = (bf16[512,2048]{1,0:T(8,128)(2,1)S(1)}, bf16[512,2048]{1,0:T(8,128)(2,1)}, u32[]{:S(2)}) copy-start(bf16[512,2048]{1,0:T(8,128)(2,1)} %param.19) | copy-start | bytes 6291460
  22.0 12.0 %copy-start.4 = (s32[64]{0:T(128)S(1)}, s32[64]{0:T(128)}, u32[]{:S(2)}) copy-start(s32[64]{0:T(128)} %param.17) | copy-start | bytes 772
  22.0 13.8 %copy-start.2 = (bf16[128,512]{1,0:T(8,128)(2,1)S(1)}, bf16[128,512]{1,0:T(8,128)(2,1)}, u32[]{:S(2)}) copy-start(bf16[128,512]{1,0:T(8,128)(2,1)} %param.12) | copy-start | bytes 393220
  22.0 63.8 %all-to-all-start = ((bf16[128,1,64,256]{3,2,1,0:T(8,128)(2,1)}), bf16[128,1,64,256]{3,2,1,0:T(8,128)(2,1)}, u32[]{:S(2)}, u32[]{:S(2)}) async-start(bf16[128,1,64,256]{3,2,1,0:T(8,128)(2,1)} %bitcast.139), calls=%async_computation | async-start | bytes 8388608 | tf_op jit(solution)/shard_map/all_to_all | solution.py:51
  33.9 106.9 %all-gather.3.cloned.1.call-start = ((), (), s32[]{:S(2)}) async-start(), calls=%async_computation.3 | async-start | bytes 1179648 | tf_op jit(solution)/shard_map/all_gather | solution.py:126
  146.3 6.8 %copy-start.3 = (bf16[2048]{0:T(1024)(128)(2,1)S(1)}, bf16[2048]{0:T(1024)(128)(2,1)}, u32[]{:S(2)}) copy-start(bf16[2048]{0:T(1024)(128)(2,1)} %param.21) | copy-start | bytes 12292
  146.3 59.9 %all-to-all-start.1 = ((bf16[16,64,2048]{2,1,0:T(8,128)(2,1)}), bf16[16,64,2048]{2,1,0:T(8,128)(2,1)}, u32[]{:S(2)}, u32[]{:S(2)}) async-start(bf16[16,64,2048]{2,1,0:T(8,128)(2,1)} %bitcast.146), calls=%async_computation.1 | async-start | bytes 8388608 | tf_op jit(solution)/shard_map/all_to_all | solution.py:133
  153.1 123.7 %all-gather.5.cloned.1.call-start = ((), (), s32[]{:S(2)}) async-start(), calls=%async_computation.4 | async-start | bytes 4456448 | tf_op jit(solution)/shard_map/all_gather | solution.py:148
  381.7 7.4 %copy-start.1 = (bf16[512,2048]{1,0:T(8,128)(2,1)S(1)}, bf16[512,2048]{1,0:T(8,128)(2,1)}, u32[]{:S(2)}) copy-start(bf16[512,2048]{1,0:T(8,128)(2,1)} %param.19) | copy-start | bytes 6291460
Sparse Core Ops, SparseCore 0:
  94.4 46.3 all-gather.2
  231.5 45.2 all-gather.4

commit v2 on v1

--- a/solution.py
+++ b/solution.py
@@ -122,8 +122,15 @@
     slot_attended = slot_attended.reshape(sessions * slot_rows, heads_local * HD)
     back_index = row_slot * slot_rows + row_ids - jnp.take(starts, row_slot, axis=0)
     attended = jnp.take(slot_attended, back_index, axis=0)
+    gathered = lax.all_to_all(
+        jnp.broadcast_to(attended[None], (replicas,) + attended.shape),
+        "replica",
+        split_axis=0,
+        concat_axis=0,
+        tiled=True,
+    ).reshape(replicas * rows_here, attended.shape[1])
     partial_out = jnp.dot(
-        lax.all_gather(attended, "replica", axis=0, tiled=True),
+        gathered,
         out_weight,
         preferred_element_type=jnp.float32,
     )
@@ -147,17 +154,27 @@
     ).astype(jnp.bfloat16)
     normed = lax.all_gather(normed_part, "tensor", axis=0, tiled=True)
     weights_local = gate_up.reshape(gate_up.shape[0], 2 * gate_up.shape[2])
-    slab = jnp.dot(normed, weights_local, preferred_element_type=jnp.float32)
-    slab_parts = lax.all_to_all(
-        slab.astype(jnp.bfloat16).reshape(replicas, rows_here, slab.shape[1]),
-        "replica",
-        split_axis=0,
-        concat_axis=0,
-        tiled=True,
-    )
-    summed = jnp.sum(slab_parts.astype(jnp.float32), axis=0)
-    paired = summed.reshape(rows_here, 2, gate_up.shape[2])
-    return (jax.nn.silu(paired[:, 0, :]) * paired[:, 1, :]).astype(jnp.bfloat16)
+    chunks = 2
+    chunk_rows = rows_here // chunks
+    normed_chunks = normed.reshape(replicas, chunks, chunk_rows, normed.shape[1])
+    outs = []
+    for c in range(chunks):
+        slab = jnp.dot(
+            normed_chunks[:, c].reshape(replicas * chunk_rows, normed.shape[1]),
+            weights_local,
+            preferred_element_type=jnp.float32,
+        )
+        slab_parts = lax.all_to_all(
+            slab.astype(jnp.bfloat16).reshape(replicas, chunk_rows, slab.shape[1]),
+            "replica",
+            split_axis=0,
+            concat_axis=0,
+            tiled=True,
+        )
+        summed = jnp.sum(slab_parts.astype(jnp.float32), axis=0)
+        paired = summed.reshape(chunk_rows, 2, gate_up.shape[2])
+        outs.append((jax.nn.silu(paired[:, 0, :]) * paired[:, 1, :]).astype(jnp.bfloat16))
+    return jnp.concatenate(outs, axis=0)
 
 
 def solution(mesh):

time: 397 us -> 389 us (0.980); the launches traced: 396 us -> 384 us
  blocking collectives: 104 us -> 36.2 us
  waiting for transfers between devices: 171 us -> 193 us
  starting transfers between devices: 18.8 us -> 39.9 us
  matrix products: 31.2 us -> 37.3 us
    all_to_all x0 -> x2, waiting for transfers between devices: none -> 67.6 us  [per_device(): lax.all_to_all(slab.astype(jnp.bfloat16).reshape(replicas, chunk_rows, sl...]
    all_to_all x1, blocking collectives: 85.2 us -> 19.1 us  [per_device(): lax.all_to_all(jnp.broadcast_to(attended[None], (replicas,) + attended.sh...]
    all_gather x1 -> x0, waiting for transfers between devices: 46.6 us -> none  [per_device(): lax.all_gather(attended, 'replica', axis=0, tiled=True)]
    all_to_all x0 -> x2, starting transfers between devices: none -> 19.5 us  [per_device(): lax.all_to_all(slab.astype(jnp.bfloat16).reshape(replicas, chunk_rows, sl...]
    dot_general x2 -> x3, matrix products: 25.2 us -> 31.3 us  [the longest x2 27 us: per_device(): jnp.dot(normed_chunks[:, c].reshape(replicas * chunk_rows, normed.shape[1...]
    slice x0 -> x3, local copies, waits for them, and re-layouts: none -> 4.84 us  [the longest x1 2.76 us: per_device(): normed_chunks[:, c].reshape(replicas * chunk_rows, normed.shape[1])]
  transfers between devices with their start and end apart: 4 -> 5, of which waited for: 4 -> 5; matrix products, arithmetic and copies ran while one was open for 7% -> 11% of each run, Pallas kernels for 0% -> 0%
where the time goes in v2:
time: 389 us; the launch traced here: 384 us
  waiting for transfers between devices  193 us (50%)
  local copies, waits for them, and re-layouts  40.3 us (10%)
  starting transfers between devices  39.9 us (10%)
  matrix products  37.3 us (10%)
  blocking collectives  36.2 us (9%)
  other arithmetic  23.8 us (6%)
  between operations  13.7 us (4%)
    all_to_all x2, waiting for transfers between devices, per_device(): lax.all_to_all(slab.astype(jnp.bfloat16).reshape(replicas, chunk_rows, sl...  67.6 us
    all_to_all x1, waiting for transfers between devices, per_device(): lax.all_to_all(partial_out.astype(jnp.bfloat16).reshape(tensors, part_row...  53 us
    all_to_all x1, waiting for transfers between devices, per_device(): lax.all_to_all(outgoing, ('replica', 'tensor'), split_axis=0, concat_axis...  40.2 us
    all_gather x1, waiting for transfers between devices, per_device(): normed = lax.all_gather(normed_part, 'tensor', axis=0, tiled=True)  31.8 us
    dot_general x2, matrix products, per_device(): jnp.dot(normed_chunks[:, c].reshape(replicas * chunk_rows, normed.shape[1...  27 us
    all_to_all x2, starting transfers between devices, per_device(): lax.all_to_all(slab.astype(jnp.bfloat16).reshape(replicas, chunk_rows, sl...  19.5 us
    all_to_all x1, blocking collectives, per_device(): lax.all_to_all(jnp.broadcast_to(attended[None], (replicas,) + attended.sh...  19.1 us
    psum x1, blocking collectives, per_device(): squares = lax.psum(jnp.sum(carried * carried, axis=1), 'replica')  17.2 us
  transfers between devices with their start and end apart: 5, of which 5 were waited for; matrix products, arithmetic and copies ran while one was open for 11% of the time, Pallas kernels for 0%

profile of v2, /device:TPU:1, one launch (start us, length us, event | category | flops | bytes accessed | tf_op | source)
XLA Modules:
  0.0 383.9 jit_solution(6299397193440588762)
XLA Ops:
  9.7 1.8 gather_fusion.1
  11.5 1.6 gather.42
  13.1 1.4 fusion.15
  14.5 2.8 gather_fusion.2
  17.3 4.7 %copy.49 = bf16[8,16,1,64,256]{4,3,1,0,2:T(8,128)(2,1)} copy(bf16[8,16,1,64,256]{4,3,0,1,2:T(8,128)(2,1)} %bitcast.154) | data formatting | bytes 8388608 | tf_op jit(solution)/shard_map/transpose | solution.py:48
  22.0 11.9 %all-to-all-start = ((bf16[128,1,64,256]{3,2,1,0:T(8,128)(2,1)}), bf16[128,1,64,256]{3,2,1,0:T(8,128)(2,1)}, u32[]{:S(2)}, u32[]{:S(2)}) async-start(bf16[128,1,64,256]{3,2,1,0:T(8,128)(2,1)} %bitcast.153), calls=%async_computation | async-start | bytes 8388608 | tf_op jit(solution)/shard_map/all_to_all | solution.py:51
  36.7 1.1 gather_fusion.4
  39.6 4.9 %compare_and_fusion.1 = (pred[128]{0:T(512)(128)(4,1)S(1)}, s32[128]{0:T(128)S(1)}) fusion(s32[128]{0:T(128)S(1)} %convert_reduce_fusion.3, s32[]{:T(128)} %bitcast.12, s32[]{:T(128)} %bitcast.11, s32[]{:T(128)} %bitcast.10, s32[]{:T(128)} %bitcast.9, s32[]{:T(128)} %bitcast.8, s32[]{:T(128)} %bitcast.7, s32[]{:T(128)} %bitcast.6, s32[]{:T(128)} %bitcast.5), kind=kLoop, calls=%fused_computation.90 | loop fusion | flops 4224 | bytes 1184 | tf_op jit(solution)/shard_map/jit(_take)/and | solution.py:124
  45.6 40.2 %all-to-all-done = bf16[128,1,64,256]{3,2,1,0:T(8,128)(2,1)} async-done(((bf16[128,1,64,256]{3,2,1,0:T(8,128)(2,1)}), bf16[128,1,64,256]{3,2,1,0:T(8,128)(2,1)}, u32[]{:S(2)}, u32[]{:S(2)}) %all-to-all-start) | async-done | bytes 4194336 | tf_op jit(solution)/shard_map/all_to_all | solution.py:51
  85.8 2.4 bitcast_reduce_fusion
  88.3 2.7 fusion.3
  93.7 19.1 %all_to_all.25 = bf16[8,128,512]{2,1,0:T(8,128)(2,1)S(1)} all-to-all(bf16[8,128,512]{2,1,0:T(8,128)(2,1)S(1)} %broadcast_in_dim.124), channel_id=1, replica_groups=mesh['replica'=8,'tensor'=16] {'replica'}, dimensions={0} | all-to-all | bytes 2097152 | tf_op jit(solution)/shard_map/all_to_all | solution.py:125
  112.8 4.3 %convolution_convert_fusion.2 = bf16[1024,2048]{1,0:T(8,128)(2,1)} fusion(bf16[1024,512]{1,0:T(8,128)(2,1)S(1)} %bitcast.165, bf16[512,2048]{1,0:T(8,128)(2,1)S(1)} %copy-done), kind=kOutput, calls=%fused_computation.15 | convolution fusion | flops 2149580800 | bytes 7340032 | tf_op jit(solution)/shard_map/dot_general | solution.py:132
  117.1 8.5 %all-to-all-start.2 = ((bf16[16,64,2048]{2,1,0:T(8,128)(2,1)}), bf16[16,64,2048]{2,1,0:T(8,128)(2,1)}, u32[]{:S(2)}, u32[]{:S(2)}) async-start(bf16[16,64,2048]{2,1,0:T(8,128)(2,1)} %bitcast.159), calls=%async_computation.2 | async-start | bytes 8388608 | tf_op jit(solution)/shard_map/all_to_all | solution.py:140
  125.6 53.0 %all-to-all-done.2 = bf16[16,64,2048]{2,1,0:T(8,128)(2,1)} async-done(((bf16[16,64,2048]{2,1,0:T(8,128)(2,1)}), bf16[16,64,2048]{2,1,0:T(8,128)(2,1)}, u32[]{:S(2)}, u32[]{:S(2)}) %all-to-all-start.2) | async-done | bytes 4194336 | tf_op jit(solution)/shard_map/all_to_all | solution.py:140
  178.6 3.0 convert_reduce_fusion
  182.8 17.2 %psum.7 = f32[64]{0:T(128)S(1)} all-reduce(f32[64]{0:T(128)S(1)} %multiply_reduce_fusion), channel_id=1, replica_groups=mesh['replica'=8,'tensor'=16] {'replica'}, use_global_device_ids=true, to_apply=%region_8.9 | all-reduce | flops 64 | bytes 512 | tf_op jit(solution)/shard_map/psum | solution.py:151
  200.0 1.8 multiply_convert_fusion
  201.8 14.2 %copy.70 = bf16[256,8,2,1664]{3,1,2,0:T(8,128)(2,1)} copy(bf16[256,8,2,1664]{3,2,1,0:T(2,128)(2,1)} %bitcast.155) | data formatting | bytes 27262976
  216.0 31.8 %all-gather.2.cloned.1.call-done = bf16[1024,2048]{1,0:T(8,128)(2,1)} async-done(((bf16[64,2048]{1,0:T(8,128)(2,1)}), bf16[1024,2048]{1,0:T(8,128)(2,1)}) %all-gather.2.cloned.1.call-update) | async-done | bytes 4194320 | tf_op jit(solution)/shard_map/all_gather | solution.py:155
  247.8 2.8 fusion.36
  250.6 13.5 %convolution_convert_fusion = bf16[512,3328]{1,0:T(8,128)(2,1)} fusion(bf16[512,2048]{1,0:T(8,128)(2,1)S(1)} %bitcast.164, bf16[2048,3328]{1,0:T(8,128)(2,1)} %bitcast.156), kind=kOutput, calls=%fused_computation.9 | convolution fusion | flops 6981025792 | bytes 19136512 | tf_op jit(solution)/shard_map/dot_general | solution.py:162
  264.1 6.2 %all-to-all-start.4 = ((bf16[8,64,3328]{2,1,0:T(8,128)(2,1)}), bf16[8,64,3328]{2,1,0:T(8,128)(2,1)}, u32[]{:S(2)}, u32[]{:S(2)}) async-start(bf16[8,64,3328]{2,1,0:T(8,128)(2,1)} %bitcast.162), calls=%async_computation.4 | async-start | bytes 6815744 | tf_op jit(solution)/shard_map/all_to_all | solution.py:167
  270.4 13.5 %convolution_convert_fusion.1 = bf16[512,3328]{1,0:T(8,128)(2,1)} fusion(bf16[512,2048]{1,0:T(8,128)(2,1)S(1)} %bitcast.163, bf16[2048,3328]{1,0:T(8,128)(2,1)} %bitcast.157), kind=kOutput, calls=%fused_computation.10 | convolution fusion | flops 6981025792 | bytes 19136512 | tf_op jit(solution)/shard_map/dot_general | solution.py:162
  283.8 29.3 %all-to-all-done.4 = bf16[8,64,3328]{2,1,0:T(8,128)(2,1)} async-done(((bf16[8,64,3328]{2,1,0:T(8,128)(2,1)}), bf16[8,64,3328]{2,1,0:T(8,128)(2,1)}, u32[]{:S(2)}, u32[]{:S(2)}) %all-to-all-start.4) | async-done | bytes 3407904 | tf_op jit(solution)/shard_map/all_to_all | solution.py:167
  313.1 13.3 %all-to-all-start.3 = ((bf16[8,64,3328]{2,1,0:T(8,128)(2,1)}), bf16[8,64,3328]{2,1,0:T(8,128)(2,1)}, u32[]{:S(2)}, u32[]{:S(2)}) async-start(bf16[8,64,3328]{2,1,0:T(8,128)(2,1)} %bitcast.161), calls=%async_computation.3 | async-start | bytes 6815744 | tf_op jit(solution)/shard_map/all_to_all | solution.py:167
  326.4 2.5 convert_reduce_fusion.1
  329.4 1.4 fusion.38
  330.8 38.3 %all-to-all-done.3 = bf16[8,64,3328]{2,1,0:T(8,128)(2,1)} async-done(((bf16[8,64,3328]{2,1,0:T(8,128)(2,1)}), bf16[8,64,3328]{2,1,0:T(8,128)(2,1)}, u32[]{:S(2)}, u32[]{:S(2)}) %all-to-all-start.3) | async-done | bytes 3407904 | tf_op jit(solution)/shard_map/all_to_all | solution.py:167
  369.1 3.6 convert_reduce_fusion.2
  372.7 1.7 reshape.301
  375.1 1.3 fusion.19
  (60 shorter events, 14.5 us)
Async XLA Ops:
  6.5 106.2 %copy-start = (bf16[512,2048]{1,0:T(8,128)(2,1)S(1)}, bf16[512,2048]{1,0:T(8,128)(2,1)}, u32[]{:S(2)}) copy-start(bf16[512,2048]{1,0:T(8,128)(2,1)} %param.19) | copy-start | bytes 6291460
  22.0 12.0 %copy-start.4 = (s32[64]{0:T(128)S(1)}, s32[64]{0:T(128)}, u32[]{:S(2)}) copy-start(s32[64]{0:T(128)} %param.17) | copy-start | bytes 772
  22.0 13.8 %copy-start.2 = (bf16[128,512]{1,0:T(8,128)(2,1)S(1)}, bf16[128,512]{1,0:T(8,128)(2,1)}, u32[]{:S(2)}) copy-start(bf16[128,512]{1,0:T(8,128)(2,1)} %param.12) | copy-start | bytes 393220
  22.0 63.8 %all-to-all-start = ((bf16[128,1,64,256]{3,2,1,0:T(8,128)(2,1)}), bf16[128,1,64,256]{3,2,1,0:T(8,128)(2,1)}, u32[]{:S(2)}, u32[]{:S(2)}) async-start(bf16[128,1,64,256]{3,2,1,0:T(8,128)(2,1)} %bitcast.153), calls=%async_computation | async-start | bytes 8388608 | tf_op jit(solution)/shard_map/all_to_all | solution.py:51
  117.1 8.5 %copy-start.3 = (bf16[2048]{0:T(1024)(128)(2,1)S(1)}, bf16[2048]{0:T(1024)(128)(2,1)}, u32[]{:S(2)}) copy-start(bf16[2048]{0:T(1024)(128)(2,1)} %param.21) | copy-start | bytes 12292
  117.1 61.6 %all-to-all-start.2 = ((bf16[16,64,2048]{2,1,0:T(8,128)(2,1)}), bf16[16,64,2048]{2,1,0:T(8,128)(2,1)}, u32[]{:S(2)}, u32[]{:S(2)}) async-start(bf16[16,64,2048]{2,1,0:T(8,128)(2,1)} %bitcast.159), calls=%async_computation.2 | async-start | bytes 8388608 | tf_op jit(solution)/shard_map/all_to_all | solution.py:140
  125.5 122.3 %all-gather.2.cloned.1.call-start = ((), (), s32[]{:S(2)}) async-start(), calls=%async_computation.5 | async-start | bytes 4456448 | tf_op jit(solution)/shard_map/all_gather | solution.py:155
  264.1 49.0 %all-to-all-start.4 = ((bf16[8,64,3328]{2,1,0:T(8,128)(2,1)}), bf16[8,64,3328]{2,1,0:T(8,128)(2,1)}, u32[]{:S(2)}, u32[]{:S(2)}) async-start(bf16[8,64,3328]{2,1,0:T(8,128)(2,1)} %bitcast.162), calls=%async_computation.4 | async-start | bytes 6815744 | tf_op jit(solution)/shard_map/all_to_all | solution.py:167
  313.1 56.0 %all-to-all-start.3 = ((bf16[8,64,3328]{2,1,0:T(8,128)(2,1)}), bf16[8,64,3328]{2,1,0:T(8,128)(2,1)}, u32[]{:S(2)}, u32[]{:S(2)}) async-start(bf16[8,64,3328]{2,1,0:T(8,128)(2,1)} %bitcast.161), calls=%async_computation.3 | async-start | bytes 6815744 | tf_op jit(solution)/shard_map/all_to_all | solution.py:167
  369.1 8.0 %copy-start.1 = (bf16[512,2048]{1,0:T(8,128)(2,1)S(1)}, bf16[512,2048]{1,0:T(8,128)(2,1)}, u32[]{:S(2)}) copy-start(bf16[512,2048]{1,0:T(8,128)(2,1)} %param.19) | copy-start | bytes 6291460
Sparse Core Ops, SparseCore 0:
  201.9 45.8 all-gather.1

commit v3 on v1

--- a/solution.py
+++ b/solution.py
@@ -122,8 +122,15 @@
     slot_attended = slot_attended.reshape(sessions * slot_rows, heads_local * HD)
     back_index = row_slot * slot_rows + row_ids - jnp.take(starts, row_slot, axis=0)
     attended = jnp.take(slot_attended, back_index, axis=0)
+    gathered = lax.all_to_all(
+        jnp.broadcast_to(attended[None], (replicas,) + attended.shape),
+        "replica",
+        split_axis=0,
+        concat_axis=0,
+        tiled=True,
+    ).reshape(replicas * rows_here, attended.shape[1])
     partial_out = jnp.dot(
-        lax.all_gather(attended, "replica", axis=0, tiled=True),
+        gathered,
         out_weight,
         preferred_element_type=jnp.float32,
     )
@@ -141,23 +148,42 @@
     my_residual = lax.dynamic_slice_in_dim(residual, tensor_idx * part_rows, part_rows, 0)
     carried = my_residual.astype(jnp.float32) + head_sum
     gain_row = norm_gain.astype(jnp.float32)
-    squares = lax.psum(jnp.sum(carried * carried, axis=1), "replica")
-    normed_part = (
-        carried * lax.rsqrt(squares / D + EPSILON)[:, None] * gain_row[None, :]
-    ).astype(jnp.bfloat16)
-    normed = lax.all_gather(normed_part, "tensor", axis=0, tiled=True)
+    lane = 128
+    part_squares = jnp.sum(carried * carried, axis=1)
+    square_hi = part_squares.astype(jnp.bfloat16)
+    square_lo = (part_squares - square_hi.astype(jnp.float32)).astype(jnp.bfloat16)
+    square_block = jnp.zeros((part_rows, lane), jnp.bfloat16)
+    square_block = square_block.at[:, 0].set(square_hi).at[:, 1].set(square_lo)
+    scaled = (carried * gain_row[None, :]).astype(jnp.bfloat16)
+    gathered_rows = lax.all_gather(
+        jnp.concatenate([scaled, square_block], axis=1), "tensor", axis=0, tiled=True
+    )
+    normed = gathered_rows[:, :width]
+    row_squares = gathered_rows[:, width].astype(jnp.float32) + gathered_rows[
+        :, width + 1
+    ].astype(jnp.float32)
     weights_local = gate_up.reshape(gate_up.shape[0], 2 * gate_up.shape[2])
     slab = jnp.dot(normed, weights_local, preferred_element_type=jnp.float32)
+    slab_cols = slab.shape[1]
+    row_hi = row_squares.astype(jnp.bfloat16)
+    row_lo = (row_squares - row_hi.astype(jnp.float32)).astype(jnp.bfloat16)
+    row_block = jnp.zeros((slab.shape[0], lane), jnp.bfloat16)
+    row_block = row_block.at[:, 0].set(row_hi).at[:, 1].set(row_lo)
+    payload = jnp.concatenate([slab.astype(jnp.bfloat16), row_block], axis=1)
     slab_parts = lax.all_to_all(
-        slab.astype(jnp.bfloat16).reshape(replicas, rows_here, slab.shape[1]),
+        payload.reshape(replicas, rows_here, slab_cols + lane),
         "replica",
         split_axis=0,
         concat_axis=0,
         tiled=True,
     )
     summed = jnp.sum(slab_parts.astype(jnp.float32), axis=0)
-    paired = summed.reshape(rows_here, 2, gate_up.shape[2])
-    return (jax.nn.silu(paired[:, 0, :]) * paired[:, 1, :]).astype(jnp.bfloat16)
+    total_squares = summed[:, slab_cols] + summed[:, slab_cols + 1]
+    inv_rms = lax.rsqrt(total_squares / D + EPSILON)
+    paired = summed[:, :slab_cols].reshape(rows_here, 2, gate_up.shape[2])
+    gate = paired[:, 0, :] * inv_rms[:, None]
+    up = paired[:, 1, :] * inv_rms[:, None]
+    return (jax.nn.silu(gate) * up).astype(jnp.bfloat16)
 
 
 def solution(mesh):

time: 397 us -> 358 us (0.902)
  waiting for transfers between devices: 171 us -> 120 us
  other arithmetic: 20.1 us -> 25 us
    all_gather x2 -> x1, waiting for transfers between devices: 77.7 us -> 27.7 us  [per_device(): lax.all_gather(jnp.concatenate([scaled, square_block], axis=1), 'tensor',...]
    all_to_all x1 -> x2, blocking collectives: 85.2 us -> 107 us  [the longest x1 87.8 us: per_device(): lax.all_to_all(payload.reshape(replicas, rows_here, slab_cols + lane), 'r...]
    psum x1 -> x0, blocking collectives: 19.3 us -> none  [per_device(): squares = lax.psum(jnp.sum(carried * carried, axis=1), 'replica')]
    another operation x1 -> x5, other arithmetic: 0.18 us -> 4.96 us
    concatenate x0 -> x2, other arithmetic: none -> 4.15 us  [the longest x1 3.42 us: per_device(): payload = jnp.concatenate([slab.astype(jnp.bfloat16), row_block], axis=1)]
    slice x0 -> x2, local copies, waits for them, and re-layouts: none -> 3.99 us  [per_device(): paired = summed[:, :slab_cols].reshape(rows_here, 2, gate_up.shape[2])]
    unnamed x13 -> x15, local copies, waits for them, and re-layouts: 14.4 us -> 14.4 us
  transfers between devices with their start and end apart: 4 -> 3, of which waited for: 4 -> 3; matrix products, arithmetic and copies ran while one was open for 7% -> 8% of each run, Pallas kernels for 0% -> 0%
where the time goes in v3:
time: 358 us; the launch traced here: 357 us
  waiting for transfers between devices  120 us (34%)
  blocking collectives  107 us (30%)
  local copies, waits for them, and re-layouts  39.7 us (11%)
  matrix products  31.6 us (9%)
  other arithmetic  25 us (7%)
  starting transfers between devices  20.4 us (6%)
  between operations  13.7 us (4%)
    all_to_all x1, blocking collectives, per_device(): lax.all_to_all(payload.reshape(replicas, rows_here, slab_cols + lane), 'r...  87.8 us
    all_to_all x1, waiting for transfers between devices, per_device(): lax.all_to_all(partial_out.astype(jnp.bfloat16).reshape(tensors, part_row...  51.8 us
    all_to_all x1, waiting for transfers between devices, per_device(): lax.all_to_all(outgoing, ('replica', 'tensor'), split_axis=0, concat_axis...  40.2 us
    all_gather x1, waiting for transfers between devices, per_device(): lax.all_gather(jnp.concatenate([scaled, square_block], axis=1), 'tensor',...  27.7 us
    dot_general x1, matrix products, per_device(): slab = jnp.dot(normed, weights_local, preferred_element_type=jnp.float32)  21.2 us
    all_to_all x1, blocking collectives, per_device(): lax.all_to_all(jnp.broadcast_to(attended[None], (replicas,) + attended.sh...  19.1 us
    unnamed x15, local copies, waits for them, and re-layouts  14.4 us
    all_to_all x1, starting transfers between devices, per_device(): lax.all_to_all(outgoing, ('replica', 'tensor'), split_axis=0, concat_axis...  11.9 us
  transfers between devices with their start and end apart: 3, of which 3 were waited for; matrix products, arithmetic and copies ran while one was open for 8% of the time, Pallas kernels for 0%

profile of v3, /device:TPU:1, one launch (start us, length us, event | category | flops | bytes accessed | tf_op | source)
XLA Modules:
  0.0 357.0 jit_solution(16755203401988401577)
XLA Ops:
  9.0 1.8 gather_fusion.1
  10.9 1.6 gather.42
  12.5 1.4 fusion.16
  13.9 2.8 gather_fusion.2
  16.7 4.7 %copy.65 = bf16[8,16,1,64,256]{4,3,1,0,2:T(8,128)(2,1)} copy(bf16[8,16,1,64,256]{4,3,0,1,2:T(8,128)(2,1)} %bitcast.146) | data formatting | bytes 8388608 | tf_op jit(solution)/shard_map/transpose | solution.py:48
  21.4 11.9 %all-to-all-start = ((bf16[128,1,64,256]{3,2,1,0:T(8,128)(2,1)}), bf16[128,1,64,256]{3,2,1,0:T(8,128)(2,1)}, u32[]{:S(2)}, u32[]{:S(2)}) async-start(bf16[128,1,64,256]{3,2,1,0:T(8,128)(2,1)} %bitcast.145), calls=%async_computation | async-start | bytes 8388608 | tf_op jit(solution)/shard_map/all_to_all | solution.py:51
  35.1 1.0 gather_fusion.3
  37.1 1.1 gather_fusion.4
  39.0 4.9 %compare_and_fusion.1 = (pred[128]{0:T(512)(128)(4,1)S(1)}, s32[128]{0:T(128)S(1)}) fusion(s32[128]{0:T(128)S(1)} %convert_reduce_fusion.2, s32[]{:T(128)} %bitcast.12, s32[]{:T(128)} %bitcast.11, s32[]{:T(128)} %bitcast.10, s32[]{:T(128)} %bitcast.9, s32[]{:T(128)} %bitcast.8, s32[]{:T(128)} %bitcast.7, s32[]{:T(128)} %bitcast.6, s32[]{:T(128)} %bitcast.5), kind=kLoop, calls=%fused_computation.104 | loop fusion | flops 4224 | bytes 1184 | tf_op jit(solution)/shard_map/jit(_take)/and | solution.py:124
  45.0 40.2 %all-to-all-done = bf16[128,1,64,256]{3,2,1,0:T(8,128)(2,1)} async-done(((bf16[128,1,64,256]{3,2,1,0:T(8,128)(2,1)}), bf16[128,1,64,256]{3,2,1,0:T(8,128)(2,1)}, u32[]{:S(2)}, u32[]{:S(2)}) %all-to-all-start) | async-done | bytes 4194336 | tf_op jit(solution)/shard_map/all_to_all | solution.py:51
  85.2 2.4 bitcast_reduce_fusion
  87.6 1.0 fusion.2
  88.7 2.7 fusion.4
  93.1 19.1 %all_to_all.20 = bf16[8,128,512]{2,1,0:T(8,128)(2,1)S(1)} all-to-all(bf16[8,128,512]{2,1,0:T(8,128)(2,1)S(1)} %broadcast_in_dim.127), channel_id=1, replica_groups=mesh['replica'=8,'tensor'=16] {'replica'}, dimensions={0} | all-to-all | bytes 2097152 | tf_op jit(solution)/shard_map/all_to_all | solution.py:125
  112.1 4.3 %convolution_convert_fusion.1 = bf16[1024,2048]{1,0:T(8,128)(2,1)} fusion(bf16[1024,512]{1,0:T(8,128)(2,1)S(1)} %bitcast.152, bf16[512,2048]{1,0:T(8,128)(2,1)S(1)} %copy-done), kind=kOutput, calls=%fused_computation.15 | convolution fusion | flops 2149580800 | bytes 7340032 | tf_op jit(solution)/shard_map/dot_general | solution.py:132
  116.4 8.5 %all-to-all-start.2 = ((bf16[16,64,2048]{2,1,0:T(8,128)(2,1)}), bf16[16,64,2048]{2,1,0:T(8,128)(2,1)}, u32[]{:S(2)}, u32[]{:S(2)}) async-start(bf16[16,64,2048]{2,1,0:T(8,128)(2,1)} %bitcast.151), calls=%async_computation.2 | async-start | bytes 8388608 | tf_op jit(solution)/shard_map/all_to_all | solution.py:140
  126.2 51.8 %all-to-all-done.2 = bf16[16,64,2048]{2,1,0:T(8,128)(2,1)} async-done(((bf16[16,64,2048]{2,1,0:T(8,128)(2,1)}), bf16[16,64,2048]{2,1,0:T(8,128)(2,1)}, u32[]{:S(2)}, u32[]{:S(2)}) %all-to-all-start.2) | async-done | bytes 4194336 | tf_op jit(solution)/shard_map/all_to_all | solution.py:140
  178.0 3.0 convert_reduce_fusion.1
  181.0 1.2 multiply_convert_fusion
  182.3 1.2 fusion.34
  184.5 14.2 %copy.83 = bf16[256,8,2,1664]{3,1,2,0:T(8,128)(2,1)} copy(bf16[256,8,2,1664]{3,2,1,0:T(2,128)(2,1)} %bitcast.147) | data formatting | bytes 27262976
  198.8 27.7 %all-gather.2.cloned.1.call-done = bf16[1024,2176]{1,0:T(8,128)(2,1)} async-done(((bf16[64,2176]{1,0:T(8,128)(2,1)}), bf16[1024,2176]{1,0:T(8,128)(2,1)}) %all-gather.2.cloned.1.call-update) | async-done | bytes 4456464 | tf_op jit(solution)/shard_map/all_gather | solution.py:158
  226.5 2.4 fusion.26
  228.9 1.0 scatter.19
  229.9 21.2 %convolution_convert_fusion = bf16[1024,3328]{1,0:T(8,128)(2,1)} fusion(bf16[2048,3328]{1,0:T(8,128)(2,1)} %bitcast.148, bf16[1024,2176]{1,0:T(8,128)(2,1)} %all-gather.2.cloned.1.call-done), kind=kOutput, calls=%fused_computation.8 | convolution fusion | flops 13962051584 | bytes 24641536 | tf_op jit(solution)/shard_map/dot_general | solution.py:166
  251.1 3.4 pad_maximum_fusion
  254.5 87.8 %all_to_all.21 = bf16[8,128,3456]{2,1,0:T(8,128)(2,1)S(1)} all-to-all(bf16[8,128,3456]{2,1,0:T(8,128)(2,1)S(1)} %bitcast.144), channel_id=1, replica_groups=mesh['replica'=8,'tensor'=16] {'replica'}, dimensions={0} | all-to-all | bytes 14155776 | tf_op jit(solution)/shard_map/all_to_all | solution.py:173
  342.3 1.0 convert_reduce_fusion
  343.4 1.3 slice.134
  344.8 2.7 copy.74
  347.5 1.7 fusion.19
  349.2 1.0 copy.75
  (63 shorter events, 11.4 us)
Async XLA Ops:
  6.5 105.6 %copy-start = (bf16[512,2048]{1,0:T(8,128)(2,1)S(1)}, bf16[512,2048]{1,0:T(8,128)(2,1)}, u32[]{:S(2)}) copy-start(bf16[512,2048]{1,0:T(8,128)(2,1)} %param.27) | copy-start | bytes 6291460
  6.5 5.9 %copy-start.4 = (s32[16]{0:T(128)S(1)}, s32[16]{0:T(128)}, u32[]{:S(2)}) copy-start(s32[16]{0:T(128)} %constant.276) | copy-start | bytes 196
  21.4 13.7 %copy-start.2 = (bf16[128,512]{1,0:T(8,128)(2,1)S(1)}, bf16[128,512]{1,0:T(8,128)(2,1)}, u32[]{:S(2)}) copy-start(bf16[128,512]{1,0:T(8,128)(2,1)} %param.20) | copy-start | bytes 393220
  21.4 14.8 %copy-start.5 = (s32[64]{0:T(128)S(1)}, s32[64]{0:T(128)}, u32[]{:S(2)}) copy-start(s32[64]{0:T(128)} %param.25) | copy-start | bytes 772
  21.4 63.8 %all-to-all-start = ((bf16[128,1,64,256]{3,2,1,0:T(8,128)(2,1)}), bf16[128,1,64,256]{3,2,1,0:T(8,128)(2,1)}, u32[]{:S(2)}, u32[]{:S(2)}) async-start(bf16[128,1,64,256]{3,2,1,0:T(8,128)(2,1)} %bitcast.145), calls=%async_computation | async-start | bytes 8388608 | tf_op jit(solution)/shard_map/all_to_all | solution.py:51
  116.4 8.5 %copy-start.3 = (bf16[2048]{0:T(1024)(128)(2,1)S(1)}, bf16[2048]{0:T(1024)(128)(2,1)}, u32[]{:S(2)}) copy-start(bf16[2048]{0:T(1024)(128)(2,1)} %param.29) | copy-start | bytes 12292
  116.4 61.6 %all-to-all-start.2 = ((bf16[16,64,2048]{2,1,0:T(8,128)(2,1)}), bf16[16,64,2048]{2,1,0:T(8,128)(2,1)}, u32[]{:S(2)}, u32[]{:S(2)}) async-start(bf16[16,64,2048]{2,1,0:T(8,128)(2,1)} %bitcast.151), calls=%async_computation.2 | async-start | bytes 8388608 | tf_op jit(solution)/shard_map/all_to_all | solution.py:140
  124.9 101.6 %all-gather.2.cloned.1.call-start = ((), (), s32[]{:S(2)}) async-start(), calls=%async_computation.4 | async-start | bytes 4734976 | tf_op jit(solution)/shard_map/all_gather | solution.py:158
  342.3 7.8 %copy-start.1 = (bf16[512,2048]{1,0:T(8,128)(2,1)S(1)}, bf16[512,2048]{1,0:T(8,128)(2,1)}, u32[]{:S(2)}) copy-start(bf16[512,2048]{1,0:T(8,128)(2,1)} %param.27) | copy-start | bytes 6291460
Sparse Core Ops, SparseCore 0:
  184.7 41.7 all-gather.1

commit v4 on v1

--- a/solution.py
+++ b/solution.py
@@ -44,13 +44,22 @@
     my_column = lax.dynamic_slice_in_dim(table_rows, tensor_idx, 1, 1)[:, 0]
     page_index = jnp.take(my_column, from_here.reshape(-1), axis=0)
     chosen = jnp.take(kv_pool, page_index, axis=0).reshape(replicas, SHARE, PAGE, KVH, pair_width)
+    half = PAGE // 2
+    core_half = np.arange(tensors) % 2
     outgoing = jnp.take(chosen, owner_head, axis=3)
-    outgoing = jnp.transpose(outgoing, (0, 3, 1, 2, 4)).reshape(
-        replicas * tensors, SHARE, PAGE, pair_width
+    outgoing = outgoing.reshape(replicas, SHARE, 2, half, tensors, pair_width)
+    outgoing = outgoing[:, :, core_half, :, np.arange(tensors), :]
+    outgoing = jnp.transpose(outgoing, (1, 0, 2, 3, 4)).reshape(
+        replicas * tensors, SHARE, half, pair_width
     )
     arrived = lax.all_to_all(
         outgoing, ("replica", "tensor"), split_axis=0, concat_axis=0, tiled=True
     )
+    partner = lax.ppermute(arrived, "tensor", [(i, i ^ 1) for i in range(tensors)])
+    mine_first = (tensor_idx % 2) == 0
+    low_half = jnp.where(mine_first, arrived, partner)
+    high_half = jnp.where(mine_first, partner, arrived)
+    arrived = jnp.concatenate([low_half, high_half], axis=2)
     arrived = arrived.reshape(replicas, tensors, SHARE, PAGE, pair_width)
     prefix_blocks = jnp.transpose(arrived, (0, 2, 1, 3, 4)).reshape(
         sessions, cached_len, pair_width
@@ -122,8 +131,15 @@
     slot_attended = slot_attended.reshape(sessions * slot_rows, heads_local * HD)
     back_index = row_slot * slot_rows + row_ids - jnp.take(starts, row_slot, axis=0)
     attended = jnp.take(slot_attended, back_index, axis=0)
+    gathered = lax.all_to_all(
+        jnp.broadcast_to(attended[None], (replicas,) + attended.shape),
+        "replica",
+        split_axis=0,
+        concat_axis=0,
+        tiled=True,
+    ).reshape(replicas * rows_here, attended.shape[1])
     partial_out = jnp.dot(
-        lax.all_gather(attended, "replica", axis=0, tiled=True),
+        gathered,
         out_weight,
         preferred_element_type=jnp.float32,
     )
@@ -141,7 +157,13 @@
     my_residual = lax.dynamic_slice_in_dim(residual, tensor_idx * part_rows, part_rows, 0)
     carried = my_residual.astype(jnp.float32) + head_sum
     gain_row = norm_gain.astype(jnp.float32)
-    squares = lax.psum(jnp.sum(carried * carried, axis=1), "replica")
+    squares = jnp.sum(carried * carried, axis=1)
+    step = 1
+    while step < replicas:
+        squares = squares + lax.ppermute(
+            squares, "replica", [(i, i ^ step) for i in range(replicas)]
+        )
+        step *= 2
     normed_part = (
         carried * lax.rsqrt(squares / D + EPSILON)[:, None] * gain_row[None, :]
     ).astype(jnp.bfloat16)

time: 397 us -> 352 us (0.89)
  waiting for transfers between devices: 171 us -> 118 us
  local copies, waits for them, and re-layouts: 36.8 us -> 44.4 us
  matrix products: 31.2 us -> 27.2 us
    all_gather x1 -> x0, waiting for transfers between devices: 46.6 us -> none  [per_device(): lax.all_gather(attended, 'replica', axis=0, tiled=True)]
    all_to_all x0 -> x1, blocking collectives: none -> 20.1 us  [per_device(): lax.all_to_all(jnp.broadcast_to(attended[None], (replicas,) + attended.sh...]
    psum x1 -> x0, blocking collectives: 19.3 us -> none  [per_device(): squares = lax.psum(jnp.sum(carried * carried, axis=1), 'replica')]
    all_to_all x1, waiting for transfers between devices: 40.2 us -> 26.7 us  [per_device(): lax.all_to_all(outgoing, ('replica', 'tensor'), split_axis=0, concat_axis...]
    ppermute x0 -> x4, waiting for transfers between devices: none -> 8.83 us  [the longest x3 8.83 us: per_device(): lax.ppermute(squares, 'replica', [(i, i ^ step) for i in range(replicas)])]
    gather x1 -> x2, local copies, waits for them, and re-layouts: 2.79 us -> 7.56 us  [per_device(): outgoing = jnp.take(chosen, owner_head, axis=3)]
    gather x0 -> x1, local copies, waits for them, and re-layouts: none -> 4.2 us  [per_device(): outgoing = outgoing[:, :, core_half, :, np.arange(tensors), :]]
    unnamed x13 -> x15, local copies, waits for them, and re-layouts: 14.4 us -> 14.4 us
  transfers between devices with their start and end apart: 4 -> 7, of which waited for: 4 -> 6; matrix products, arithmetic and copies ran while one was open for 7% -> 7% of each run, Pallas kernels for 0% -> 0%
where the time goes in v4:
time: 352 us; the launch traced here: 351 us
  waiting for transfers between devices  118 us (34%)
  blocking collectives  105 us (30%)
  local copies, waits for them, and re-layouts  44.4 us (13%)
  matrix products  27.2 us (8%)
  other arithmetic  22.4 us (6%)
  starting transfers between devices  20.1 us (6%)
  between operations  13.6 us (4%)
    all_to_all x1, blocking collectives, per_device(): lax.all_to_all(slab.astype(jnp.bfloat16).reshape(replicas, rows_here, sla...  85.2 us
    all_to_all x1, waiting for transfers between devices, per_device(): lax.all_to_all(partial_out.astype(jnp.bfloat16).reshape(tensors, part_row...  52.4 us
    all_gather x1, waiting for transfers between devices, per_device(): normed = lax.all_gather(normed_part, 'tensor', axis=0, tiled=True)  29.8 us
    all_to_all x1, waiting for transfers between devices, per_device(): lax.all_to_all(outgoing, ('replica', 'tensor'), split_axis=0, concat_axis...  26.7 us
    all_to_all x1, blocking collectives, per_device(): lax.all_to_all(jnp.broadcast_to(attended[None], (replicas,) + attended.sh...  20.1 us
    dot_general x1, matrix products, per_device(): slab = jnp.dot(normed, weights_local, preferred_element_type=jnp.float32)  19.7 us
    unnamed x15, local copies, waits for them, and re-layouts  14.4 us
    all_to_all x1, starting transfers between devices, per_device(): lax.all_to_all(outgoing, ('replica', 'tensor'), split_axis=0, concat_axis...  11.9 us
  transfers between devices with their start and end apart: 7, of which 6 were waited for; matrix products, arithmetic and copies ran while one was open for 7% of the time, Pallas kernels for 0%

profile of v4, /device:TPU:1, one launch (start us, length us, event | category | flops | bytes accessed | tf_op | source)
XLA Modules:
  0.0 350.8 jit_solution(9514415767228485865)
XLA Ops:
  9.7 1.8 gather_fusion.1
  11.5 1.6 gather.47
  13.1 1.4 fusion.18
  14.5 2.8 gather_fusion.2
  17.3 4.8 %copy.50 = bf16[8,2,32,16,256]{4,2,3,1,0:T(8,128)(2,1)} copy(bf16[8,2,32,16,256]{4,2,1,0,3:T(8,128)(2,1)} %bitcast.157) | data formatting | bytes 8388608 | tf_op jit(solution)/shard_map/jit(_take)/gather | solution.py:49
  22.1 4.2 %gather_fusion.3 = bf16[16,8,32,256]{3,2,1,0:T(8,128)(2,1)} fusion(bf16[8,2,32,16,256]{4,2,3,1,0:T(8,128)(2,1)} %copy.50, s32[16]{0:T(128)S(1)} %copy-done.2), kind=kCustom, calls=%fused_computation.3 | custom fusion | bytes 4194432 | tf_op jit(solution)/shard_map/gather | solution.py:51
  26.3 3.2 copy.51
  29.4 11.9 %all-to-all-start = ((bf16[128,1,32,256]{3,2,1,0:T(8,128)(2,1)}), bf16[128,1,32,256]{3,2,1,0:T(8,128)(2,1)}, u32[]{:S(2)}, u32[]{:S(2)}) async-start(bf16[128,1,32,256]{3,2,1,0:T(8,128)(2,1)} %bitcast.160), calls=%async_computation | async-start | bytes 4194304 | tf_op jit(solution)/shard_map/all_to_all | solution.py:55
  44.0 26.7 %all-to-all-done = bf16[128,1,32,256]{3,2,1,0:T(8,128)(2,1)} async-done(((bf16[128,1,32,256]{3,2,1,0:T(8,128)(2,1)}), bf16[128,1,32,256]{3,2,1,0:T(8,128)(2,1)}, u32[]{:S(2)}, u32[]{:S(2)}) %all-to-all-start) | async-done | bytes 2097184 | tf_op jit(solution)/shard_map/all_to_all | solution.py:55
  70.7 1.3 collective-permute-start
  72.2 1.2 gather_fusion.5
  75.1 5.0 %compare_and_fusion.1 = (pred[128]{0:T(512)(128)(4,1)S(1)}, s32[128]{0:T(128)S(1)}) fusion(s32[128]{0:T(128)S(1)} %convert_reduce_fusion.2, s32[]{:T(128)} %bitcast.12, s32[]{:T(128)} %bitcast.11, s32[]{:T(128)} %bitcast.10, s32[]{:T(128)} %bitcast.9, s32[]{:T(128)} %bitcast.8, s32[]{:T(128)} %bitcast.7, s32[]{:T(128)} %bitcast.6, s32[]{:T(128)} %bitcast.5), kind=kLoop, calls=%fused_computation.89 | loop fusion | flops 4224 | bytes 1184 | tf_op jit(solution)/shard_map/jit(_take)/and | solution.py:133
  81.1 2.5 broadcast_select_fusion.1
  85.4 1.1 fusion.1
  86.4 1.4 fusion.22
  89.1 20.1 %all_to_all.20 = bf16[8,128,512]{2,1,0:T(8,128)(2,1)S(1)} all-to-all(bf16[8,128,512]{2,1,0:T(8,128)(2,1)S(1)} %broadcast_in_dim.132), channel_id=1, replica_groups=mesh['replica'=8,'tensor'=16] {'replica'}, dimensions={0} | all-to-all | bytes 2097152 | tf_op jit(solution)/shard_map/all_to_all | solution.py:134
  109.2 4.3 %convolution_convert_fusion.1 = bf16[1024,2048]{1,0:T(8,128)(2,1)} fusion(bf16[1024,512]{1,0:T(8,128)(2,1)S(1)} %bitcast.168, bf16[512,2048]{1,0:T(8,128)(2,1)S(1)} %copy-done), kind=kOutput, calls=%fused_computation.15 | convolution fusion | flops 2149580800 | bytes 7340032 | tf_op jit(solution)/shard_map/dot_general | solution.py:141
  113.5 5.1 %all-to-all-start.2 = ((bf16[16,64,2048]{2,1,0:T(8,128)(2,1)}), bf16[16,64,2048]{2,1,0:T(8,128)(2,1)}, u32[]{:S(2)}, u32[]{:S(2)}) async-start(bf16[16,64,2048]{2,1,0:T(8,128)(2,1)} %bitcast.167), calls=%async_computation.2 | async-start | bytes 8388608 | tf_op jit(solution)/shard_map/all_to_all | solution.py:149
  118.8 52.4 %all-to-all-done.2 = bf16[16,64,2048]{2,1,0:T(8,128)(2,1)} async-done(((bf16[16,64,2048]{2,1,0:T(8,128)(2,1)}), bf16[16,64,2048]{2,1,0:T(8,128)(2,1)}, u32[]{:S(2)}, u32[]{:S(2)}) %all-to-all-start.2) | async-done | bytes 4194336 | tf_op jit(solution)/shard_map/all_to_all | solution.py:149
  171.2 3.0 convert_reduce_fusion.1
  174.2 1.1 multiply_reduce_fusion
  176.0 1.8 collective-permute-done.1
  178.4 3.3 collective-permute-done.2
  182.1 3.6 %collective-permute-done.3 = f32[64]{0:T(128)S(1)} collective-permute-done((f32[64]{0:T(128)S(1)}, f32[64]{0:T(128)S(1)}, u32[]{:S(2)}, u32[]{:S(2)}) %collective-permute-start.3) | collective-permute-done | bytes 288 | tf_op jit(solution)/shard_map/ppermute | solution.py:163
  185.7 1.8 multiply_convert_fusion
  187.5 14.2 %copy.67 = bf16[256,8,2,1664]{3,1,2,0:T(8,128)(2,1)} copy(bf16[256,8,2,1664]{3,2,1,0:T(2,128)(2,1)} %bitcast.158) | data formatting | bytes 27262976
  201.8 29.8 %all-gather.2.cloned.1.call-done = bf16[1024,2048]{1,0:T(8,128)(2,1)} async-done(((bf16[64,2048]{1,0:T(8,128)(2,1)}), bf16[1024,2048]{1,0:T(8,128)(2,1)}) %all-gather.2.cloned.1.call-update) | async-done | bytes 4194320 | tf_op jit(solution)/shard_map/all_gather | solution.py:170
  231.6 19.7 %convolution_convert_fusion = bf16[1024,3328]{1,0:T(8,128)(2,1)S(1)} fusion(bf16[1024,2048]{1,0:T(8,128)(2,1)} %all-gather.2.cloned.1.call-done, bf16[2048,3328]{1,0:T(8,128)(2,1)} %bitcast.159), kind=kOutput, calls=%fused_computation.9 | convolution fusion | flops 13962051584 | bytes 24641536 | tf_op jit(solution)/shard_map/dot_general | solution.py:172
  251.3 85.2 %all_to_all.21 = bf16[8,128,3328]{2,1,0:T(8,128)(2,1)S(1)} all-to-all(bf16[8,128,3328]{2,1,0:T(8,128)(2,1)S(1)} %bitcast.162), channel_id=1, replica_groups=mesh['replica'=8,'tensor'=16] {'replica'}, dimensions={0} | all-to-all | bytes 13631488 | tf_op jit(solution)/shard_map/all_to_all | solution.py:173
  336.5 2.1 convert_reduce_fusion
  338.6 2.7 copy.58
  341.3 1.6 fusion.26
  (65 shorter events, 14.2 us)
Async XLA Ops:
  6.5 102.7 %copy-start = (bf16[512,2048]{1,0:T(8,128)(2,1)S(1)}, bf16[512,2048]{1,0:T(8,128)(2,1)}, u32[]{:S(2)}) copy-start(bf16[512,2048]{1,0:T(8,128)(2,1)} %param.23) | copy-start | bytes 6291460
  17.3 4.8 %copy-start.2 = (s32[16]{0:T(128)S(1)}, s32[16]{0:T(128)}, u32[]{:S(2)}) copy-start(s32[16]{0:T(128)} %constant.223) | copy-start | bytes 196
  26.3 45.8 %copy-start.5 = (s32[64]{0:T(128)S(1)}, s32[64]{0:T(128)}, u32[]{:S(2)}) copy-start(s32[64]{0:T(128)} %param.21) | copy-start | bytes 772
  26.3 45.9 %copy-start.3 = (bf16[128,512]{1,0:T(8,128)(2,1)S(1)}, bf16[128,512]{1,0:T(8,128)(2,1)}, u32[]{:S(2)}) copy-start(bf16[128,512]{1,0:T(8,128)(2,1)} %param.16) | copy-start | bytes 393220
  29.4 41.3 %all-to-all-start = ((bf16[128,1,32,256]{3,2,1,0:T(8,128)(2,1)}), bf16[128,1,32,256]{3,2,1,0:T(8,128)(2,1)}, u32[]{:S(2)}, u32[]{:S(2)}) async-start(bf16[128,1,32,256]{3,2,1,0:T(8,128)(2,1)} %bitcast.160), calls=%async_computation | async-start | bytes 4194304 | tf_op jit(solution)/shard_map/all_to_all | solution.py:55
  70.7 10.4 %collective-permute-start = (bf16[128,1,32,256]{3,2,1,0:T(8,128)(2,1)}, bf16[128,1,32,256]{3,2,1,0:T(8,128)(2,1)}, u32[]{:S(2)}, u32[]{:S(2)}) collective-permute-start(bf16[128,1,32,256]{3,2,1,0:T(8,128)(2,1)} %all-to-all-done), channel_id=1, source_target_pairs={{0,1},{1,0},{2,3},{3,2},{4,5},{5,4},{6,7},{7,6},{8,9},{9,8},{10,11... | collective-permute-start | bytes 6291464 | tf_op jit(solution)/shard_map/ppermute | solution.py:58
  113.5 57.7 %all-to-all-start.2 = ((bf16[16,64,2048]{2,1,0:T(8,128)(2,1)}), bf16[16,64,2048]{2,1,0:T(8,128)(2,1)}, u32[]{:S(2)}, u32[]{:S(2)}) async-start(bf16[16,64,2048]{2,1,0:T(8,128)(2,1)} %bitcast.167), calls=%async_computation.2 | async-start | bytes 8388608 | tf_op jit(solution)/shard_map/all_to_all | solution.py:149
  118.6 63.5 %copy-start.4 = (bf16[2048]{0:T(1024)(128)(2,1)S(1)}, bf16[2048]{0:T(1024)(128)(2,1)}, u32[]{:S(2)}) copy-start(bf16[2048]{0:T(1024)(128)(2,1)} %param.25) | copy-start | bytes 12292
  118.6 113.0 %all-gather.2.cloned.1.call-start = ((), (), s32[]{:S(2)}) async-start(), calls=%async_computation.4 | async-start | bytes 4456448 | tf_op jit(solution)/shard_map/all_gather | solution.py:170
  175.4 2.5 collective-permute-start.1
  177.9 3.9 %collective-permute-start.2 = (f32[64]{0:T(128)S(1)}, f32[64]{0:T(128)S(1)}, u32[]{:S(2)}, u32[]{:S(2)}) collective-permute-start(f32[64]{0:T(128)S(1)} %add.227), channel_id=1, source_target_pairs={{0,32},{16,48},{32,0},{48,16},{64,96},{80,112},{96,64},{112,80},{1... | collective-permute-start | bytes 776 | tf_op jit(solution)/shard_map/ppermute | solution.py:163
  181.8 3.9 %collective-permute-start.3 = (f32[64]{0:T(128)S(1)}, f32[64]{0:T(128)S(1)}, u32[]{:S(2)}, u32[]{:S(2)}) collective-permute-start(f32[64]{0:T(128)S(1)} %add.228), channel_id=1, source_target_pairs={{0,64},{16,80},{32,96},{48,112},{64,0},{80,16},{96,32},{112,48},{1... | collective-permute-start | bytes 776 | tf_op jit(solution)/shard_map/ppermute | solution.py:163
  336.5 7.4 %copy-start.1 = (bf16[512,2048]{1,0:T(8,128)(2,1)S(1)}, bf16[512,2048]{1,0:T(8,128)(2,1)}, u32[]{:S(2)}) copy-start(bf16[512,2048]{1,0:T(8,128)(2,1)} %param.23) | copy-start | bytes 6291460
Sparse Core Ops, SparseCore 0:
  187.6 43.8 all-gather.1

commit v5 on v4

--- a/solution.py
+++ b/solution.py
@@ -30,10 +30,10 @@
     norm_gain,
     gate_up,
 ):
-    replicas = lax.axis_size("replica")
-    tensors = lax.axis_size("tensor")
-    replica_idx = lax.axis_index("replica")
-    tensor_idx = lax.axis_index("tensor")
+    replicas = lax.axis_size(("zh", "y"))
+    tensors = lax.axis_size(("x", "zl", "core"))
+    replica_idx = lax.axis_index(("zh", "y"))
+    tensor_idx = lax.axis_index(("x", "zl", "core"))
     sessions = SHARE * replicas
     heads_local = HEADS // tensors
     pair_width = 2 * HD
@@ -53,9 +53,9 @@
         replicas * tensors, SHARE, half, pair_width
     )
     arrived = lax.all_to_all(
-        outgoing, ("replica", "tensor"), split_axis=0, concat_axis=0, tiled=True
-    )
-    partner = lax.ppermute(arrived, "tensor", [(i, i ^ 1) for i in range(tensors)])
+        outgoing, ("zh", "y", "x", "zl", "core"), split_axis=0, concat_axis=0, tiled=True
+    )
+    partner = lax.ppermute(arrived, ("x", "zl", "core"), [(i, i ^ 1) for i in range(tensors)])
     mine_first = (tensor_idx % 2) == 0
     low_half = jnp.where(mine_first, arrived, partner)
     high_half = jnp.where(mine_first, partner, arrived)
@@ -133,7 +133,7 @@
     attended = jnp.take(slot_attended, back_index, axis=0)
     gathered = lax.all_to_all(
         jnp.broadcast_to(attended[None], (replicas,) + attended.shape),
-        "replica",
+        ("zh", "y"),
         split_axis=0,
         concat_axis=0,
         tiled=True,
@@ -148,7 +148,7 @@
     part_rows = all_rows // tensors
     head_parts = lax.all_to_all(
         partial_out.astype(jnp.bfloat16).reshape(tensors, part_rows, width),
-        "tensor",
+        ("x", "zl", "core"),
         split_axis=0,
         concat_axis=0,
         tiled=True,
@@ -161,41 +161,59 @@
     step = 1
     while step < replicas:
         squares = squares + lax.ppermute(
-            squares, "replica", [(i, i ^ step) for i in range(replicas)]
+            squares, ("zh", "y"), [(i, i ^ step) for i in range(replicas)]
         )
         step *= 2
     normed_part = (
         carried * lax.rsqrt(squares / D + EPSILON)[:, None] * gain_row[None, :]
     ).astype(jnp.bfloat16)
-    normed = lax.all_gather(normed_part, "tensor", axis=0, tiled=True)
+    normed = lax.all_gather(normed_part, ("x", "zl", "core"), axis=0, tiled=True)
     weights_local = gate_up.reshape(gate_up.shape[0], 2 * gate_up.shape[2])
     slab = jnp.dot(normed, weights_local, preferred_element_type=jnp.float32)
-    slab_parts = lax.all_to_all(
-        slab.astype(jnp.bfloat16).reshape(replicas, rows_here, slab.shape[1]),
-        "replica",
-        split_axis=0,
-        concat_axis=0,
-        tiled=True,
-    )
-    summed = jnp.sum(slab_parts.astype(jnp.float32), axis=0)
+    slab_cols = slab.shape[1]
+    high = lax.axis_size("zh")
+    ring = lax.axis_size("y")
+    high_idx = lax.axis_index("zh")
+    by_ring = jnp.transpose(
+        slab.reshape(high, ring, rows_here, slab_cols), (1, 0, 2, 3)
+    ).astype(jnp.bfloat16)
+    ring_parts = lax.all_to_all(by_ring, "y", split_axis=0, concat_axis=0, tiled=True)
+    ring_sum = jnp.sum(ring_parts.astype(jnp.float32), axis=0)
+    keep = lax.dynamic_index_in_dim(ring_sum, high_idx, 0, keepdims=False)
+    give = lax.dynamic_index_in_dim(ring_sum, 1 - high_idx, 0, keepdims=False)
+    give_hi = give.astype(jnp.bfloat16)
+    give_lo = (give - give_hi.astype(jnp.float32)).astype(jnp.bfloat16)
+    got = lax.ppermute(
+        jnp.stack([give_hi, give_lo]), "zh", [(i, i ^ 1) for i in range(high)]
+    ).astype(jnp.float32)
+    summed = keep + got[0] + got[1]
     paired = summed.reshape(rows_here, 2, gate_up.shape[2])
     return (jax.nn.silu(paired[:, 0, :]) * paired[:, 1, :]).astype(jnp.bfloat16)
 
 
 def solution(mesh):
+    fine = jax.sharding.Mesh(
+        mesh.devices.reshape(2, 4, 4, 2, 2), ("zh", "y", "x", "zl", "core")
+    )
+    rep = ("zh", "y")
+    ten = ("x", "zl", "core")
+
+    def body(*args):
+        return per_device(*args)
+
     placed = (
-        P("replica", "tensor"),
-        P("replica", None),
-        P(("replica", "tensor"), None, None),
-        P(),
-        P(),
-        P(),
-        P(),
-        P("tensor", "replica"),
-        P(None, "replica"),
-        P("replica"),
-        P("replica", None, "tensor"),
+        P(rep, ten),
+        P(rep, None),
+        P(rep + ten, None, None),
+        P(),
+        P(),
+        P(),
+        P(),
+        P(ten, rep),
+        P(None, rep),
+        P(rep),
+        P(rep, None, ten),
     )
     return jax.shard_map(
-        per_device, mesh=mesh, in_specs=placed, out_specs=P("replica", "tensor"), check_vma=False
-    )
+        body, mesh=fine, in_specs=placed, out_specs=P(rep, ten), check_vma=False
+    )

time: 352 us -> 401 us (1.14)
  waiting for transfers between devices: 118 us -> 216 us
  blocking collectives: 105 us -> 20.1 us
  local copies, waits for them, and re-layouts: 44.4 us -> 65 us
  starting transfers between devices: 20.1 us -> 27.9 us
  other arithmetic: 22.4 us -> 29 us
    all_to_all x1 -> x0, blocking collectives: 85.2 us -> none  [per_device(): lax.all_to_all(slab.astype(jnp.bfloat16).reshape(replicas, rows_here, sla...]
    all_to_all x1 -> x2, waiting for transfers between devices: 26.7 us -> 103 us  [the longest x1 76.8 us: per_device(): lax.all_to_all(by_ring, 'y', split_axis=0, concat_axis=0, tiled=True)]
    ppermute x4 -> x5, waiting for transfers between devices: 8.83 us -> 45.6 us  [the longest x1 36.8 us: per_device(): lax.ppermute(jnp.stack([give_hi, give_lo]), 'zh', [(i, i ^ 1) for i in ra...]
    reshape x0 -> x1, local copies, waits for them, and re-layouts: none -> 29.8 us  [per_device(): weights_local = gate_up.reshape(gate_up.shape[0], 2 * gate_up.shape[2])]
    all_gather x1, waiting for transfers between devices: 29.8 us -> 14.3 us  [per_device(): lax.all_gather(normed_part, ('x', 'zl', 'core'), axis=0, tiled=True)]
    unnamed x15 -> x18, local copies, waits for them, and re-layouts: 14.4 us -> 1.88 us
    all_to_all x1 -> x2, starting transfers between devices: 11.9 us -> 17.3 us  [the longest x1 11.9 us: per_device(): lax.all_to_all(outgoing, ('zh', 'y', 'x', 'zl', 'core'), split_axis=0, co...]
  transfers between devices with their start and end apart: 7 -> 9, of which waited for: 6 -> 8; matrix products, arithmetic and copies ran while one was open for 7% -> 10% of each run, Pallas kernels for 0% -> 0%
where the time goes in v5:
time: 401 us; the launch traced here: 399 us
  waiting for transfers between devices  216 us (54%)
  local copies, waits for them, and re-layouts  65 us (16%)
  other arithmetic  29 us (7%)
  starting transfers between devices  27.9 us (7%)
  matrix products  27.1 us (7%)
  blocking collectives  20.1 us (5%)
  between operations  13.7 us (3%)
    all_to_all x1, waiting for transfers between devices, per_device(): lax.all_to_all(by_ring, 'y', split_axis=0, concat_axis=0, tiled=True)  76.8 us
    all_to_all x1, waiting for transfers between devices, per_device(): lax.all_to_all(partial_out.astype(jnp.bfloat16).reshape(tensors, part_row...  52.4 us
    ppermute x1, waiting for transfers between devices, per_device(): lax.ppermute(jnp.stack([give_hi, give_lo]), 'zh', [(i, i ^ 1) for i in ra...  36.8 us
    reshape x1, local copies, waits for them, and re-layouts, per_device(): weights_local = gate_up.reshape(gate_up.shape[0], 2 * gate_up.shape[2])  29.8 us
    all_to_all x1, waiting for transfers between devices, per_device(): lax.all_to_all(outgoing, ('zh', 'y', 'x', 'zl', 'core'), split_axis=0, co...  26.7 us
    all_to_all x1, blocking collectives, per_device(): lax.all_to_all(jnp.broadcast_to(attended[None], (replicas,) + attended.sh...  20.1 us
    dot_general x1, matrix products, per_device(): slab = jnp.dot(normed, weights_local, preferred_element_type=jnp.float32)  19.6 us
    all_gather x1, waiting for transfers between devices, per_device(): lax.all_gather(normed_part, ('x', 'zl', 'core'), axis=0, tiled=True)  14.3 us
  transfers between devices with their start and end apart: 9, of which 8 were waited for; matrix products, arithmetic and copies ran while one was open for 10% of the time, Pallas kernels for 0%

profile of v5, /device:TPU:1, one launch (start us, length us, event | category | flops | bytes accessed | tf_op | source)
XLA Modules:
  0.0 398.7 jit_solution(4797066843837476393)
XLA Ops:
  9.0 1.8 gather_fusion.1
  10.9 1.6 gather.47
  13.9 2.8 gather_fusion.2
  16.6 4.8 %copy.52 = bf16[8,2,32,16,256]{4,2,3,1,0:T(8,128)(2,1)} copy(bf16[8,2,32,16,256]{4,2,1,0,3:T(8,128)(2,1)} %bitcast.163) | data formatting | bytes 8388608 | tf_op jit(solution)/shard_map/jit(_take)/gather | solution.py:49
  21.4 4.2 %gather_fusion.3 = bf16[16,8,32,256]{3,2,1,0:T(8,128)(2,1)} fusion(bf16[8,2,32,16,256]{4,2,3,1,0:T(8,128)(2,1)} %copy.52, s32[16]{0:T(128)S(1)} %copy-done.3), kind=kCustom, calls=%fused_computation.3 | custom fusion | bytes 4194432 | tf_op jit(solution)/shard_map/gather | solution.py:51
  25.6 3.2 copy.53
  28.8 11.9 %all-to-all-start = ((bf16[128,1,32,256]{3,2,1,0:T(8,128)(2,1)}), bf16[128,1,32,256]{3,2,1,0:T(8,128)(2,1)}, u32[]{:S(2)}, u32[]{:S(2)}) async-start(bf16[128,1,32,256]{3,2,1,0:T(8,128)(2,1)} %bitcast.164), calls=%async_computation | async-start | bytes 4194304 | tf_op jit(solution)/shard_map/all_to_all | solution.py:55
  43.3 26.7 %all-to-all-done = bf16[128,1,32,256]{3,2,1,0:T(8,128)(2,1)} async-done(((bf16[128,1,32,256]{3,2,1,0:T(8,128)(2,1)}), bf16[128,1,32,256]{3,2,1,0:T(8,128)(2,1)}, u32[]{:S(2)}, u32[]{:S(2)}) %all-to-all-start) | async-done | bytes 2097184 | tf_op jit(solution)/shard_map/all_to_all | solution.py:55
  74.5 5.0 %compare_and_fusion.1 = (pred[128]{0:T(512)(128)(4,1)S(1)}, s32[128]{0:T(128)S(1)}) fusion(s32[128]{0:T(128)S(1)} %convert_reduce_fusion.2, s32[]{:T(128)} %bitcast.12, s32[]{:T(128)} %bitcast.11, s32[]{:T(128)} %bitcast.10, s32[]{:T(128)} %bitcast.9, s32[]{:T(128)} %bitcast.8, s32[]{:T(128)} %bitcast.7, s32[]{:T(128)} %bitcast.6, s32[]{:T(128)} %bitcast.5), kind=kLoop, calls=%fused_computation.97 | loop fusion | flops 4224 | bytes 1184 | tf_op jit(solution)/shard_map/jit(_take)/and | solution.py:133
  80.5 2.5 broadcast_select_fusion.1
  88.5 20.1 %all_to_all.20 = bf16[8,128,512]{2,1,0:T(8,128)(2,1)S(1)} all-to-all(bf16[8,128,512]{2,1,0:T(8,128)(2,1)S(1)} %broadcast_in_dim.132), channel_id=1, replica_groups=mesh['zh'=2,'y'=4,'x'=4,'zl'=2,'core'=2] {'zh','y'}, dimensions={0} | all-to-all | bytes 2097152 | tf_op jit(solution)/shard_map/all_to_all | solution.py:134
  108.6 4.3 %convolution_convert_fusion = bf16[1024,2048]{1,0:T(8,128)(2,1)} fusion(bf16[1024,512]{1,0:T(8,128)(2,1)S(1)} %bitcast.171, bf16[512,2048]{1,0:T(8,128)(2,1)S(1)} %copy-done), kind=kOutput, calls=%fused_computation.18 | convolution fusion | flops 2149580800 | bytes 7340032 | tf_op jit(solution)/shard_map/dot_general | solution.py:141
  112.9 5.1 %all-to-all-start.2 = ((bf16[16,64,2048]{2,1,0:T(8,128)(2,1)}), bf16[16,64,2048]{2,1,0:T(8,128)(2,1)}, u32[]{:S(2)}, u32[]{:S(2)}) async-start(bf16[16,64,2048]{2,1,0:T(8,128)(2,1)} %bitcast.170), calls=%async_computation.2 | async-start | bytes 8388608 | tf_op jit(solution)/shard_map/all_to_all | solution.py:149
  118.2 52.4 %all-to-all-done.2 = bf16[16,64,2048]{2,1,0:T(8,128)(2,1)} async-done(((bf16[16,64,2048]{2,1,0:T(8,128)(2,1)}), bf16[16,64,2048]{2,1,0:T(8,128)(2,1)}, u32[]{:S(2)}, u32[]{:S(2)}) %all-to-all-start.2) | async-done | bytes 4194336 | tf_op jit(solution)/shard_map/all_to_all | solution.py:149
  170.6 3.0 convert_reduce_fusion.1
  175.4 1.8 collective-permute-done.1
  177.8 3.3 collective-permute-done.2
  181.5 3.6 collective-permute-done.3
  185.1 1.8 multiply_convert_fusion
  186.9 29.8 %reshape.405 = bf16[2048,3328,1,1]{1,0,2,3:T(8,128)(2,1)} reshape(bf16[2048,2,1664]{2,1,0:T(2,128)(2,1)} %param.26) | data formatting | bytes 27262976 | tf_op jit(solution)/shard_map/reshape | solution.py:171
  216.7 14.3 %all-gather.2.cloned.1.call-done = bf16[1024,2048]{1,0:T(8,128)(2,1)} async-done(((bf16[64,2048]{1,0:T(8,128)(2,1)}), bf16[1024,2048]{1,0:T(8,128)(2,1)}) %all-gather.2.cloned.1.call-update) | async-done | bytes 4194320 | tf_op jit(solution)/shard_map/all_gather | solution.py:170
  231.0 19.6 %fusion.5 = bf16[4,2,128,3328]{3,2,0,1:T(8,128)(2,1)S(1)} fusion(bf16[2,4,128,2048]{3,2,1,0:T(8,128)(2,1)} %bitcast.179, bf16[2048,3328,1,1]{1,0,2,3:T(8,128)(2,1)} %reshape.405), kind=kOutput, calls=%fused_computation.12 | convolution fusion | flops 13962051584 | bytes 24641536 | tf_op jit(solution)/shard_map/dot_general | solution.py:172
  250.6 3.3 copy.60
  254.0 5.3 %all-to-all-start.3 = ((bf16[4,2,128,3328]{3,2,1,0:T(8,128)(2,1)}), bf16[4,2,128,3328]{3,2,1,0:T(8,128)(2,1)}, u32[]{:S(2)}, u32[]{:S(2)}) async-start(bf16[4,2,128,3328]{3,2,1,0:T(8,128)(2,1)} %copy.60), calls=%async_computation.3 | async-start | bytes 13631488 | tf_op jit(solution)/shard_map/all_to_all | solution.py:180
  259.3 76.8 %all-to-all-done.3 = bf16[4,2,128,3328]{3,2,1,0:T(8,128)(2,1)} async-done(((bf16[4,2,128,3328]{3,2,1,0:T(8,128)(2,1)}), bf16[4,2,128,3328]{3,2,1,0:T(8,128)(2,1)}, u32[]{:S(2)}, u32[]{:S(2)}) %all-to-all-start.3) | async-done | bytes 6815776 | tf_op jit(solution)/shard_map/all_to_all | solution.py:180
  336.1 4.4 %convert_reduce_fusion = f32[2,128,3328]{2,1,0:T(8,128)S(1)} fusion(bf16[4,2,128,3328]{3,2,1,0:T(8,128)(2,1)} %all-to-all-done.3), kind=kLoop, calls=%fused_computation.9 | loop fusion | flops 5963776 | bytes 10223616 | tf_op jit(solution)/shard_map/reduce_sum | solution.py:181
  340.4 1.7 copy-done.2
  343.7 2.5 collective-permute-start.4
  346.2 36.8 %collective-permute-done.4 = bf16[2,128,3328]{2,1,0:T(8,128)(2,1)S(1)} collective-permute-done((bf16[2,128,3328]{2,1,0:T(8,128)(2,1)}, bf16[2,128,3328]{2,1,0:T(8,128)(2,1)S(1)}, u32[]{:S(2)}, u32[]{:S(2)}) %collective-permute-start.4) | collective-permute-done | bytes 1703968 | tf_op jit(solution)/shard_map/ppermute | solution.py:186
  383.3 3.2 slice_add_fusion
  386.5 2.7 copy.62
  389.2 1.6 fusion.34
  (77 shorter events, 22.9 us)
Async XLA Ops:
  6.5 102.1 %copy-start = (bf16[512,2048]{1,0:T(8,128)(2,1)S(1)}, bf16[512,2048]{1,0:T(8,128)(2,1)}, u32[]{:S(2)}) copy-start(bf16[512,2048]{1,0:T(8,128)(2,1)} %param.23) | copy-start | bytes 6291460
  6.5 5.9 %copy-start.6 = (s32[16]{0:T(128)S(1)}, s32[16]{0:T(128)}, u32[]{:S(2)}) copy-start(s32[16]{0:T(128)} %constant.233) | copy-start | bytes 196
  16.6 4.8 %copy-start.3 = (s32[16]{0:T(128)S(1)}, s32[16]{0:T(128)}, u32[]{:S(2)}) copy-start(s32[16]{0:T(128)} %constant.241) | copy-start | bytes 196
  25.6 45.8 %copy-start.4 = (bf16[128,512]{1,0:T(8,128)(2,1)S(1)}, bf16[128,512]{1,0:T(8,128)(2,1)}, u32[]{:S(2)}) copy-start(bf16[128,512]{1,0:T(8,128)(2,1)} %param.16) | copy-start | bytes 393220
  25.6 46.9 %copy-start.7 = (s32[64]{0:T(128)S(1)}, s32[64]{0:T(128)}, u32[]{:S(2)}) copy-start(s32[64]{0:T(128)} %param.21) | copy-start | bytes 772
  28.8 41.3 %all-to-all-start = ((bf16[128,1,32,256]{3,2,1,0:T(8,128)(2,1)}), bf16[128,1,32,256]{3,2,1,0:T(8,128)(2,1)}, u32[]{:S(2)}, u32[]{:S(2)}) async-start(bf16[128,1,32,256]{3,2,1,0:T(8,128)(2,1)} %bitcast.164), calls=%async_computation | async-start | bytes 4194304 | tf_op jit(solution)/shard_map/all_to_all | solution.py:55
  70.1 10.5 %collective-permute-start = (bf16[128,1,32,256]{3,2,1,0:T(8,128)(2,1)}, bf16[128,1,32,256]{3,2,1,0:T(8,128)(2,1)}, u32[]{:S(2)}, u32[]{:S(2)}) collective-permute-start(bf16[128,1,32,256]{3,2,1,0:T(8,128)(2,1)} %all-to-all-done), channel_id=1, source_target_pairs={{0,1},{1,0},{2,3},{3,2},{4,5},{5,4},{6,7},{7,6},{8,9},{9,8},{10,11... | collective-permute-start | bytes 6291464 | tf_op jit(solution)/shard_map/ppermute | solution.py:58
  112.9 57.7 %all-to-all-start.2 = ((bf16[16,64,2048]{2,1,0:T(8,128)(2,1)}), bf16[16,64,2048]{2,1,0:T(8,128)(2,1)}, u32[]{:S(2)}, u32[]{:S(2)}) async-start(bf16[16,64,2048]{2,1,0:T(8,128)(2,1)} %bitcast.170), calls=%async_computation.2 | async-start | bytes 8388608 | tf_op jit(solution)/shard_map/all_to_all | solution.py:149
  118.0 63.5 %copy-start.5 = (bf16[2048]{0:T(1024)(128)(2,1)S(1)}, bf16[2048]{0:T(1024)(128)(2,1)}, u32[]{:S(2)}) copy-start(bf16[2048]{0:T(1024)(128)(2,1)} %param.25) | copy-start | bytes 12292
  118.0 113.0 %all-gather.2.cloned.1.call-start = ((), (), s32[]{:S(2)}) async-start(), calls=%async_computation.4 | async-start | bytes 4456448 | tf_op jit(solution)/shard_map/all_gather | solution.py:170
  174.8 2.5 collective-permute-start.1
  177.3 3.9 collective-permute-start.2
  181.2 3.9 collective-permute-start.3
  254.0 82.1 %all-to-all-start.3 = ((bf16[4,2,128,3328]{3,2,1,0:T(8,128)(2,1)}), bf16[4,2,128,3328]{3,2,1,0:T(8,128)(2,1)}, u32[]{:S(2)}, u32[]{:S(2)}) async-start(bf16[4,2,128,3328]{3,2,1,0:T(8,128)(2,1)} %copy.60), calls=%async_computation.3 | async-start | bytes 13631488 | tf_op jit(solution)/shard_map/all_to_all | solution.py:180
  340.4 1.7 copy-start.2
  343.7 39.3 %collective-permute-start.4 = (bf16[2,128,3328]{2,1,0:T(8,128)(2,1)}, bf16[2,128,3328]{2,1,0:T(8,128)(2,1)S(1)}, u32[]{:S(2)}, u32[]{:S(2)}) collective-permute-start(bf16[2,128,3328]{2,1,0:T(8,128)(2,1)} %pad_maximum_fusion.1), channel_id=1, source_target_pairs={{0,64},{64,0},{1,65},{65,1},{2,66},{66,2},{3,67},{67,3},{4,68},{68... | collective-permute-start | bytes 5111816 | tf_op jit(solution)/shard_map/ppermute | solution.py:186
  383.3 8.5 %copy-start.1 = (bf16[512,2048]{1,0:T(8,128)(2,1)S(1)}, bf16[512,2048]{1,0:T(8,128)(2,1)}, u32[]{:S(2)}) copy-start(bf16[512,2048]{1,0:T(8,128)(2,1)} %param.23) | copy-start | bytes 6291460
Sparse Core Ops, SparseCore 0:
  187.0 43.9 all-gather.1

commit v6 on v4

--- a/solution.py
+++ b/solution.py
@@ -45,13 +45,14 @@
     page_index = jnp.take(my_column, from_here.reshape(-1), axis=0)
     chosen = jnp.take(kv_pool, page_index, axis=0).reshape(replicas, SHARE, PAGE, KVH, pair_width)
     half = PAGE // 2
-    core_half = np.arange(tensors) % 2
-    outgoing = jnp.take(chosen, owner_head, axis=3)
-    outgoing = outgoing.reshape(replicas, SHARE, 2, half, tensors, pair_width)
-    outgoing = outgoing[:, :, core_half, :, np.arange(tensors), :]
-    outgoing = jnp.transpose(outgoing, (1, 0, 2, 3, 4)).reshape(
-        replicas * tensors, SHARE, half, pair_width
-    )
+    lanes_per_head = tensors // KVH
+    outgoing = jnp.transpose(
+        chosen.reshape(replicas, 2, half, KVH, pair_width), (0, 3, 1, 2, 4)
+    )
+    outgoing = jnp.broadcast_to(
+        outgoing[:, :, None],
+        (replicas, KVH, lanes_per_head // 2, 2, half, pair_width),
+    ).reshape(replicas * tensors, SHARE, half, pair_width)
     arrived = lax.all_to_all(
         outgoing, ("replica", "tensor"), split_axis=0, concat_axis=0, tiled=True
     )
@@ -178,8 +179,10 @@
         tiled=True,
     )
     summed = jnp.sum(slab_parts.astype(jnp.float32), axis=0)
-    paired = summed.reshape(rows_here, 2, gate_up.shape[2])
-    return (jax.nn.silu(paired[:, 0, :]) * paired[:, 1, :]).astype(jnp.bfloat16)
+    ff_here = gate_up.shape[2]
+    gate = summed[:, :ff_here]
+    up = summed[:, ff_here:]
+    return (jax.nn.silu(gate) * up).astype(jnp.bfloat16)
 
 
 def solution(mesh):

time: 352 us -> 333 us (0.946)
  local copies, waits for them, and re-layouts: 44.4 us -> 28.8 us
    gather x3 -> x0, local copies, waits for them, and re-layouts: 11.8 us -> none  [the longest x2 7.56 us: per_device(): outgoing = jnp.take(chosen, owner_head, axis=3)]
    unnamed x15 -> x13, local copies, waits for them, and re-layouts: 14.4 us -> 14.4 us
  transfers between devices with their start and end apart: 7 -> 7, of which waited for: 6 -> 6; matrix products, arithmetic and copies ran while one was open for 7% -> 8% of each run, Pallas kernels for 0% -> 0%
where the time goes in v6:
time: 333 us; the launch traced here: 332 us
  waiting for transfers between devices  118 us (35%)
  blocking collectives  105 us (32%)
  local copies, waits for them, and re-layouts  28.8 us (9%)
  matrix products  27.2 us (8%)
  starting transfers between devices  20.1 us (6%)
  other arithmetic  19.1 us (6%)
  between operations  13.7 us (4%)
    all_to_all x1, blocking collectives, per_device(): lax.all_to_all(slab.astype(jnp.bfloat16).reshape(replicas, rows_here, sla...  85.3 us
    all_to_all x1, waiting for transfers between devices, per_device(): lax.all_to_all(partial_out.astype(jnp.bfloat16).reshape(tensors, part_row...  52.6 us
    all_gather x1, waiting for transfers between devices, per_device(): normed = lax.all_gather(normed_part, 'tensor', axis=0, tiled=True)  29.8 us
    all_to_all x1, waiting for transfers between devices, per_device(): lax.all_to_all(outgoing, ('replica', 'tensor'), split_axis=0, concat_axis...  26.7 us
    all_to_all x1, blocking collectives, per_device(): lax.all_to_all(jnp.broadcast_to(attended[None], (replicas,) + attended.sh...  20.1 us
    dot_general x1, matrix products, per_device(): slab = jnp.dot(normed, weights_local, preferred_element_type=jnp.float32)  19.7 us
    unnamed x13, local copies, waits for them, and re-layouts  14.4 us
    all_to_all x1, starting transfers between devices, per_device(): lax.all_to_all(outgoing, ('replica', 'tensor'), split_axis=0, concat_axis...  11.9 us
  transfers between devices with their start and end apart: 7, of which 6 were waited for; matrix products, arithmetic and copies ran while one was open for 8% of the time, Pallas kernels for 0%

profile of v6, /device:TPU:1, one launch (start us, length us, event | category | flops | bytes accessed | tf_op | source)
XLA Modules:
  0.0 332.2 jit_solution(8920408444918263134)
XLA Ops:
  6.5 0.9 constant_dynamic-slice_fusion.1
  9.0 2.8 gather_fusion.1
  11.8 1.9 gather.38
  14.4 1.6 broadcast_in_dim.105
  16.0 11.9 %all-to-all-start = ((bf16[128,1,32,256]{3,2,1,0:T(8,128)(2,1)}), bf16[128,1,32,256]{3,2,1,0:T(8,128)(2,1)}, u32[]{:S(2)}, u32[]{:S(2)}) async-start(bf16[128,1,32,256]{3,2,1,0:T(8,128)(2,1)} %bitcast.140), calls=%async_computation | async-start | bytes 4194304 | tf_op jit(solution)/shard_map/all_to_all | solution.py:56
  29.7 0.8 constant_dynamic-slice_fusion
  30.5 26.7 %all-to-all-done = bf16[128,1,32,256]{3,2,1,0:T(8,128)(2,1)} async-done(((bf16[128,1,32,256]{3,2,1,0:T(8,128)(2,1)}), bf16[128,1,32,256]{3,2,1,0:T(8,128)(2,1)}, u32[]{:S(2)}, u32[]{:S(2)}) %all-to-all-start) | async-done | bytes 2097184 | tf_op jit(solution)/shard_map/all_to_all | solution.py:56
  57.2 1.3 collective-permute-start
  58.7 1.2 gather_fusion.3
  59.9 1.0 gather_fusion.2
  61.7 5.0 %compare_and_fusion.1 = (pred[128]{0:T(512)(128)(4,1)S(1)}, s32[128]{0:T(128)S(1)}) fusion(s32[128]{0:T(128)S(1)} %convert_reduce_fusion.2, s32[]{:T(128)} %bitcast.12, s32[]{:T(128)} %bitcast.11, s32[]{:T(128)} %bitcast.10, s32[]{:T(128)} %bitcast.9, s32[]{:T(128)} %bitcast.8, s32[]{:T(128)} %bitcast.7, s32[]{:T(128)} %bitcast.6, s32[]{:T(128)} %bitcast.5), kind=kLoop, calls=%fused_computation.83 | loop fusion | flops 4224 | bytes 1184 | tf_op jit(solution)/shard_map/jit(_take)/and | solution.py:134
  67.7 2.5 broadcast_select_fusion.1
  70.6 0.9 bitcast_reduce_fusion
  71.9 1.1 fusion.1
  73.0 1.4 fusion.21
  74.6 0.8 gather_fusion.4
  75.7 20.1 %all_to_all.20 = bf16[8,128,512]{2,1,0:T(8,128)(2,1)S(1)} all-to-all(bf16[8,128,512]{2,1,0:T(8,128)(2,1)S(1)} %broadcast_in_dim.116), channel_id=1, replica_groups=mesh['replica'=8,'tensor'=16] {'replica'}, dimensions={0} | all-to-all | bytes 2097152 | tf_op jit(solution)/shard_map/all_to_all | solution.py:135
  95.8 4.3 %convolution_convert_fusion.1 = bf16[1024,2048]{1,0:T(8,128)(2,1)} fusion(bf16[1024,512]{1,0:T(8,128)(2,1)S(1)} %bitcast.146, bf16[512,2048]{1,0:T(8,128)(2,1)S(1)} %copy-done), kind=kOutput, calls=%fused_computation.13 | convolution fusion | flops 2149580800 | bytes 7340032 | tf_op jit(solution)/shard_map/dot_general | solution.py:142
  100.1 5.1 %all-to-all-start.2 = ((bf16[16,64,2048]{2,1,0:T(8,128)(2,1)}), bf16[16,64,2048]{2,1,0:T(8,128)(2,1)}, u32[]{:S(2)}, u32[]{:S(2)}) async-start(bf16[16,64,2048]{2,1,0:T(8,128)(2,1)} %bitcast.145), calls=%async_computation.2 | async-start | bytes 8388608 | tf_op jit(solution)/shard_map/all_to_all | solution.py:150
  105.2 52.6 %all-to-all-done.2 = bf16[16,64,2048]{2,1,0:T(8,128)(2,1)} async-done(((bf16[16,64,2048]{2,1,0:T(8,128)(2,1)}), bf16[16,64,2048]{2,1,0:T(8,128)(2,1)}, u32[]{:S(2)}, u32[]{:S(2)}) %all-to-all-start.2) | async-done | bytes 4194336 | tf_op jit(solution)/shard_map/all_to_all | solution.py:150
  157.8 3.0 convert_reduce_fusion.1
  160.8 1.1 multiply_reduce_fusion
  162.8 1.8 collective-permute-done.1
  165.2 3.3 %collective-permute-done.2 = f32[64]{0:T(128)S(1)} collective-permute-done((f32[64]{0:T(128)S(1)}, f32[64]{0:T(128)S(1)}, u32[]{:S(2)}, u32[]{:S(2)}) %collective-permute-start.2) | collective-permute-done | bytes 288 | tf_op jit(solution)/shard_map/ppermute | solution.py:164
  168.8 3.6 %collective-permute-done.3 = f32[64]{0:T(128)S(1)} collective-permute-done((f32[64]{0:T(128)S(1)}, f32[64]{0:T(128)S(1)}, u32[]{:S(2)}, u32[]{:S(2)}) %collective-permute-start.3) | collective-permute-done | bytes 288 | tf_op jit(solution)/shard_map/ppermute | solution.py:164
  172.5 1.8 multiply_convert_fusion
  174.3 14.2 %copy.49 = bf16[256,8,2,1664]{3,1,2,0:T(8,128)(2,1)} copy(bf16[256,8,2,1664]{3,2,1,0:T(2,128)(2,1)} %bitcast.138) | data formatting | bytes 27262976
  188.5 29.8 %all-gather.2.cloned.1.call-done = bf16[1024,2048]{1,0:T(8,128)(2,1)} async-done(((bf16[64,2048]{1,0:T(8,128)(2,1)}), bf16[1024,2048]{1,0:T(8,128)(2,1)}) %all-gather.2.cloned.1.call-update) | async-done | bytes 4194320 | tf_op jit(solution)/shard_map/all_gather | solution.py:171
  218.3 19.7 %convolution_convert_fusion = bf16[1024,3328]{1,0:T(8,128)(2,1)S(1)} fusion(bf16[1024,2048]{1,0:T(8,128)(2,1)} %all-gather.2.cloned.1.call-done, bf16[2048,3328]{1,0:T(8,128)(2,1)} %bitcast.139), kind=kOutput, calls=%fused_computation.7 | convolution fusion | flops 13962051584 | bytes 24641536 | tf_op jit(solution)/shard_map/dot_general | solution.py:173
  238.0 85.3 %all_to_all.21 = bf16[8,128,3328]{2,1,0:T(8,128)(2,1)S(1)} all-to-all(bf16[8,128,3328]{2,1,0:T(8,128)(2,1)S(1)} %bitcast.141), channel_id=1, replica_groups=mesh['replica'=8,'tensor'=16] {'replica'}, dimensions={0} | all-to-all | bytes 13631488 | tf_op jit(solution)/shard_map/all_to_all | solution.py:174
  323.4 1.0 convert_reduce_fusion
  324.3 1.0 fusion.24
  (58 shorter events, 8.9 us)
Async XLA Ops:
  6.5 89.2 %copy-start = (bf16[512,2048]{1,0:T(8,128)(2,1)S(1)}, bf16[512,2048]{1,0:T(8,128)(2,1)}, u32[]{:S(2)}) copy-start(bf16[512,2048]{1,0:T(8,128)(2,1)} %param.18) | copy-start | bytes 6291460
  14.4 44.2 %copy-start.4 = (s32[64]{0:T(128)S(1)}, s32[64]{0:T(128)}, u32[]{:S(2)}) copy-start(s32[64]{0:T(128)} %param.16) | copy-start | bytes 772
  14.4 44.3 %copy-start.2 = (bf16[128,512]{1,0:T(8,128)(2,1)S(1)}, bf16[128,512]{1,0:T(8,128)(2,1)}, u32[]{:S(2)}) copy-start(bf16[128,512]{1,0:T(8,128)(2,1)} %param.11) | copy-start | bytes 393220
  16.0 41.3 %all-to-all-start = ((bf16[128,1,32,256]{3,2,1,0:T(8,128)(2,1)}), bf16[128,1,32,256]{3,2,1,0:T(8,128)(2,1)}, u32[]{:S(2)}, u32[]{:S(2)}) async-start(bf16[128,1,32,256]{3,2,1,0:T(8,128)(2,1)} %bitcast.140), calls=%async_computation | async-start | bytes 4194304 | tf_op jit(solution)/shard_map/all_to_all | solution.py:56
  57.2 10.4 %collective-permute-start = (bf16[128,1,32,256]{3,2,1,0:T(8,128)(2,1)}, bf16[128,1,32,256]{3,2,1,0:T(8,128)(2,1)}, u32[]{:S(2)}, u32[]{:S(2)}) collective-permute-start(bf16[128,1,32,256]{3,2,1,0:T(8,128)(2,1)} %all-to-all-done), channel_id=1, source_target_pairs={{0,1},{1,0},{2,3},{3,2},{4,5},{5,4},{6,7},{7,6},{8,9},{9,8},{10,11... | collective-permute-start | bytes 6291464 | tf_op jit(solution)/shard_map/ppermute | solution.py:59
  100.1 57.7 %all-to-all-start.2 = ((bf16[16,64,2048]{2,1,0:T(8,128)(2,1)}), bf16[16,64,2048]{2,1,0:T(8,128)(2,1)}, u32[]{:S(2)}, u32[]{:S(2)}) async-start(bf16[16,64,2048]{2,1,0:T(8,128)(2,1)} %bitcast.145), calls=%async_computation.2 | async-start | bytes 8388608 | tf_op jit(solution)/shard_map/all_to_all | solution.py:150
  105.2 63.7 %copy-start.3 = (bf16[2048]{0:T(1024)(128)(2,1)S(1)}, bf16[2048]{0:T(1024)(128)(2,1)}, u32[]{:S(2)}) copy-start(bf16[2048]{0:T(1024)(128)(2,1)} %param.20) | copy-start | bytes 12292
  105.2 113.2 %all-gather.2.cloned.1.call-start = ((), (), s32[]{:S(2)}) async-start(), calls=%async_computation.4 | async-start | bytes 4456448 | tf_op jit(solution)/shard_map/all_gather | solution.py:171
  161.9 2.7 collective-permute-start.1
  164.6 3.9 %collective-permute-start.2 = (f32[64]{0:T(128)S(1)}, f32[64]{0:T(128)S(1)}, u32[]{:S(2)}, u32[]{:S(2)}) collective-permute-start(f32[64]{0:T(128)S(1)} %add.214), channel_id=1, source_target_pairs={{0,32},{16,48},{32,0},{48,16},{64,96},{80,112},{96,64},{112,80},{1... | collective-permute-start | bytes 776 | tf_op jit(solution)/shard_map/ppermute | solution.py:164
  168.5 3.9 %collective-permute-start.3 = (f32[64]{0:T(128)S(1)}, f32[64]{0:T(128)S(1)}, u32[]{:S(2)}, u32[]{:S(2)}) collective-permute-start(f32[64]{0:T(128)S(1)} %add.215), channel_id=1, source_target_pairs={{0,64},{16,80},{32,96},{48,112},{64,0},{80,16},{96,32},{112,48},{1... | collective-permute-start | bytes 776 | tf_op jit(solution)/shard_map/ppermute | solution.py:164
  238.0 87.3 %copy-start.1 = (bf16[512,2048]{1,0:T(8,128)(2,1)S(1)}, bf16[512,2048]{1,0:T(8,128)(2,1)}, u32[]{:S(2)}) copy-start(bf16[512,2048]{1,0:T(8,128)(2,1)} %param.18) | copy-start | bytes 6291460
Sparse Core Ops, SparseCore 0:
  174.4 43.8 all-gather.1

commit v7 on v6

--- a/solution.py
+++ b/solution.py
@@ -158,13 +158,15 @@
     my_residual = lax.dynamic_slice_in_dim(residual, tensor_idx * part_rows, part_rows, 0)
     carried = my_residual.astype(jnp.float32) + head_sum
     gain_row = norm_gain.astype(jnp.float32)
-    squares = jnp.sum(carried * carried, axis=1)
-    step = 1
-    while step < replicas:
-        squares = squares + lax.ppermute(
-            squares, "replica", [(i, i ^ step) for i in range(replicas)]
-        )
-        step *= 2
+    own_squares = jnp.sum(carried * carried, axis=1)
+    received = [own_squares] + [
+        lax.ppermute(own_squares, "replica", [(i, i ^ k) for i in range(replicas)])
+        for k in range(1, replicas)
+    ]
+    by_source = jnp.take(
+        jnp.stack(received), jnp.arange(replicas, dtype=jnp.int32) ^ replica_idx, axis=0
+    )
+    squares = jnp.sum(by_source, axis=0)
     normed_part = (
         carried * lax.rsqrt(squares / D + EPSILON)[:, None] * gain_row[None, :]
     ).astype(jnp.bfloat16)

time: 333 us -> 337 us (1.012)
  starting transfers between devices: 20.1 us -> 30.2 us
  waiting for transfers between devices: 118 us -> 111 us
    ppermute x3 -> x7, starting transfers between devices: 1.69 us -> 11.9 us  [per_device(): lax.ppermute(own_squares, 'replica', [(i, i ^ k) for i in range(replicas)])]
    ppermute x3 -> x7, waiting for transfers between devices: 8.83 us -> 1.52 us  [per_device(): lax.ppermute(own_squares, 'replica', [(i, i ^ k) for i in range(replicas)])]
  transfers between devices with their start and end apart: 7 -> 11, of which waited for: 6 -> 5; matrix products, arithmetic and copies ran while one was open for 8% -> 8% of each run, Pallas kernels for 0% -> 0%
where the time goes in v7:
time: 337 us; the launch traced here: 336 us
  waiting for transfers between devices  111 us (33%)
  blocking collectives  105 us (31%)
  starting transfers between devices  30.2 us (9%)
  local copies, waits for them, and re-layouts  29.4 us (9%)
  matrix products  27.2 us (8%)
  other arithmetic  19.2 us (6%)
  between operations  13.7 us (4%)
    all_to_all x1, blocking collectives, per_device(): lax.all_to_all(slab.astype(jnp.bfloat16).reshape(replicas, rows_here, sla...  85.3 us
    all_to_all x1, waiting for transfers between devices, per_device(): lax.all_to_all(partial_out.astype(jnp.bfloat16).reshape(tensors, part_row...  52.5 us
    all_gather x1, waiting for transfers between devices, per_device(): normed = lax.all_gather(normed_part, 'tensor', axis=0, tiled=True)  29.9 us
    all_to_all x1, waiting for transfers between devices, per_device(): lax.all_to_all(outgoing, ('replica', 'tensor'), split_axis=0, concat_axis...  26.7 us
    all_to_all x1, blocking collectives, per_device(): lax.all_to_all(jnp.broadcast_to(attended[None], (replicas,) + attended.sh...  20.1 us
    dot_general x1, matrix products, per_device(): slab = jnp.dot(normed, weights_local, preferred_element_type=jnp.float32)  19.7 us
    unnamed x13, local copies, waits for them, and re-layouts  14.4 us
    all_to_all x1, starting transfers between devices, per_device(): lax.all_to_all(outgoing, ('replica', 'tensor'), split_axis=0, concat_axis...  11.9 us
  transfers between devices with their start and end apart: 11, of which 5 were waited for; matrix products, arithmetic and copies ran while one was open for 8% of the time, Pallas kernels for 0%

profile of v7, /device:TPU:1, one launch (start us, length us, event | category | flops | bytes accessed | tf_op | source)
XLA Modules:
  0.0 335.8 jit_solution(7700906408553352681)
XLA Ops:
  6.5 0.9 constant_dynamic-slice_fusion.1
  9.0 2.8 gather_fusion.1
  11.8 1.9 gather.42
  14.4 1.6 broadcast_in_dim.115
  16.0 11.9 %all-to-all-start = ((bf16[128,1,32,256]{3,2,1,0:T(8,128)(2,1)}), bf16[128,1,32,256]{3,2,1,0:T(8,128)(2,1)}, u32[]{:S(2)}, u32[]{:S(2)}) async-start(bf16[128,1,32,256]{3,2,1,0:T(8,128)(2,1)} %bitcast.150), calls=%async_computation | async-start | bytes 4194304 | tf_op jit(solution)/shard_map/all_to_all | solution.py:56
  30.5 26.7 %all-to-all-done = bf16[128,1,32,256]{3,2,1,0:T(8,128)(2,1)} async-done(((bf16[128,1,32,256]{3,2,1,0:T(8,128)(2,1)}), bf16[128,1,32,256]{3,2,1,0:T(8,128)(2,1)}, u32[]{:S(2)}, u32[]{:S(2)}) %all-to-all-start) | async-done | bytes 2097184 | tf_op jit(solution)/shard_map/all_to_all | solution.py:56
  57.2 1.3 collective-permute-start
  58.7 1.2 gather_fusion.3
  59.9 1.0 gather_fusion.2
  61.7 5.0 %compare_and_fusion.2 = (pred[128]{0:T(512)(128)(4,1)S(1)}, s32[128]{0:T(128)S(1)}) fusion(s32[128]{0:T(128)S(1)} %convert_reduce_fusion.2, s32[]{:T(128)} %bitcast.12, s32[]{:T(128)} %bitcast.11, s32[]{:T(128)} %bitcast.10, s32[]{:T(128)} %bitcast.9, s32[]{:T(128)} %bitcast.8, s32[]{:T(128)} %bitcast.7, s32[]{:T(128)} %bitcast.6, s32[]{:T(128)} %bitcast.5), kind=kLoop, calls=%fused_computation.89 | loop fusion | flops 4224 | bytes 1184 | tf_op jit(solution)/shard_map/jit(_take)/and | solution.py:134
  67.7 2.5 broadcast_select_fusion.1
  71.9 1.1 fusion.1
  73.0 1.4 fusion.21
  75.7 20.1 %all_to_all.20 = bf16[8,128,512]{2,1,0:T(8,128)(2,1)S(1)} all-to-all(bf16[8,128,512]{2,1,0:T(8,128)(2,1)S(1)} %broadcast_in_dim.126), channel_id=1, replica_groups=mesh['replica'=8,'tensor'=16] {'replica'}, dimensions={0} | all-to-all | bytes 2097152 | tf_op jit(solution)/shard_map/all_to_all | solution.py:135
  95.8 4.3 %convolution_convert_fusion.1 = bf16[1024,2048]{1,0:T(8,128)(2,1)} fusion(bf16[1024,512]{1,0:T(8,128)(2,1)S(1)} %bitcast.156, bf16[512,2048]{1,0:T(8,128)(2,1)S(1)} %copy-done), kind=kOutput, calls=%fused_computation.14 | convolution fusion | flops 2149580800 | bytes 7340032 | tf_op jit(solution)/shard_map/dot_general | solution.py:142
  100.1 5.1 %all-to-all-start.2 = ((bf16[16,64,2048]{2,1,0:T(8,128)(2,1)}), bf16[16,64,2048]{2,1,0:T(8,128)(2,1)}, u32[]{:S(2)}, u32[]{:S(2)}) async-start(bf16[16,64,2048]{2,1,0:T(8,128)(2,1)} %bitcast.155), calls=%async_computation.2 | async-start | bytes 8388608 | tf_op jit(solution)/shard_map/all_to_all | solution.py:150
  105.2 52.5 %all-to-all-done.2 = bf16[16,64,2048]{2,1,0:T(8,128)(2,1)} async-done(((bf16[16,64,2048]{2,1,0:T(8,128)(2,1)}), bf16[16,64,2048]{2,1,0:T(8,128)(2,1)}, u32[]{:S(2)}, u32[]{:S(2)}) %all-to-all-start.2) | async-done | bytes 4194336 | tf_op jit(solution)/shard_map/all_to_all | solution.py:150
  157.8 3.0 convert_reduce_fusion.1
  160.8 1.1 multiply_reduce_fusion
  161.9 1.4 collective-permute-start.7
  163.4 3.6 %collective-permute-start.6 = (f32[64]{0:T(128)S(1)}, f32[64]{0:T(128)S(1)}, u32[]{:S(2)}, u32[]{:S(2)}) collective-permute-start(f32[64]{0:T(128)S(1)} %multiply_reduce_fusion), channel_id=1, source_target_pairs={{0,96},{16,112},{32,64},{48,80},{64,32},{80,48},{96,0},{112,16},{1... | collective-permute-start | bytes 776 | tf_op jit(solution)/shard_map/ppermute | solution.py:163
  167.9 2.7 collective-permute-start.4
  171.4 1.5 collective-permute-start.2
  172.9 0.9 collective-permute-start.1
  174.2 1.1 collective-permute-done.2
  176.0 1.8 multiply_convert_fusion
  177.8 14.2 %copy.49 = bf16[256,8,2,1664]{3,1,2,0:T(8,128)(2,1)} copy(bf16[256,8,2,1664]{3,2,1,0:T(2,128)(2,1)} %bitcast.148) | data formatting | bytes 27262976
  192.1 29.9 %all-gather.2.cloned.1.call-done = bf16[1024,2048]{1,0:T(8,128)(2,1)} async-done(((bf16[64,2048]{1,0:T(8,128)(2,1)}), bf16[1024,2048]{1,0:T(8,128)(2,1)}) %all-gather.2.cloned.1.call-update) | async-done | bytes 4194320 | tf_op jit(solution)/shard_map/all_gather | solution.py:173
  222.0 19.7 %convolution_convert_fusion = bf16[1024,3328]{1,0:T(8,128)(2,1)S(1)} fusion(bf16[1024,2048]{1,0:T(8,128)(2,1)} %all-gather.2.cloned.1.call-done, bf16[2048,3328]{1,0:T(8,128)(2,1)} %bitcast.149), kind=kOutput, calls=%fused_computation.8 | convolution fusion | flops 13962051584 | bytes 24641536 | tf_op jit(solution)/shard_map/dot_general | solution.py:175
  241.7 85.3 %all_to_all.21 = bf16[8,128,3328]{2,1,0:T(8,128)(2,1)S(1)} all-to-all(bf16[8,128,3328]{2,1,0:T(8,128)(2,1)S(1)} %bitcast.151), channel_id=1, replica_groups=mesh['replica'=8,'tensor'=16] {'replica'}, dimensions={0} | all-to-all | bytes 13631488 | tf_op jit(solution)/shard_map/all_to_all | solution.py:176
  327.0 1.0 convert_reduce_fusion
  328.0 1.0 fusion.24
  (70 shorter events, 12.5 us)
Async XLA Ops:
  6.5 89.2 %copy-start = (bf16[512,2048]{1,0:T(8,128)(2,1)S(1)}, bf16[512,2048]{1,0:T(8,128)(2,1)}, u32[]{:S(2)}) copy-start(bf16[512,2048]{1,0:T(8,128)(2,1)} %param.18) | copy-start | bytes 6291460
  14.4 44.2 %copy-start.4 = (s32[64]{0:T(128)S(1)}, s32[64]{0:T(128)}, u32[]{:S(2)}) copy-start(s32[64]{0:T(128)} %param.16) | copy-start | bytes 772
  14.4 44.3 %copy-start.2 = (bf16[128,512]{1,0:T(8,128)(2,1)S(1)}, bf16[128,512]{1,0:T(8,128)(2,1)}, u32[]{:S(2)}) copy-start(bf16[128,512]{1,0:T(8,128)(2,1)} %param.11) | copy-start | bytes 393220
  16.0 41.3 %all-to-all-start = ((bf16[128,1,32,256]{3,2,1,0:T(8,128)(2,1)}), bf16[128,1,32,256]{3,2,1,0:T(8,128)(2,1)}, u32[]{:S(2)}, u32[]{:S(2)}) async-start(bf16[128,1,32,256]{3,2,1,0:T(8,128)(2,1)} %bitcast.150), calls=%async_computation | async-start | bytes 4194304 | tf_op jit(solution)/shard_map/all_to_all | solution.py:56
  57.2 10.4 %collective-permute-start = (bf16[128,1,32,256]{3,2,1,0:T(8,128)(2,1)}, bf16[128,1,32,256]{3,2,1,0:T(8,128)(2,1)}, u32[]{:S(2)}, u32[]{:S(2)}) collective-permute-start(bf16[128,1,32,256]{3,2,1,0:T(8,128)(2,1)} %all-to-all-done), channel_id=1, source_target_pairs={{0,1},{1,0},{2,3},{3,2},{4,5},{5,4},{6,7},{7,6},{8,9},{9,8},{10,11... | collective-permute-start | bytes 6291464 | tf_op jit(solution)/shard_map/ppermute | solution.py:59
  100.1 57.7 %all-to-all-start.2 = ((bf16[16,64,2048]{2,1,0:T(8,128)(2,1)}), bf16[16,64,2048]{2,1,0:T(8,128)(2,1)}, u32[]{:S(2)}, u32[]{:S(2)}) async-start(bf16[16,64,2048]{2,1,0:T(8,128)(2,1)} %bitcast.155), calls=%async_computation.2 | async-start | bytes 8388608 | tf_op jit(solution)/shard_map/all_to_all | solution.py:150
  105.2 68.7 %copy-start.3 = (bf16[2048]{0:T(1024)(128)(2,1)S(1)}, bf16[2048]{0:T(1024)(128)(2,1)}, u32[]{:S(2)}) copy-start(bf16[2048]{0:T(1024)(128)(2,1)} %param.20) | copy-start | bytes 12292
  105.2 116.8 %all-gather.2.cloned.1.call-start = ((), (), s32[]{:S(2)}) async-start(), calls=%async_computation.4 | async-start | bytes 4456448 | tf_op jit(solution)/shard_map/all_gather | solution.py:173
  161.9 9.4 %collective-permute-start.7 = (f32[64]{0:T(128)S(1)}, f32[64]{0:T(128)S(1)}, u32[]{:S(2)}, u32[]{:S(2)}) collective-permute-start(f32[64]{0:T(128)S(1)} %multiply_reduce_fusion), channel_id=1, source_target_pairs={{0,112},{16,96},{32,80},{48,64},{64,48},{80,32},{96,16},{112,0},{1... | collective-permute-start | bytes 776 | tf_op jit(solution)/shard_map/ppermute | solution.py:163
  163.4 9.5 %collective-permute-start.6 = (f32[64]{0:T(128)S(1)}, f32[64]{0:T(128)S(1)}, u32[]{:S(2)}, u32[]{:S(2)}) collective-permute-start(f32[64]{0:T(128)S(1)} %multiply_reduce_fusion), channel_id=1, source_target_pairs={{0,96},{16,112},{32,64},{48,80},{64,32},{80,48},{96,0},{112,16},{1... | collective-permute-start | bytes 776 | tf_op jit(solution)/shard_map/ppermute | solution.py:163
  167.0 6.8 %collective-permute-start.5 = (f32[64]{0:T(128)S(1)}, f32[64]{0:T(128)S(1)}, u32[]{:S(2)}, u32[]{:S(2)}) collective-permute-start(f32[64]{0:T(128)S(1)} %multiply_reduce_fusion), channel_id=1, source_target_pairs={{0,80},{16,64},{32,112},{48,96},{64,16},{80,0},{96,48},{112,32},{1... | collective-permute-start | bytes 776 | tf_op jit(solution)/shard_map/ppermute | solution.py:163
  167.9 6.0 %collective-permute-start.4 = (f32[64]{0:T(128)S(1)}, f32[64]{0:T(128)S(1)}, u32[]{:S(2)}, u32[]{:S(2)}) collective-permute-start(f32[64]{0:T(128)S(1)} %multiply_reduce_fusion), channel_id=1, source_target_pairs={{0,64},{16,80},{32,96},{48,112},{64,0},{80,16},{96,32},{112,48},{1... | collective-permute-start | bytes 776 | tf_op jit(solution)/shard_map/ppermute | solution.py:163
  170.5 3.6 %collective-permute-start.3 = (f32[64]{0:T(128)S(1)}, f32[64]{0:T(128)S(1)}, u32[]{:S(2)}, u32[]{:S(2)}) collective-permute-start(f32[64]{0:T(128)S(1)} %multiply_reduce_fusion), channel_id=1, source_target_pairs={{0,48},{16,32},{32,16},{48,0},{64,112},{80,96},{96,80},{112,64},{1... | collective-permute-start | bytes 776 | tf_op jit(solution)/shard_map/ppermute | solution.py:163
  171.4 3.9 %collective-permute-start.2 = (f32[64]{0:T(128)S(1)}, f32[64]{0:T(128)S(1)}, u32[]{:S(2)}, u32[]{:S(2)}) collective-permute-start(f32[64]{0:T(128)S(1)} %multiply_reduce_fusion), channel_id=1, source_target_pairs={{0,32},{16,48},{32,0},{48,16},{64,96},{80,112},{96,64},{112,80},{1... | collective-permute-start | bytes 776 | tf_op jit(solution)/shard_map/ppermute | solution.py:163
  172.9 2.4 collective-permute-start.1
  241.7 87.3 %copy-start.1 = (bf16[512,2048]{1,0:T(8,128)(2,1)S(1)}, bf16[512,2048]{1,0:T(8,128)(2,1)}, u32[]{:S(2)}) copy-start(bf16[512,2048]{1,0:T(8,128)(2,1)} %param.18) | copy-start | bytes 6291460
Sparse Core Ops, SparseCore 0:
  177.9 44.0 all-gather.1

commit v8 on v6

--- a/solution.py
+++ b/solution.py
@@ -57,10 +57,7 @@
         outgoing, ("replica", "tensor"), split_axis=0, concat_axis=0, tiled=True
     )
     partner = lax.ppermute(arrived, "tensor", [(i, i ^ 1) for i in range(tensors)])
-    mine_first = (tensor_idx % 2) == 0
-    low_half = jnp.where(mine_first, arrived, partner)
-    high_half = jnp.where(mine_first, partner, arrived)
-    arrived = jnp.concatenate([low_half, high_half], axis=2)
+    arrived = jnp.concatenate([arrived, partner], axis=2)
     arrived = arrived.reshape(replicas, tensors, SHARE, PAGE, pair_width)
     prefix_blocks = jnp.transpose(arrived, (0, 2, 1, 3, 4)).reshape(
         sessions, cached_len, pair_width
@@ -84,7 +81,8 @@
     )
     slot_fresh = jnp.take(fresh_pair, padded_index, axis=0).reshape(sessions, slot_rows, pair_width)
     lengths = lax.dynamic_slice_in_dim(prefix_len, replica_idx * sessions, sessions, 0)
-    key_pos = jnp.arange(cached_len, dtype=jnp.int32)
+    key_ids = jnp.arange(cached_len, dtype=jnp.int32)
+    key_pos = (key_ids // PAGE) * PAGE + (key_ids % PAGE + (tensor_idx % 2) * half) % PAGE
     prefix_mask = (key_pos[None, :] < lengths[:, None])[:, None, :]
     fresh_mask = (offsets[None, None, :] <= offsets[None, :, None]) & (
         offsets[None, None, :] < counts[:, None, None]

time: 333 us -> 332 us (level)
  no operation moved by 1% of the time
where the time goes in v8:
time: 332 us; the launch traced here: 331 us
  waiting for transfers between devices  117 us (35%)
  blocking collectives  105 us (32%)
  local copies, waits for them, and re-layouts  28.8 us (9%)
  matrix products  27.2 us (8%)
  starting transfers between devices  19.9 us (6%)
  other arithmetic  19 us (6%)
  between operations  13.7 us (4%)
    all_to_all x1, blocking collectives, per_device(): lax.all_to_all(slab.astype(jnp.bfloat16).reshape(replicas, rows_here, sla...  85.3 us
    all_to_all x1, waiting for transfers between devices, per_device(): lax.all_to_all(partial_out.astype(jnp.bfloat16).reshape(tensors, part_row...  52.6 us
    all_gather x1, waiting for transfers between devices, per_device(): normed = lax.all_gather(normed_part, 'tensor', axis=0, tiled=True)  29.8 us
    all_to_all x1, waiting for transfers between devices, per_device(): lax.all_to_all(outgoing, ('replica', 'tensor'), split_axis=0, concat_axis...  26 us
    all_to_all x1, blocking collectives, per_device(): lax.all_to_all(jnp.broadcast_to(attended[None], (replicas,) + attended.sh...  20.1 us
    dot_general x1, matrix products, per_device(): slab = jnp.dot(normed, weights_local, preferred_element_type=jnp.float32)  19.7 us
    unnamed x13, local copies, waits for them, and re-layouts  14.4 us
    all_to_all x1, starting transfers between devices, per_device(): lax.all_to_all(outgoing, ('replica', 'tensor'), split_axis=0, concat_axis...  11.9 us
  transfers between devices with their start and end apart: 7, of which 6 were waited for; matrix products, arithmetic and copies ran while one was open for 8% of the time, Pallas kernels for 0%

profile of v8, /device:TPU:1, one launch (start us, length us, event | category | flops | bytes accessed | tf_op | source)
XLA Modules:
  0.0 331.2 jit_solution(5428948567921480693)
XLA Ops:
  6.5 0.9 constant_dynamic-slice_fusion.1
  9.0 2.8 gather_fusion.1
  11.8 1.9 gather.38
  14.4 1.6 broadcast_in_dim.105
  16.0 11.9 %all-to-all-start = ((bf16[128,1,32,256]{3,2,1,0:T(8,128)(2,1)}), bf16[128,1,32,256]{3,2,1,0:T(8,128)(2,1)}, u32[]{:S(2)}, u32[]{:S(2)}) async-start(bf16[128,1,32,256]{3,2,1,0:T(8,128)(2,1)} %bitcast.140), calls=%async_computation | async-start | bytes 4194304 | tf_op jit(solution)/shard_map/all_to_all | solution.py:56
  30.4 0.8 constant_dynamic-slice_fusion
  31.2 26.0 %all-to-all-done = bf16[128,1,32,256]{3,2,1,0:T(8,128)(2,1)} async-done(((bf16[128,1,32,256]{3,2,1,0:T(8,128)(2,1)}), bf16[128,1,32,256]{3,2,1,0:T(8,128)(2,1)}, u32[]{:S(2)}, u32[]{:S(2)}) %all-to-all-start) | async-done | bytes 2097184 | tf_op jit(solution)/shard_map/all_to_all | solution.py:56
  57.2 1.3 collective-permute-start
  58.7 1.2 gather_fusion.3
  59.9 1.0 gather_fusion.2
  61.0 5.0 %compare_and_fusion.1 = (pred[128]{0:T(512)(128)(4,1)S(1)}, s32[128]{0:T(128)S(1)}) fusion(s32[128]{0:T(128)S(1)} %convert_reduce_fusion.2, s32[]{:T(128)} %bitcast.12, s32[]{:T(128)} %bitcast.11, s32[]{:T(128)} %bitcast.10, s32[]{:T(128)} %bitcast.9, s32[]{:T(128)} %bitcast.8, s32[]{:T(128)} %bitcast.7, s32[]{:T(128)} %bitcast.6, s32[]{:T(128)} %bitcast.5), kind=kLoop, calls=%fused_computation.99 | loop fusion | flops 4224 | bytes 1184 | tf_op jit(solution)/shard_map/jit(_take)/and | solution.py:132
  67.1 2.7 pad_maximum_fusion
  69.8 0.9 bitcast_reduce_fusion
  71.1 1.1 fusion.1
  72.2 1.4 fusion.21
  73.8 0.8 gather_fusion.4
  74.9 20.1 %all_to_all.20 = bf16[8,128,512]{2,1,0:T(8,128)(2,1)S(1)} all-to-all(bf16[8,128,512]{2,1,0:T(8,128)(2,1)S(1)} %broadcast_in_dim.116), channel_id=1, replica_groups=mesh['replica'=8,'tensor'=16] {'replica'}, dimensions={0} | all-to-all | bytes 2097152 | tf_op jit(solution)/shard_map/all_to_all | solution.py:133
  95.0 4.3 %convolution_convert_fusion.1 = bf16[1024,2048]{1,0:T(8,128)(2,1)} fusion(bf16[1024,512]{1,0:T(8,128)(2,1)S(1)} %bitcast.146, bf16[512,2048]{1,0:T(8,128)(2,1)S(1)} %copy-done), kind=kOutput, calls=%fused_computation.13 | convolution fusion | flops 2149580800 | bytes 7340032 | tf_op jit(solution)/shard_map/dot_general | solution.py:140
  99.3 5.1 %all-to-all-start.2 = ((bf16[16,64,2048]{2,1,0:T(8,128)(2,1)}), bf16[16,64,2048]{2,1,0:T(8,128)(2,1)}, u32[]{:S(2)}, u32[]{:S(2)}) async-start(bf16[16,64,2048]{2,1,0:T(8,128)(2,1)} %bitcast.145), calls=%async_computation.2 | async-start | bytes 8388608 | tf_op jit(solution)/shard_map/all_to_all | solution.py:148
  104.4 52.6 %all-to-all-done.2 = bf16[16,64,2048]{2,1,0:T(8,128)(2,1)} async-done(((bf16[16,64,2048]{2,1,0:T(8,128)(2,1)}), bf16[16,64,2048]{2,1,0:T(8,128)(2,1)}, u32[]{:S(2)}, u32[]{:S(2)}) %all-to-all-start.2) | async-done | bytes 4194336 | tf_op jit(solution)/shard_map/all_to_all | solution.py:148
  157.0 3.0 convert_reduce_fusion.1
  160.0 1.1 multiply_reduce_fusion
  161.8 1.8 collective-permute-done.1
  164.2 3.3 %collective-permute-done.2 = f32[64]{0:T(128)S(1)} collective-permute-done((f32[64]{0:T(128)S(1)}, f32[64]{0:T(128)S(1)}, u32[]{:S(2)}, u32[]{:S(2)}) %collective-permute-start.2) | collective-permute-done | bytes 288 | tf_op jit(solution)/shard_map/ppermute | solution.py:162
  167.8 3.6 %collective-permute-done.3 = f32[64]{0:T(128)S(1)} collective-permute-done((f32[64]{0:T(128)S(1)}, f32[64]{0:T(128)S(1)}, u32[]{:S(2)}, u32[]{:S(2)}) %collective-permute-start.3) | collective-permute-done | bytes 288 | tf_op jit(solution)/shard_map/ppermute | solution.py:162
  171.5 1.8 multiply_convert_fusion
  173.3 14.2 %copy.49 = bf16[256,8,2,1664]{3,1,2,0:T(8,128)(2,1)} copy(bf16[256,8,2,1664]{3,2,1,0:T(2,128)(2,1)} %bitcast.138) | data formatting | bytes 27262976
  187.5 29.8 %all-gather.2.cloned.1.call-done = bf16[1024,2048]{1,0:T(8,128)(2,1)} async-done(((bf16[64,2048]{1,0:T(8,128)(2,1)}), bf16[1024,2048]{1,0:T(8,128)(2,1)}) %all-gather.2.cloned.1.call-update) | async-done | bytes 4194320 | tf_op jit(solution)/shard_map/all_gather | solution.py:169
  217.3 19.7 %convolution_convert_fusion = bf16[1024,3328]{1,0:T(8,128)(2,1)S(1)} fusion(bf16[1024,2048]{1,0:T(8,128)(2,1)} %all-gather.2.cloned.1.call-done, bf16[2048,3328]{1,0:T(8,128)(2,1)} %bitcast.139), kind=kOutput, calls=%fused_computation.7 | convolution fusion | flops 13962051584 | bytes 24641536 | tf_op jit(solution)/shard_map/dot_general | solution.py:171
  237.0 85.3 %all_to_all.21 = bf16[8,128,3328]{2,1,0:T(8,128)(2,1)S(1)} all-to-all(bf16[8,128,3328]{2,1,0:T(8,128)(2,1)S(1)} %bitcast.141), channel_id=1, replica_groups=mesh['replica'=8,'tensor'=16] {'replica'}, dimensions={0} | all-to-all | bytes 13631488 | tf_op jit(solution)/shard_map/all_to_all | solution.py:172
  322.4 1.0 convert_reduce_fusion
  323.3 1.0 fusion.24
  (59 shorter events, 8.4 us)
Async XLA Ops:
  6.5 88.4 %copy-start = (bf16[512,2048]{1,0:T(8,128)(2,1)S(1)}, bf16[512,2048]{1,0:T(8,128)(2,1)}, u32[]{:S(2)}) copy-start(bf16[512,2048]{1,0:T(8,128)(2,1)} %param.18) | copy-start | bytes 6291460
  14.4 44.2 %copy-start.4 = (s32[64]{0:T(128)S(1)}, s32[64]{0:T(128)}, u32[]{:S(2)}) copy-start(s32[64]{0:T(128)} %param.16) | copy-start | bytes 772
  14.4 44.3 %copy-start.2 = (bf16[128,512]{1,0:T(8,128)(2,1)S(1)}, bf16[128,512]{1,0:T(8,128)(2,1)}, u32[]{:S(2)}) copy-start(bf16[128,512]{1,0:T(8,128)(2,1)} %param.11) | copy-start | bytes 393220
  16.0 41.3 %all-to-all-start = ((bf16[128,1,32,256]{3,2,1,0:T(8,128)(2,1)}), bf16[128,1,32,256]{3,2,1,0:T(8,128)(2,1)}, u32[]{:S(2)}, u32[]{:S(2)}) async-start(bf16[128,1,32,256]{3,2,1,0:T(8,128)(2,1)} %bitcast.140), calls=%async_computation | async-start | bytes 4194304 | tf_op jit(solution)/shard_map/all_to_all | solution.py:56
  57.2 9.8 %collective-permute-start = (bf16[128,1,32,256]{3,2,1,0:T(8,128)(2,1)}, bf16[128,1,32,256]{3,2,1,0:T(8,128)(2,1)}, u32[]{:S(2)}, u32[]{:S(2)}) collective-permute-start(bf16[128,1,32,256]{3,2,1,0:T(8,128)(2,1)} %all-to-all-done), channel_id=1, source_target_pairs={{0,1},{1,0},{2,3},{3,2},{4,5},{5,4},{6,7},{7,6},{8,9},{9,8},{10,11... | collective-permute-start | bytes 6291464 | tf_op jit(solution)/shard_map/ppermute | solution.py:59
  99.3 57.7 %all-to-all-start.2 = ((bf16[16,64,2048]{2,1,0:T(8,128)(2,1)}), bf16[16,64,2048]{2,1,0:T(8,128)(2,1)}, u32[]{:S(2)}, u32[]{:S(2)}) async-start(bf16[16,64,2048]{2,1,0:T(8,128)(2,1)} %bitcast.145), calls=%async_computation.2 | async-start | bytes 8388608 | tf_op jit(solution)/shard_map/all_to_all | solution.py:148
  104.3 63.5 %copy-start.3 = (bf16[2048]{0:T(1024)(128)(2,1)S(1)}, bf16[2048]{0:T(1024)(128)(2,1)}, u32[]{:S(2)}) copy-start(bf16[2048]{0:T(1024)(128)(2,1)} %param.20) | copy-start | bytes 12292
  104.3 113.0 %all-gather.2.cloned.1.call-start = ((), (), s32[]{:S(2)}) async-start(), calls=%async_computation.4 | async-start | bytes 4456448 | tf_op jit(solution)/shard_map/all_gather | solution.py:169
  161.1 2.5 collective-permute-start.1
  163.6 3.9 %collective-permute-start.2 = (f32[64]{0:T(128)S(1)}, f32[64]{0:T(128)S(1)}, u32[]{:S(2)}, u32[]{:S(2)}) collective-permute-start(f32[64]{0:T(128)S(1)} %add.259), channel_id=1, source_target_pairs={{0,32},{16,48},{32,0},{48,16},{64,96},{80,112},{96,64},{112,80},{1... | collective-permute-start | bytes 776 | tf_op jit(solution)/shard_map/ppermute | solution.py:162
  167.5 3.9 %collective-permute-start.3 = (f32[64]{0:T(128)S(1)}, f32[64]{0:T(128)S(1)}, u32[]{:S(2)}, u32[]{:S(2)}) collective-permute-start(f32[64]{0:T(128)S(1)} %add.260), channel_id=1, source_target_pairs={{0,64},{16,80},{32,96},{48,112},{64,0},{80,16},{96,32},{112,48},{1... | collective-permute-start | bytes 776 | tf_op jit(solution)/shard_map/ppermute | solution.py:162
  237.0 87.3 %copy-start.1 = (bf16[512,2048]{1,0:T(8,128)(2,1)S(1)}, bf16[512,2048]{1,0:T(8,128)(2,1)}, u32[]{:S(2)}) copy-start(bf16[512,2048]{1,0:T(8,128)(2,1)} %param.18) | copy-start | bytes 6291460
Sparse Core Ops, SparseCore 0:
  173.4 43.8 all-gather.1

commit v9 on v6

--- a/solution.py
+++ b/solution.py
@@ -56,6 +56,8 @@
     arrived = lax.all_to_all(
         outgoing, ("replica", "tensor"), split_axis=0, concat_axis=0, tiled=True
     )
+    weights_local = gate_up.reshape(gate_up.shape[0], 2 * gate_up.shape[2])
+    arrived, weights_local = lax.optimization_barrier((arrived, weights_local))
     partner = lax.ppermute(arrived, "tensor", [(i, i ^ 1) for i in range(tensors)])
     mine_first = (tensor_idx % 2) == 0
     low_half = jnp.where(mine_first, arrived, partner)
@@ -169,7 +171,6 @@
         carried * lax.rsqrt(squares / D + EPSILON)[:, None] * gain_row[None, :]
     ).astype(jnp.bfloat16)
     normed = lax.all_gather(normed_part, "tensor", axis=0, tiled=True)
-    weights_local = gate_up.reshape(gate_up.shape[0], 2 * gate_up.shape[2])
     slab = jnp.dot(normed, weights_local, preferred_element_type=jnp.float32)
     slab_parts = lax.all_to_all(
         slab.astype(jnp.bfloat16).reshape(replicas, rows_here, slab.shape[1]),

time: 333 us -> 333 us (level)
    all_to_all x1, waiting for transfers between devices: 26.7 us -> 12.4 us  [per_device(): lax.all_to_all(outgoing, ('replica', 'tensor'), split_axis=0, concat_axis...]
    all_gather x1, waiting for transfers between devices: 29.8 us -> 44.1 us  [per_device(): normed = lax.all_gather(normed_part, 'tensor', axis=0, tiled=True)]
where the time goes in v9:
time: 333 us; the launch traced here: 332 us
  waiting for transfers between devices  118 us (35%)
  blocking collectives  105 us (32%)
  local copies, waits for them, and re-layouts  28.9 us (9%)
  matrix products  27.2 us (8%)
  starting transfers between devices  20.1 us (6%)
  other arithmetic  19.1 us (6%)
  between operations  13.7 us (4%)
    all_to_all x1, blocking collectives, per_device(): lax.all_to_all(slab.astype(jnp.bfloat16).reshape(replicas, rows_here, sla...  85.3 us
    all_to_all x1, waiting for transfers between devices, per_device(): lax.all_to_all(partial_out.astype(jnp.bfloat16).reshape(tensors, part_row...  52.4 us
    all_gather x1, waiting for transfers between devices, per_device(): normed = lax.all_gather(normed_part, 'tensor', axis=0, tiled=True)  44.1 us
    all_to_all x1, blocking collectives, per_device(): lax.all_to_all(jnp.broadcast_to(attended[None], (replicas,) + attended.sh...  20.1 us
    dot_general x1, matrix products, per_device(): slab = jnp.dot(normed, weights_local, preferred_element_type=jnp.float32)  19.7 us
    unnamed x13, local copies, waits for them, and re-layouts  14.4 us
    all_to_all x1, waiting for transfers between devices, per_device(): lax.all_to_all(outgoing, ('replica', 'tensor'), split_axis=0, concat_axis...  12.4 us
    all_to_all x1, starting transfers between devices, per_device(): lax.all_to_all(outgoing, ('replica', 'tensor'), split_axis=0, concat_axis...  11.9 us
  transfers between devices with their start and end apart: 7, of which 6 were waited for; matrix products, arithmetic and copies ran while one was open for 8% of the time, Pallas kernels for 0%

profile of v9, /device:TPU:1, one launch (start us, length us, event | category | flops | bytes accessed | tf_op | source)
XLA Modules:
  0.0 332.1 jit_solution(4833544376566334796)
XLA Ops:
  6.5 0.9 constant_dynamic-slice_fusion.1
  9.0 2.8 gather_fusion.1
  11.8 1.9 gather.38
  14.4 1.6 broadcast_in_dim.105
  16.0 11.9 %all-to-all-start = ((bf16[128,1,32,256]{3,2,1,0:T(8,128)(2,1)}), bf16[128,1,32,256]{3,2,1,0:T(8,128)(2,1)}, u32[]{:S(2)}, u32[]{:S(2)}) async-start(bf16[128,1,32,256]{3,2,1,0:T(8,128)(2,1)} %bitcast.140), calls=%async_computation | async-start | bytes 4194304 | tf_op jit(solution)/shard_map/all_to_all | solution.py:56
  29.7 14.3 %copy.48 = bf16[256,8,2,1664]{3,1,2,0:T(8,128)(2,1)} copy(bf16[256,8,2,1664]{3,2,1,0:T(2,128)(2,1)} %bitcast.138) | data formatting | bytes 27262976
  44.0 0.8 constant_dynamic-slice_fusion
  44.8 12.4 %all-to-all-done = bf16[128,1,32,256]{3,2,1,0:T(8,128)(2,1)} async-done(((bf16[128,1,32,256]{3,2,1,0:T(8,128)(2,1)}), bf16[128,1,32,256]{3,2,1,0:T(8,128)(2,1)}, u32[]{:S(2)}, u32[]{:S(2)}) %all-to-all-start) | async-done | bytes 2097184 | tf_op jit(solution)/shard_map/all_to_all | solution.py:56
  57.2 1.3 collective-permute-start
  58.7 1.2 gather_fusion.3
  59.9 1.0 gather_fusion.2
  61.7 5.0 %compare_and_fusion.1 = (pred[128]{0:T(512)(128)(4,1)S(1)}, s32[128]{0:T(128)S(1)}) fusion(s32[128]{0:T(128)S(1)} %convert_reduce_fusion.2, s32[]{:T(128)} %bitcast.12, s32[]{:T(128)} %bitcast.11, s32[]{:T(128)} %bitcast.10, s32[]{:T(128)} %bitcast.9, s32[]{:T(128)} %bitcast.8, s32[]{:T(128)} %bitcast.7, s32[]{:T(128)} %bitcast.6, s32[]{:T(128)} %bitcast.5), kind=kLoop, calls=%fused_computation.83 | loop fusion | flops 4224 | bytes 1184 | tf_op jit(solution)/shard_map/jit(_take)/and | solution.py:136
  67.7 2.5 broadcast_select_fusion.1
  70.7 0.9 bitcast_reduce_fusion
  72.0 1.1 fusion.1
  73.1 1.4 fusion.21
  74.7 0.8 gather_fusion.4
  75.7 20.1 %all_to_all.20 = bf16[8,128,512]{2,1,0:T(8,128)(2,1)S(1)} all-to-all(bf16[8,128,512]{2,1,0:T(8,128)(2,1)S(1)} %broadcast_in_dim.116), channel_id=1, replica_groups=mesh['replica'=8,'tensor'=16] {'replica'}, dimensions={0} | all-to-all | bytes 2097152 | tf_op jit(solution)/shard_map/all_to_all | solution.py:137
  95.8 4.3 %convolution_convert_fusion.1 = bf16[1024,2048]{1,0:T(8,128)(2,1)} fusion(bf16[1024,512]{1,0:T(8,128)(2,1)S(1)} %bitcast.146, bf16[512,2048]{1,0:T(8,128)(2,1)S(1)} %copy-done), kind=kOutput, calls=%fused_computation.13 | convolution fusion | flops 2149580800 | bytes 7340032 | tf_op jit(solution)/shard_map/dot_general | solution.py:144
  100.2 5.1 %all-to-all-start.2 = ((bf16[16,64,2048]{2,1,0:T(8,128)(2,1)}), bf16[16,64,2048]{2,1,0:T(8,128)(2,1)}, u32[]{:S(2)}, u32[]{:S(2)}) async-start(bf16[16,64,2048]{2,1,0:T(8,128)(2,1)} %bitcast.145), calls=%async_computation.2 | async-start | bytes 8388608 | tf_op jit(solution)/shard_map/all_to_all | solution.py:152
  105.5 52.4 %all-to-all-done.2 = bf16[16,64,2048]{2,1,0:T(8,128)(2,1)} async-done(((bf16[16,64,2048]{2,1,0:T(8,128)(2,1)}), bf16[16,64,2048]{2,1,0:T(8,128)(2,1)}, u32[]{:S(2)}, u32[]{:S(2)}) %all-to-all-start.2) | async-done | bytes 4194336 | tf_op jit(solution)/shard_map/all_to_all | solution.py:152
  157.9 3.0 convert_reduce_fusion.1
  160.9 1.1 multiply_reduce_fusion
  162.7 1.8 collective-permute-done.1
  165.1 3.3 %collective-permute-done.2 = f32[64]{0:T(128)S(1)} collective-permute-done((f32[64]{0:T(128)S(1)}, f32[64]{0:T(128)S(1)}, u32[]{:S(2)}, u32[]{:S(2)}) %collective-permute-start.2) | collective-permute-done | bytes 288 | tf_op jit(solution)/shard_map/ppermute | solution.py:166
  168.7 3.6 %collective-permute-done.3 = f32[64]{0:T(128)S(1)} collective-permute-done((f32[64]{0:T(128)S(1)}, f32[64]{0:T(128)S(1)}, u32[]{:S(2)}, u32[]{:S(2)}) %collective-permute-start.3) | collective-permute-done | bytes 288 | tf_op jit(solution)/shard_map/ppermute | solution.py:166
  172.4 1.8 multiply_convert_fusion
  174.2 44.1 %all-gather.2.cloned.1.call-done = bf16[1024,2048]{1,0:T(8,128)(2,1)} async-done(((bf16[64,2048]{1,0:T(8,128)(2,1)}), bf16[1024,2048]{1,0:T(8,128)(2,1)}) %all-gather.2.cloned.1.call-update) | async-done | bytes 4194320 | tf_op jit(solution)/shard_map/all_gather | solution.py:173
  218.2 19.7 %convolution_convert_fusion = bf16[1024,3328]{1,0:T(8,128)(2,1)S(1)} fusion(bf16[1024,2048]{1,0:T(8,128)(2,1)} %all-gather.2.cloned.1.call-done, bf16[2048,3328]{1,0:T(8,128)(2,1)} %bitcast.139), kind=kOutput, calls=%fused_computation.7 | convolution fusion | flops 13962051584 | bytes 24641536 | tf_op jit(solution)/shard_map/dot_general | solution.py:174
  238.0 85.3 %all_to_all.21 = bf16[8,128,3328]{2,1,0:T(8,128)(2,1)S(1)} all-to-all(bf16[8,128,3328]{2,1,0:T(8,128)(2,1)S(1)} %bitcast.141), channel_id=1, replica_groups=mesh['replica'=8,'tensor'=16] {'replica'}, dimensions={0} | all-to-all | bytes 13631488 | tf_op jit(solution)/shard_map/all_to_all | solution.py:175
  323.3 1.0 convert_reduce_fusion
  324.2 1.0 fusion.24
  (58 shorter events, 8.9 us)
Async XLA Ops:
  6.5 89.3 %copy-start = (bf16[512,2048]{1,0:T(8,128)(2,1)S(1)}, bf16[512,2048]{1,0:T(8,128)(2,1)}, u32[]{:S(2)}) copy-start(bf16[512,2048]{1,0:T(8,128)(2,1)} %param.18) | copy-start | bytes 6291460
  16.0 41.3 %all-to-all-start = ((bf16[128,1,32,256]{3,2,1,0:T(8,128)(2,1)}), bf16[128,1,32,256]{3,2,1,0:T(8,128)(2,1)}, u32[]{:S(2)}, u32[]{:S(2)}) async-start(bf16[128,1,32,256]{3,2,1,0:T(8,128)(2,1)} %bitcast.140), calls=%async_computation | async-start | bytes 4194304 | tf_op jit(solution)/shard_map/all_to_all | solution.py:56
  29.7 28.9 %copy-start.4 = (s32[64]{0:T(128)S(1)}, s32[64]{0:T(128)}, u32[]{:S(2)}) copy-start(s32[64]{0:T(128)} %param.16) | copy-start | bytes 772
  29.7 29.0 %copy-start.2 = (bf16[128,512]{1,0:T(8,128)(2,1)S(1)}, bf16[128,512]{1,0:T(8,128)(2,1)}, u32[]{:S(2)}) copy-start(bf16[128,512]{1,0:T(8,128)(2,1)} %param.11) | copy-start | bytes 393220
  57.2 10.5 %collective-permute-start = (bf16[128,1,32,256]{3,2,1,0:T(8,128)(2,1)}, bf16[128,1,32,256]{3,2,1,0:T(8,128)(2,1)}, u32[]{:S(2)}, u32[]{:S(2)}) collective-permute-start(bf16[128,1,32,256]{3,2,1,0:T(8,128)(2,1)} %all-to-all-done), channel_id=1, source_target_pairs={{0,1},{1,0},{2,3},{3,2},{4,5},{5,4},{6,7},{7,6},{8,9},{9,8},{10,11... | collective-permute-start | bytes 6291464 | tf_op jit(solution)/shard_map/ppermute | solution.py:61
  100.2 57.7 %all-to-all-start.2 = ((bf16[16,64,2048]{2,1,0:T(8,128)(2,1)}), bf16[16,64,2048]{2,1,0:T(8,128)(2,1)}, u32[]{:S(2)}, u32[]{:S(2)}) async-start(bf16[16,64,2048]{2,1,0:T(8,128)(2,1)} %bitcast.145), calls=%async_computation.2 | async-start | bytes 8388608 | tf_op jit(solution)/shard_map/all_to_all | solution.py:152
  105.2 63.5 %copy-start.3 = (bf16[2048]{0:T(1024)(128)(2,1)S(1)}, bf16[2048]{0:T(1024)(128)(2,1)}, u32[]{:S(2)}) copy-start(bf16[2048]{0:T(1024)(128)(2,1)} %param.20) | copy-start | bytes 12292
  105.2 113.0 %all-gather.2.cloned.1.call-start = ((), (), s32[]{:S(2)}) async-start(), calls=%async_computation.4 | async-start | bytes 4456448 | tf_op jit(solution)/shard_map/all_gather | solution.py:173
  162.0 2.5 collective-permute-start.1
  164.5 3.9 %collective-permute-start.2 = (f32[64]{0:T(128)S(1)}, f32[64]{0:T(128)S(1)}, u32[]{:S(2)}, u32[]{:S(2)}) collective-permute-start(f32[64]{0:T(128)S(1)} %add.214), channel_id=1, source_target_pairs={{0,32},{16,48},{32,0},{48,16},{64,96},{80,112},{96,64},{112,80},{1... | collective-permute-start | bytes 776 | tf_op jit(solution)/shard_map/ppermute | solution.py:166
  168.4 3.9 %collective-permute-start.3 = (f32[64]{0:T(128)S(1)}, f32[64]{0:T(128)S(1)}, u32[]{:S(2)}, u32[]{:S(2)}) collective-permute-start(f32[64]{0:T(128)S(1)} %add.215), channel_id=1, source_target_pairs={{0,64},{16,80},{32,96},{48,112},{64,0},{80,16},{96,32},{112,48},{1... | collective-permute-start | bytes 776 | tf_op jit(solution)/shard_map/ppermute | solution.py:166
  237.9 87.3 %copy-start.1 = (bf16[512,2048]{1,0:T(8,128)(2,1)S(1)}, bf16[512,2048]{1,0:T(8,128)(2,1)}, u32[]{:S(2)}) copy-start(bf16[512,2048]{1,0:T(8,128)(2,1)} %param.18) | copy-start | bytes 6291460
Sparse Core Ops, SparseCore 0:
  174.3 43.9 all-gather.1

commit v10 on v7

--- a/solution.py
+++ b/solution.py
@@ -159,14 +159,16 @@
     carried = my_residual.astype(jnp.float32) + head_sum
     gain_row = norm_gain.astype(jnp.float32)
     own_squares = jnp.sum(carried * carried, axis=1)
-    received = [own_squares] + [
-        lax.ppermute(own_squares, "replica", [(i, i ^ k) for i in range(replicas)])
-        for k in range(1, replicas)
-    ]
-    by_source = jnp.take(
-        jnp.stack(received), jnp.arange(replicas, dtype=jnp.int32) ^ replica_idx, axis=0
-    )
-    squares = jnp.sum(by_source, axis=0)
+    squares = jnp.sum(
+        lax.all_to_all(
+            jnp.broadcast_to(own_squares[None], (replicas,) + own_squares.shape),
+            "replica",
+            split_axis=0,
+            concat_axis=0,
+            tiled=True,
+        ),
+        axis=0,
+    )
     normed_part = (
         carried * lax.rsqrt(squares / D + EPSILON)[:, None] * gain_row[None, :]
     ).astype(jnp.bfloat16)

time: 337 us -> 331 us (0.982)
  starting transfers between devices: 30.2 us -> 21.9 us
    ppermute x7 -> x0, starting transfers between devices: 11.9 us -> none  [per_device(): lax.ppermute(own_squares, 'replica', [(i, i ^ k) for i in range(replicas)])]
    all_to_all x0 -> x1, waiting for transfers between devices: none -> 6.14 us  [per_device(): lax.all_to_all(jnp.broadcast_to(own_squares[None], (replicas,) + own_squa...]
  transfers between devices with their start and end apart: 11 -> 5, of which waited for: 5 -> 4; matrix products, arithmetic and copies ran while one was open for 8% -> 8% of each run, Pallas kernels for 0% -> 0%
where the time goes in v10:
time: 331 us; the launch traced here: 330 us
  waiting for transfers between devices  113 us (34%)
  blocking collectives  106 us (32%)
  local copies, waits for them, and re-layouts  29.4 us (9%)
  matrix products  27.2 us (8%)
  starting transfers between devices  21.9 us (7%)
  other arithmetic  19.1 us (6%)
  between operations  13.7 us (4%)
    all_to_all x1, blocking collectives, per_device(): lax.all_to_all(slab.astype(jnp.bfloat16).reshape(replicas, rows_here, sla...  85.5 us
    all_to_all x1, waiting for transfers between devices, per_device(): lax.all_to_all(partial_out.astype(jnp.bfloat16).reshape(tensors, part_row...  52.6 us
    all_gather x1, waiting for transfers between devices, per_device(): normed = lax.all_gather(normed_part, 'tensor', axis=0, tiled=True)  27.6 us
    all_to_all x1, waiting for transfers between devices, per_device(): lax.all_to_all(outgoing, ('replica', 'tensor'), split_axis=0, concat_axis...  26.7 us
    all_to_all x1, blocking collectives, per_device(): lax.all_to_all(jnp.broadcast_to(attended[None], (replicas,) + attended.sh...  20.1 us
    dot_general x1, matrix products, per_device(): slab = jnp.dot(normed, weights_local, preferred_element_type=jnp.float32)  19.7 us
    unnamed x13, local copies, waits for them, and re-layouts  14.4 us
    all_to_all x1, starting transfers between devices, per_device(): lax.all_to_all(outgoing, ('replica', 'tensor'), split_axis=0, concat_axis...  11.9 us
  transfers between devices with their start and end apart: 5, of which 4 were waited for; matrix products, arithmetic and copies ran while one was open for 8% of the time, Pallas kernels for 0%

profile of v10, /device:TPU:1, one launch (start us, length us, event | category | flops | bytes accessed | tf_op | source)
XLA Modules:
  0.0 329.9 jit_solution(10015219738113494823)
XLA Ops:
  6.5 0.9 constant_dynamic-slice_fusion.1
  7.6 0.8 dynamic-slice_bitcast_fusion
  9.0 2.8 gather_fusion.1
  11.8 1.9 gather.38
  14.4 1.6 broadcast_in_dim.111
  16.0 11.9 %all-to-all-start = ((bf16[128,1,32,256]{3,2,1,0:T(8,128)(2,1)}), bf16[128,1,32,256]{3,2,1,0:T(8,128)(2,1)}, u32[]{:S(2)}, u32[]{:S(2)}) async-start(bf16[128,1,32,256]{3,2,1,0:T(8,128)(2,1)} %bitcast.141), calls=%async_computation | async-start | bytes 4194304 | tf_op jit(solution)/shard_map/all_to_all | solution.py:56
  29.7 0.8 constant_dynamic-slice_fusion
  30.5 26.7 %all-to-all-done = bf16[128,1,32,256]{3,2,1,0:T(8,128)(2,1)} async-done(((bf16[128,1,32,256]{3,2,1,0:T(8,128)(2,1)}), bf16[128,1,32,256]{3,2,1,0:T(8,128)(2,1)}, u32[]{:S(2)}, u32[]{:S(2)}) %all-to-all-start) | async-done | bytes 2097184 | tf_op jit(solution)/shard_map/all_to_all | solution.py:56
  57.2 1.3 collective-permute-start
  58.7 1.2 gather_fusion.3
  59.9 1.0 gather_fusion.2
  61.7 5.0 %compare_and_fusion.1 = (pred[128]{0:T(512)(128)(4,1)S(1)}, s32[128]{0:T(128)S(1)}) fusion(s32[128]{0:T(128)S(1)} %convert_reduce_fusion.2, s32[]{:T(128)} %bitcast.12, s32[]{:T(128)} %bitcast.11, s32[]{:T(128)} %bitcast.10, s32[]{:T(128)} %bitcast.9, s32[]{:T(128)} %bitcast.8, s32[]{:T(128)} %bitcast.7, s32[]{:T(128)} %bitcast.6, s32[]{:T(128)} %bitcast.5), kind=kLoop, calls=%fused_computation.83 | loop fusion | flops 4224 | bytes 1184 | tf_op jit(solution)/shard_map/jit(_take)/and | solution.py:134
  67.7 2.5 broadcast_select_fusion.1
  70.6 0.9 bitcast_reduce_fusion
  71.9 1.1 fusion.1
  73.0 1.4 fusion.21
  74.6 0.8 gather_fusion.4
  75.7 20.1 %all_to_all.26 = bf16[8,128,512]{2,1,0:T(8,128)(2,1)S(1)} all-to-all(bf16[8,128,512]{2,1,0:T(8,128)(2,1)S(1)} %broadcast_in_dim.122), channel_id=1, replica_groups=mesh['replica'=8,'tensor'=16] {'replica'}, dimensions={0} | all-to-all | bytes 2097152 | tf_op jit(solution)/shard_map/all_to_all | solution.py:135
  95.8 4.3 %convolution_convert_fusion.1 = bf16[1024,2048]{1,0:T(8,128)(2,1)} fusion(bf16[1024,512]{1,0:T(8,128)(2,1)S(1)} %bitcast.147, bf16[512,2048]{1,0:T(8,128)(2,1)S(1)} %copy-done), kind=kOutput, calls=%fused_computation.13 | convolution fusion | flops 2149580800 | bytes 7340032 | tf_op jit(solution)/shard_map/dot_general | solution.py:142
  100.1 5.1 %all-to-all-start.2 = ((bf16[16,64,2048]{2,1,0:T(8,128)(2,1)}), bf16[16,64,2048]{2,1,0:T(8,128)(2,1)}, u32[]{:S(2)}, u32[]{:S(2)}) async-start(bf16[16,64,2048]{2,1,0:T(8,128)(2,1)} %bitcast.146), calls=%async_computation.2 | async-start | bytes 8388608 | tf_op jit(solution)/shard_map/all_to_all | solution.py:150
  105.2 52.6 %all-to-all-done.2 = bf16[16,64,2048]{2,1,0:T(8,128)(2,1)} async-done(((bf16[16,64,2048]{2,1,0:T(8,128)(2,1)}), bf16[16,64,2048]{2,1,0:T(8,128)(2,1)}, u32[]{:S(2)}, u32[]{:S(2)}) %all-to-all-start.2) | async-done | bytes 4194336 | tf_op jit(solution)/shard_map/all_to_all | solution.py:150
  157.8 3.0 convert_reduce_fusion.1
  160.8 1.1 multiply_reduce_fusion
  162.5 3.3 %all-to-all-start.3 = ((f32[8,1,64]{2,1,0:T(1,128)}), f32[8,1,64]{2,1,0:T(1,128)S(1)}, u32[]{:S(2)}, u32[]{:S(2)}) async-start(f32[8,1,64]{2,1,0:T(1,128)} %broadcast_in_dim.123), calls=%async_computation.3 | async-start | bytes 8192 | tf_op jit(solution)/shard_map/all_to_all | solution.py:163
  166.1 6.1 %all-to-all-done.3 = f32[8,1,64]{2,1,0:T(1,128)S(1)} async-done(((f32[8,1,64]{2,1,0:T(1,128)}), f32[8,1,64]{2,1,0:T(1,128)S(1)}, u32[]{:S(2)}, u32[]{:S(2)}) %all-to-all-start.3) | async-done | bytes 2080 | tf_op jit(solution)/shard_map/all_to_all | solution.py:163
  172.3 1.8 multiply_convert_fusion
  174.1 14.2 %copy.57 = bf16[256,8,2,1664]{3,1,2,0:T(8,128)(2,1)} copy(bf16[256,8,2,1664]{3,2,1,0:T(2,128)(2,1)} %bitcast.139) | data formatting | bytes 27262976
  188.3 27.6 %all-gather.2.cloned.1.call-done = bf16[1024,2048]{1,0:T(8,128)(2,1)} async-done(((bf16[64,2048]{1,0:T(8,128)(2,1)}), bf16[1024,2048]{1,0:T(8,128)(2,1)}) %all-gather.2.cloned.1.call-update) | async-done | bytes 4194320 | tf_op jit(solution)/shard_map/all_gather | solution.py:175
  215.9 19.7 %convolution_convert_fusion = bf16[1024,3328]{1,0:T(8,128)(2,1)S(1)} fusion(bf16[1024,2048]{1,0:T(8,128)(2,1)} %all-gather.2.cloned.1.call-done, bf16[2048,3328]{1,0:T(8,128)(2,1)} %bitcast.140), kind=kOutput, calls=%fused_computation.7 | convolution fusion | flops 13962051584 | bytes 24641536 | tf_op jit(solution)/shard_map/dot_general | solution.py:177
  235.6 85.5 %all_to_all.27 = bf16[8,128,3328]{2,1,0:T(8,128)(2,1)S(1)} all-to-all(bf16[8,128,3328]{2,1,0:T(8,128)(2,1)S(1)} %bitcast.142), channel_id=1, replica_groups=mesh['replica'=8,'tensor'=16] {'replica'}, dimensions={0} | all-to-all | bytes 13631488 | tf_op jit(solution)/shard_map/all_to_all | solution.py:178
  321.1 1.0 convert_reduce_fusion
  322.1 1.0 fusion.24
  (54 shorter events, 7.2 us)
Async XLA Ops:
  6.5 89.2 %copy-start = (bf16[512,2048]{1,0:T(8,128)(2,1)S(1)}, bf16[512,2048]{1,0:T(8,128)(2,1)}, u32[]{:S(2)}) copy-start(bf16[512,2048]{1,0:T(8,128)(2,1)} %param.18) | copy-start | bytes 6291460
  14.4 44.2 %copy-start.4 = (s32[64]{0:T(128)S(1)}, s32[64]{0:T(128)}, u32[]{:S(2)}) copy-start(s32[64]{0:T(128)} %param.16) | copy-start | bytes 772
  14.4 44.3 %copy-start.2 = (bf16[128,512]{1,0:T(8,128)(2,1)S(1)}, bf16[128,512]{1,0:T(8,128)(2,1)}, u32[]{:S(2)}) copy-start(bf16[128,512]{1,0:T(8,128)(2,1)} %param.11) | copy-start | bytes 393220
  16.0 41.3 %all-to-all-start = ((bf16[128,1,32,256]{3,2,1,0:T(8,128)(2,1)}), bf16[128,1,32,256]{3,2,1,0:T(8,128)(2,1)}, u32[]{:S(2)}, u32[]{:S(2)}) async-start(bf16[128,1,32,256]{3,2,1,0:T(8,128)(2,1)} %bitcast.141), calls=%async_computation | async-start | bytes 4194304 | tf_op jit(solution)/shard_map/all_to_all | solution.py:56
  57.2 10.4 %collective-permute-start = (bf16[128,1,32,256]{3,2,1,0:T(8,128)(2,1)}, bf16[128,1,32,256]{3,2,1,0:T(8,128)(2,1)}, u32[]{:S(2)}, u32[]{:S(2)}) collective-permute-start(bf16[128,1,32,256]{3,2,1,0:T(8,128)(2,1)} %all-to-all-done), channel_id=1, source_target_pairs={{0,1},{1,0},{2,3},{3,2},{4,5},{5,4},{6,7},{7,6},{8,9},{9,8},{10,11... | collective-permute-start | bytes 6291464 | tf_op jit(solution)/shard_map/ppermute | solution.py:59
  100.1 57.7 %all-to-all-start.2 = ((bf16[16,64,2048]{2,1,0:T(8,128)(2,1)}), bf16[16,64,2048]{2,1,0:T(8,128)(2,1)}, u32[]{:S(2)}, u32[]{:S(2)}) async-start(bf16[16,64,2048]{2,1,0:T(8,128)(2,1)} %bitcast.146), calls=%async_computation.2 | async-start | bytes 8388608 | tf_op jit(solution)/shard_map/all_to_all | solution.py:150
  105.2 60.9 %copy-start.3 = (bf16[2048]{0:T(1024)(128)(2,1)S(1)}, bf16[2048]{0:T(1024)(128)(2,1)}, u32[]{:S(2)}) copy-start(bf16[2048]{0:T(1024)(128)(2,1)} %param.20) | copy-start | bytes 12292
  162.5 9.7 %all-to-all-start.3 = ((f32[8,1,64]{2,1,0:T(1,128)}), f32[8,1,64]{2,1,0:T(1,128)S(1)}, u32[]{:S(2)}, u32[]{:S(2)}) async-start(f32[8,1,64]{2,1,0:T(1,128)} %broadcast_in_dim.123), calls=%async_computation.3 | async-start | bytes 8192 | tf_op jit(solution)/shard_map/all_to_all | solution.py:163
  165.9 50.0 %all-gather.2.cloned.1.call-start = ((), (), s32[]{:S(2)}) async-start(), calls=%async_computation.5 | async-start | bytes 4456448 | tf_op jit(solution)/shard_map/all_gather | solution.py:175
  235.6 87.5 %copy-start.1 = (bf16[512,2048]{1,0:T(8,128)(2,1)S(1)}, bf16[512,2048]{1,0:T(8,128)(2,1)}, u32[]{:S(2)}) copy-start(bf16[512,2048]{1,0:T(8,128)(2,1)} %param.18) | copy-start | bytes 6291460
Sparse Core Ops, SparseCore 0:
  174.2 41.6 all-gather.1

commit v11 on v10

--- a/solution.py
+++ b/solution.py
@@ -30,10 +30,10 @@
     norm_gain,
     gate_up,
 ):
-    replicas = lax.axis_size("replica")
-    tensors = lax.axis_size("tensor")
-    replica_idx = lax.axis_index("replica")
-    tensor_idx = lax.axis_index("tensor")
+    replicas = lax.axis_size(("zh", "y"))
+    tensors = lax.axis_size(("x", "zl", "core"))
+    replica_idx = lax.axis_index(("zh", "y"))
+    tensor_idx = lax.axis_index(("x", "zl", "core"))
     sessions = SHARE * replicas
     heads_local = HEADS // tensors
     pair_width = 2 * HD
@@ -54,9 +54,9 @@
         (replicas, KVH, lanes_per_head // 2, 2, half, pair_width),
     ).reshape(replicas * tensors, SHARE, half, pair_width)
     arrived = lax.all_to_all(
-        outgoing, ("replica", "tensor"), split_axis=0, concat_axis=0, tiled=True
-    )
-    partner = lax.ppermute(arrived, "tensor", [(i, i ^ 1) for i in range(tensors)])
+        outgoing, ("zh", "y", "x", "zl", "core"), split_axis=0, concat_axis=0, tiled=True
+    )
+    partner = lax.ppermute(arrived, ("x", "zl", "core"), [(i, i ^ 1) for i in range(tensors)])
     mine_first = (tensor_idx % 2) == 0
     low_half = jnp.where(mine_first, arrived, partner)
     high_half = jnp.where(mine_first, partner, arrived)
@@ -134,11 +134,17 @@
     attended = jnp.take(slot_attended, back_index, axis=0)
     gathered = lax.all_to_all(
         jnp.broadcast_to(attended[None], (replicas,) + attended.shape),
-        "replica",
+        ("zh", "y"),
         split_axis=0,
         concat_axis=0,
         tiled=True,
     ).reshape(replicas * rows_here, attended.shape[1])
+    blocks = lax.axis_size(("x", "zl", "core"))
+    pairs = blocks // 2
+    block_of = (np.arange(blocks) % 2) * pairs + np.arange(blocks) // 2
+    gathered = gathered.reshape(blocks, -1, gathered.shape[1])[block_of].reshape(
+        gathered.shape
+    )
     partial_out = jnp.dot(
         gathered,
         out_weight,
@@ -149,20 +155,21 @@
     part_rows = all_rows // tensors
     head_parts = lax.all_to_all(
         partial_out.astype(jnp.bfloat16).reshape(tensors, part_rows, width),
-        "tensor",
+        ("x", "zl", "core"),
         split_axis=0,
         concat_axis=0,
         tiled=True,
     )
     head_sum = jnp.sum(head_parts.astype(jnp.float32), axis=0)
-    my_residual = lax.dynamic_slice_in_dim(residual, tensor_idx * part_rows, part_rows, 0)
+    my_block = (tensor_idx % 2) * pairs + tensor_idx // 2
+    my_residual = lax.dynamic_slice_in_dim(residual, my_block * part_rows, part_rows, 0)
     carried = my_residual.astype(jnp.float32) + head_sum
     gain_row = norm_gain.astype(jnp.float32)
     own_squares = jnp.sum(carried * carried, axis=1)
     squares = jnp.sum(
         lax.all_to_all(
             jnp.broadcast_to(own_squares[None], (replicas,) + own_squares.shape),
-            "replica",
+            ("zh", "y"),
             split_axis=0,
             concat_axis=0,
             tiled=True,
@@ -172,12 +179,14 @@
     normed_part = (
         carried * lax.rsqrt(squares / D + EPSILON)[:, None] * gain_row[None, :]
     ).astype(jnp.bfloat16)
-    normed = lax.all_gather(normed_part, "tensor", axis=0, tiled=True)
+    normed = lax.all_gather(
+        lax.all_gather(normed_part, ("x", "zl"), axis=0, tiled=True), "core", axis=0, tiled=True
+    )
     weights_local = gate_up.reshape(gate_up.shape[0], 2 * gate_up.shape[2])
     slab = jnp.dot(normed, weights_local, preferred_element_type=jnp.float32)
     slab_parts = lax.all_to_all(
         slab.astype(jnp.bfloat16).reshape(replicas, rows_here, slab.shape[1]),
-        "replica",
+        ("zh", "y"),
         split_axis=0,
         concat_axis=0,
         tiled=True,
@@ -190,19 +199,24 @@
 
 
 def solution(mesh):
+    fine = jax.sharding.Mesh(
+        mesh.devices.reshape(2, 4, 4, 2, 2), ("zh", "y", "x", "zl", "core")
+    )
+    rep = ("zh", "y")
+    ten = ("x", "zl", "core")
     placed = (
-        P("replica", "tensor"),
-        P("replica", None),
-        P(("replica", "tensor"), None, None),
-        P(),
-        P(),
-        P(),
-        P(),
-        P("tensor", "replica"),
-        P(None, "replica"),
-        P("replica"),
-        P("replica", None, "tensor"),
+        P(rep, ten),
+        P(rep, None),
+        P(rep + ten, None, None),
+        P(),
+        P(),
+        P(),
+        P(),
+        P(ten, rep),
+        P(None, rep),
+        P(rep),
+        P(rep, None, ten),
     )
     return jax.shard_map(
-        per_device, mesh=mesh, in_specs=placed, out_specs=P("replica", "tensor"), check_vma=False
-    )
+        per_device, mesh=fine, in_specs=placed, out_specs=P(rep, ten), check_vma=False
+    )

time: 331 us -> 369 us (1.11)
  waiting for transfers between devices: 113 us -> 164 us
  blocking collectives: 106 us -> 85.8 us
    all_gather x1 -> x2, waiting for transfers between devices: 27.6 us -> 60.8 us  [the longest x1 53.8 us: per_device(): lax.all_gather(normed_part, ('x', 'zl'), axis=0, tiled=True)]
    all_to_all x1 -> x0, blocking collectives: 20.1 us -> none  [per_device(): lax.all_to_all(jnp.broadcast_to(attended[None], (replicas,) + attended.sh...]
    all_to_all x1 -> x2, waiting for transfers between devices: 26.7 us -> 44 us  [the longest x1 26.7 us: per_device(): lax.all_to_all(outgoing, ('zh', 'y', 'x', 'zl', 'core'), split_axis=0, co...]
    all_to_all x1 -> x2, starting transfers between devices: 11.9 us -> 15.5 us  [the longest x1 11.9 us: per_device(): lax.all_to_all(outgoing, ('zh', 'y', 'x', 'zl', 'core'), split_axis=0, co...]
    unnamed x13 -> x15, local copies, waits for them, and re-layouts: 14.4 us -> 14.4 us
  transfers between devices with their start and end apart: 5 -> 7, of which waited for: 4 -> 6; matrix products, arithmetic and copies ran while one was open for 8% -> 7% of each run, Pallas kernels for 0% -> 0%
where the time goes in v11:
time: 369 us; the launch traced here: 368 us
  waiting for transfers between devices  164 us (44%)
  blocking collectives  85.8 us (23%)
  local copies, waits for them, and re-layouts  32 us (9%)
  matrix products  28.4 us (8%)
  starting transfers between devices  25.5 us (7%)
  other arithmetic  19.1 us (5%)
  between operations  13.8 us (4%)
    all_to_all x1, blocking collectives, per_device(): lax.all_to_all(slab.astype(jnp.bfloat16).reshape(replicas, rows_here, sla...  85.8 us
    all_gather x1, waiting for transfers between devices, per_device(): lax.all_gather(normed_part, ('x', 'zl'), axis=0, tiled=True)  53.8 us
    all_to_all x1, waiting for transfers between devices, per_device(): lax.all_to_all(partial_out.astype(jnp.bfloat16).reshape(tensors, part_row...  52.6 us
    all_to_all x1, waiting for transfers between devices, per_device(): lax.all_to_all(outgoing, ('zh', 'y', 'x', 'zl', 'core'), split_axis=0, co...  26.7 us
    dot_general x1, matrix products, per_device(): slab = jnp.dot(normed, weights_local, preferred_element_type=jnp.float32)  19.7 us
    all_to_all x1, waiting for transfers between devices, per_device(): lax.all_to_all(jnp.broadcast_to(attended[None], (replicas,) + attended.sh...  17.3 us
    unnamed x15, local copies, waits for them, and re-layouts  14.4 us
    all_to_all x1, starting transfers between devices, per_device(): lax.all_to_all(outgoing, ('zh', 'y', 'x', 'zl', 'core'), split_axis=0, co...  11.9 us
  transfers between devices with their start and end apart: 7, of which 6 were waited for; matrix products, arithmetic and copies ran while one was open for 7% of the time, Pallas kernels for 0%

profile of v11, /device:TPU:1, one launch (start us, length us, event | category | flops | bytes accessed | tf_op | source)
XLA Modules:
  0.0 368.2 jit_solution(13538674326756462328)
XLA Ops:
  6.5 0.9 constant_dynamic-slice_fusion.1
  9.0 2.8 gather_fusion.1
  11.8 1.9 gather.41
  14.4 1.6 broadcast_in_dim.114
  16.0 11.9 %all-to-all-start = ((bf16[128,1,32,256]{3,2,1,0:T(8,128)(2,1)}), bf16[128,1,32,256]{3,2,1,0:T(8,128)(2,1)}, u32[]{:S(2)}, u32[]{:S(2)}) async-start(bf16[128,1,32,256]{3,2,1,0:T(8,128)(2,1)} %bitcast.142), calls=%async_computation | async-start | bytes 4194304 | tf_op jit(solution)/shard_map/all_to_all | solution.py:56
  30.5 26.7 %all-to-all-done = bf16[128,1,32,256]{3,2,1,0:T(8,128)(2,1)} async-done(((bf16[128,1,32,256]{3,2,1,0:T(8,128)(2,1)}), bf16[128,1,32,256]{3,2,1,0:T(8,128)(2,1)}, u32[]{:S(2)}, u32[]{:S(2)}) %all-to-all-start) | async-done | bytes 2097184 | tf_op jit(solution)/shard_map/all_to_all | solution.py:56
  57.2 1.3 collective-permute-start
  58.7 1.2 gather_fusion.3
  59.9 1.0 gather_fusion.2
  61.7 5.0 %compare_and_fusion.1 = (pred[128]{0:T(512)(128)(4,1)S(1)}, s32[128]{0:T(128)S(1)}) fusion(s32[128]{0:T(128)S(1)} %convert_reduce_fusion.2, s32[]{:T(128)} %bitcast.12, s32[]{:T(128)} %bitcast.11, s32[]{:T(128)} %bitcast.10, s32[]{:T(128)} %bitcast.9, s32[]{:T(128)} %bitcast.8, s32[]{:T(128)} %bitcast.7, s32[]{:T(128)} %bitcast.6, s32[]{:T(128)} %bitcast.5), kind=kLoop, calls=%fused_computation.85 | loop fusion | flops 4224 | bytes 1184 | tf_op jit(solution)/shard_map/jit(_take)/and | solution.py:134
  67.7 2.5 broadcast_select_fusion.1
  71.9 1.1 fusion.1
  73.0 1.4 fusion.21
  75.6 1.1 broadcast_in_dim.125
  76.7 3.6 all-to-all-start.1
  80.3 17.3 %all-to-all-done.1 = bf16[8,128,512]{2,1,0:T(8,128)(2,1)S(1)} async-done(((bf16[8,128,512]{2,1,0:T(8,128)(2,1)}), bf16[8,128,512]{2,1,0:T(8,128)(2,1)S(1)}, u32[]{:S(2)}, u32[]{:S(2)}) %all-to-all-start.1) | async-done | bytes 1048608 | tf_op jit(solution)/shard_map/all_to_all | solution.py:135
  97.6 1.6 gather_fusion.5
  99.2 5.5 %convolution_convert_fusion.1 = bf16[1024,2048]{1,0:T(8,128)(2,1)} fusion(bf16[1024,512]{1,0:T(8,128)(2,1)} %bitcast.149, bf16[512,2048]{1,0:T(8,128)(2,1)S(1)} %copy-done), kind=kOutput, calls=%fused_computation.14 | convolution fusion | flops 2149580800 | bytes 7340032 | tf_op jit(solution)/shard_map/dot_general | solution.py:148
  104.6 5.0 %all-to-all-start.2 = ((bf16[16,64,2048]{2,1,0:T(8,128)(2,1)}), bf16[16,64,2048]{2,1,0:T(8,128)(2,1)}, u32[]{:S(2)}, u32[]{:S(2)}) async-start(bf16[16,64,2048]{2,1,0:T(8,128)(2,1)} %bitcast.146), calls=%async_computation.2 | async-start | bytes 8388608 | tf_op jit(solution)/shard_map/all_to_all | solution.py:156
  109.7 52.6 %all-to-all-done.2 = bf16[16,64,2048]{2,1,0:T(8,128)(2,1)} async-done(((bf16[16,64,2048]{2,1,0:T(8,128)(2,1)}), bf16[16,64,2048]{2,1,0:T(8,128)(2,1)}, u32[]{:S(2)}, u32[]{:S(2)}) %all-to-all-start.2) | async-done | bytes 4194336 | tf_op jit(solution)/shard_map/all_to_all | solution.py:156
  162.3 3.0 convert_reduce_fusion.1
  165.3 1.1 multiply_reduce_fusion
  167.1 3.5 all-to-all-start.3
  170.6 6.3 %all-to-all-done.3 = f32[8,1,64]{2,1,0:T(1,128)S(1)} async-done(((f32[8,1,64]{2,1,0:T(1,128)}), f32[8,1,64]{2,1,0:T(1,128)S(1)}, u32[]{:S(2)}, u32[]{:S(2)}) %all-to-all-start.3) | async-done | bytes 2080 | tf_op jit(solution)/shard_map/all_to_all | solution.py:170
  177.0 1.8 multiply_convert_fusion
  178.8 53.8 %all-gather.3.cloned.1.call-done = bf16[512,2048]{1,0:T(8,128)(2,1)} async-done(((bf16[64,2048]{1,0:T(8,128)(2,1)}), bf16[512,2048]{1,0:T(8,128)(2,1)}) %all-gather.3.cloned.1.call-update) | async-done | bytes 2097168 | tf_op jit(solution)/shard_map/all_gather | solution.py:183
  232.6 14.2 %copy.59 = bf16[256,8,2,1664]{3,1,2,0:T(8,128)(2,1)} copy(bf16[256,8,2,1664]{3,2,1,0:T(2,128)(2,1)} %bitcast.140) | data formatting | bytes 27262976
  246.9 7.0 %all-gather.5.cloned.1.call-done = bf16[1024,2048]{1,0:T(8,128)(2,1)} async-done(((bf16[512,2048]{1,0:T(8,128)(2,1)}), bf16[1024,2048]{1,0:T(8,128)(2,1)}) %all-gather.5.cloned.1.call-update) | async-done | bytes 4194320 | tf_op jit(solution)/shard_map/all_gather | solution.py:182
  253.9 19.7 %convolution_convert_fusion = bf16[1024,3328]{1,0:T(8,128)(2,1)S(1)} fusion(bf16[1024,2048]{1,0:T(8,128)(2,1)} %all-gather.5.cloned.1.call-done, bf16[2048,3328]{1,0:T(8,128)(2,1)} %bitcast.141), kind=kOutput, calls=%fused_computation.8 | convolution fusion | flops 13962051584 | bytes 24641536 | tf_op jit(solution)/shard_map/dot_general | solution.py:186
  273.6 85.8 %all_to_all.26 = bf16[8,128,3328]{2,1,0:T(8,128)(2,1)S(1)} all-to-all(bf16[8,128,3328]{2,1,0:T(8,128)(2,1)S(1)} %bitcast.143), channel_id=1, replica_groups=mesh['zh'=2,'y'=4,'x'=4,'zl'=2,'core'=2] {'zh','y'}, dimensions={0} | all-to-all | bytes 13631488 | tf_op jit(solution)/shard_map/all_to_all | solution.py:187
  359.4 1.0 convert_reduce_fusion
  360.3 1.0 fusion.24
  (62 shorter events, 10.4 us)
Async XLA Ops:
  6.5 92.6 %copy-start = (bf16[512,2048]{1,0:T(8,128)(2,1)S(1)}, bf16[512,2048]{1,0:T(8,128)(2,1)}, u32[]{:S(2)}) copy-start(bf16[512,2048]{1,0:T(8,128)(2,1)} %param.20) | copy-start | bytes 6291460
  14.4 44.2 %copy-start.5 = (s32[64]{0:T(128)S(1)}, s32[64]{0:T(128)}, u32[]{:S(2)}) copy-start(s32[64]{0:T(128)} %param.18) | copy-start | bytes 772
  14.4 44.3 %copy-start.2 = (bf16[128,512]{1,0:T(8,128)(2,1)S(1)}, bf16[128,512]{1,0:T(8,128)(2,1)}, u32[]{:S(2)}) copy-start(bf16[128,512]{1,0:T(8,128)(2,1)} %param.13) | copy-start | bytes 393220
  16.0 41.3 %all-to-all-start = ((bf16[128,1,32,256]{3,2,1,0:T(8,128)(2,1)}), bf16[128,1,32,256]{3,2,1,0:T(8,128)(2,1)}, u32[]{:S(2)}, u32[]{:S(2)}) async-start(bf16[128,1,32,256]{3,2,1,0:T(8,128)(2,1)} %bitcast.142), calls=%async_computation | async-start | bytes 4194304 | tf_op jit(solution)/shard_map/all_to_all | solution.py:56
  57.2 10.4 %collective-permute-start = (bf16[128,1,32,256]{3,2,1,0:T(8,128)(2,1)}, bf16[128,1,32,256]{3,2,1,0:T(8,128)(2,1)}, u32[]{:S(2)}, u32[]{:S(2)}) collective-permute-start(bf16[128,1,32,256]{3,2,1,0:T(8,128)(2,1)} %all-to-all-done), channel_id=1, source_target_pairs={{0,1},{1,0},{2,3},{3,2},{4,5},{5,4},{6,7},{7,6},{8,9},{9,8},{10,11... | collective-permute-start | bytes 6291464 | tf_op jit(solution)/shard_map/ppermute | solution.py:59
  74.5 5.8 %copy-start.4 = (s32[16]{0:T(128)S(1)}, s32[16]{0:T(128)}, u32[]{:S(2)}) copy-start(s32[16]{0:T(128)} %constant.194) | copy-start | bytes 196
  76.7 20.9 %all-to-all-start.1 = ((bf16[8,128,512]{2,1,0:T(8,128)(2,1)}), bf16[8,128,512]{2,1,0:T(8,128)(2,1)S(1)}, u32[]{:S(2)}, u32[]{:S(2)}) async-start(bf16[8,128,512]{2,1,0:T(8,128)(2,1)} %broadcast_in_dim.125), calls=%async_computation.1 | async-start | bytes 2097152 | tf_op jit(solution)/shard_map/all_to_all | solution.py:135
  104.6 57.7 %all-to-all-start.2 = ((bf16[16,64,2048]{2,1,0:T(8,128)(2,1)}), bf16[16,64,2048]{2,1,0:T(8,128)(2,1)}, u32[]{:S(2)}, u32[]{:S(2)}) async-start(bf16[16,64,2048]{2,1,0:T(8,128)(2,1)} %bitcast.146), calls=%async_computation.2 | async-start | bytes 8388608 | tf_op jit(solution)/shard_map/all_to_all | solution.py:156
  109.7 60.9 %copy-start.3 = (bf16[2048]{0:T(1024)(128)(2,1)S(1)}, bf16[2048]{0:T(1024)(128)(2,1)}, u32[]{:S(2)}) copy-start(bf16[2048]{0:T(1024)(128)(2,1)} %param.22) | copy-start | bytes 12292
  167.1 9.9 %all-to-all-start.3 = ((f32[8,1,64]{2,1,0:T(1,128)}), f32[8,1,64]{2,1,0:T(1,128)S(1)}, u32[]{:S(2)}, u32[]{:S(2)}) async-start(f32[8,1,64]{2,1,0:T(1,128)} %broadcast_in_dim.127), calls=%async_computation.3 | async-start | bytes 8192 | tf_op jit(solution)/shard_map/all_to_all | solution.py:170
  170.6 62.0 %all-gather.3.cloned.1.call-start = ((), (), s32[]{:S(2)}) async-start(), calls=%async_computation.5 | async-start | bytes 2359296 | tf_op jit(solution)/shard_map/all_gather | solution.py:183
  178.8 75.1 %all-gather.5.cloned.1.call-start = ((), (), s32[]{:S(2)}) async-start(), calls=%async_computation.6 | async-start | bytes 6291456 | tf_op jit(solution)/shard_map/all_gather | solution.py:182
  273.6 87.7 %copy-start.1 = (bf16[512,2048]{1,0:T(8,128)(2,1)S(1)}, bf16[512,2048]{1,0:T(8,128)(2,1)}, u32[]{:S(2)}) copy-start(bf16[512,2048]{1,0:T(8,128)(2,1)} %param.20) | copy-start | bytes 6291460
Sparse Core Ops, SparseCore 0:
  178.9 53.6 all-gather.2
  234.2 19.5 all-gather.4

commit v12 on v10

--- a/solution.py
+++ b/solution.py
@@ -57,10 +57,7 @@
         outgoing, ("replica", "tensor"), split_axis=0, concat_axis=0, tiled=True
     )
     partner = lax.ppermute(arrived, "tensor", [(i, i ^ 1) for i in range(tensors)])
-    mine_first = (tensor_idx % 2) == 0
-    low_half = jnp.where(mine_first, arrived, partner)
-    high_half = jnp.where(mine_first, partner, arrived)
-    arrived = jnp.concatenate([low_half, high_half], axis=2)
+    arrived = jnp.concatenate([arrived, partner], axis=2)
     arrived = arrived.reshape(replicas, tensors, SHARE, PAGE, pair_width)
     prefix_blocks = jnp.transpose(arrived, (0, 2, 1, 3, 4)).reshape(
         sessions, cached_len, pair_width
@@ -84,7 +81,8 @@
     )
     slot_fresh = jnp.take(fresh_pair, padded_index, axis=0).reshape(sessions, slot_rows, pair_width)
     lengths = lax.dynamic_slice_in_dim(prefix_len, replica_idx * sessions, sessions, 0)
-    key_pos = jnp.arange(cached_len, dtype=jnp.int32)
+    key_ids = jnp.arange(cached_len, dtype=jnp.int32)
+    key_pos = (key_ids // PAGE) * PAGE + (key_ids % PAGE + (tensor_idx % 2) * half) % PAGE
     prefix_mask = (key_pos[None, :] < lengths[:, None])[:, None, :]
     fresh_mask = (offsets[None, None, :] <= offsets[None, :, None]) & (
         offsets[None, None, :] < counts[:, None, None]

time: 331 us -> 330 us (level)
  no operation moved by 1% of the time
where the time goes in v12:
time: 330 us; the launch traced here: 329 us
  waiting for transfers between devices  112 us (34%)
  blocking collectives  106 us (32%)
  local copies, waits for them, and re-layouts  29.4 us (9%)
  matrix products  27.2 us (8%)
  starting transfers between devices  21.9 us (7%)
  other arithmetic  19 us (6%)
  between operations  13.7 us (4%)
    all_to_all x1, blocking collectives, per_device(): lax.all_to_all(slab.astype(jnp.bfloat16).reshape(replicas, rows_here, sla...  85.5 us
    all_to_all x1, waiting for transfers between devices, per_device(): lax.all_to_all(partial_out.astype(jnp.bfloat16).reshape(tensors, part_row...  52.6 us
    all_gather x1, waiting for transfers between devices, per_device(): normed = lax.all_gather(normed_part, 'tensor', axis=0, tiled=True)  27.6 us
    all_to_all x1, waiting for transfers between devices, per_device(): lax.all_to_all(outgoing, ('replica', 'tensor'), split_axis=0, concat_axis...  26 us
    all_to_all x1, blocking collectives, per_device(): lax.all_to_all(jnp.broadcast_to(attended[None], (replicas,) + attended.sh...  20.1 us
    dot_general x1, matrix products, per_device(): slab = jnp.dot(normed, weights_local, preferred_element_type=jnp.float32)  19.7 us
    unnamed x13, local copies, waits for them, and re-layouts  14.4 us
    all_to_all x1, starting transfers between devices, per_device(): lax.all_to_all(outgoing, ('replica', 'tensor'), split_axis=0, concat_axis...  11.9 us
  transfers between devices with their start and end apart: 5, of which 4 were waited for; matrix products, arithmetic and copies ran while one was open for 8% of the time, Pallas kernels for 0%

profile of v12, /device:TPU:1, one launch (start us, length us, event | category | flops | bytes accessed | tf_op | source)
XLA Modules:
  0.0 329.1 jit_solution(6830536024076237477)
XLA Ops:
  6.5 0.9 constant_dynamic-slice_fusion.1
  7.6 0.8 dynamic-slice_bitcast_fusion
  9.0 2.8 gather_fusion.1
  11.8 1.9 gather.38
  14.4 1.6 broadcast_in_dim.111
  16.0 11.9 %all-to-all-start = ((bf16[128,1,32,256]{3,2,1,0:T(8,128)(2,1)}), bf16[128,1,32,256]{3,2,1,0:T(8,128)(2,1)}, u32[]{:S(2)}, u32[]{:S(2)}) async-start(bf16[128,1,32,256]{3,2,1,0:T(8,128)(2,1)} %bitcast.141), calls=%async_computation | async-start | bytes 4194304 | tf_op jit(solution)/shard_map/all_to_all | solution.py:56
  30.4 0.8 constant_dynamic-slice_fusion
  31.2 26.0 %all-to-all-done = bf16[128,1,32,256]{3,2,1,0:T(8,128)(2,1)} async-done(((bf16[128,1,32,256]{3,2,1,0:T(8,128)(2,1)}), bf16[128,1,32,256]{3,2,1,0:T(8,128)(2,1)}, u32[]{:S(2)}, u32[]{:S(2)}) %all-to-all-start) | async-done | bytes 2097184 | tf_op jit(solution)/shard_map/all_to_all | solution.py:56
  57.2 1.3 collective-permute-start
  58.7 1.2 gather_fusion.3
  59.9 1.0 gather_fusion.2
  61.0 5.0 %compare_and_fusion.1 = (pred[128]{0:T(512)(128)(4,1)S(1)}, s32[128]{0:T(128)S(1)}) fusion(s32[128]{0:T(128)S(1)} %convert_reduce_fusion.2, s32[]{:T(128)} %bitcast.12, s32[]{:T(128)} %bitcast.11, s32[]{:T(128)} %bitcast.10, s32[]{:T(128)} %bitcast.9, s32[]{:T(128)} %bitcast.8, s32[]{:T(128)} %bitcast.7, s32[]{:T(128)} %bitcast.6, s32[]{:T(128)} %bitcast.5), kind=kLoop, calls=%fused_computation.99 | loop fusion | flops 4224 | bytes 1184 | tf_op jit(solution)/shard_map/jit(_take)/and | solution.py:132
  67.1 2.7 pad_maximum_fusion
  69.8 0.9 bitcast_reduce_fusion
  71.1 1.1 fusion.1
  72.2 1.4 fusion.21
  73.8 0.8 gather_fusion.4
  74.9 20.1 %all_to_all.26 = bf16[8,128,512]{2,1,0:T(8,128)(2,1)S(1)} all-to-all(bf16[8,128,512]{2,1,0:T(8,128)(2,1)S(1)} %broadcast_in_dim.122), channel_id=1, replica_groups=mesh['replica'=8,'tensor'=16] {'replica'}, dimensions={0} | all-to-all | bytes 2097152 | tf_op jit(solution)/shard_map/all_to_all | solution.py:133
  95.0 4.3 %convolution_convert_fusion.1 = bf16[1024,2048]{1,0:T(8,128)(2,1)} fusion(bf16[1024,512]{1,0:T(8,128)(2,1)S(1)} %bitcast.147, bf16[512,2048]{1,0:T(8,128)(2,1)S(1)} %copy-done), kind=kOutput, calls=%fused_computation.13 | convolution fusion | flops 2149580800 | bytes 7340032 | tf_op jit(solution)/shard_map/dot_general | solution.py:140
  99.3 5.1 %all-to-all-start.2 = ((bf16[16,64,2048]{2,1,0:T(8,128)(2,1)}), bf16[16,64,2048]{2,1,0:T(8,128)(2,1)}, u32[]{:S(2)}, u32[]{:S(2)}) async-start(bf16[16,64,2048]{2,1,0:T(8,128)(2,1)} %bitcast.146), calls=%async_computation.2 | async-start | bytes 8388608 | tf_op jit(solution)/shard_map/all_to_all | solution.py:148
  104.3 52.6 %all-to-all-done.2 = bf16[16,64,2048]{2,1,0:T(8,128)(2,1)} async-done(((bf16[16,64,2048]{2,1,0:T(8,128)(2,1)}), bf16[16,64,2048]{2,1,0:T(8,128)(2,1)}, u32[]{:S(2)}, u32[]{:S(2)}) %all-to-all-start.2) | async-done | bytes 4194336 | tf_op jit(solution)/shard_map/all_to_all | solution.py:148
  157.0 3.0 convert_reduce_fusion.1
  160.0 1.1 multiply_reduce_fusion
  161.7 3.3 %all-to-all-start.3 = ((f32[8,1,64]{2,1,0:T(1,128)}), f32[8,1,64]{2,1,0:T(1,128)S(1)}, u32[]{:S(2)}, u32[]{:S(2)}) async-start(f32[8,1,64]{2,1,0:T(1,128)} %broadcast_in_dim.123), calls=%async_computation.3 | async-start | bytes 8192 | tf_op jit(solution)/shard_map/all_to_all | solution.py:161
  165.3 6.1 %all-to-all-done.3 = f32[8,1,64]{2,1,0:T(1,128)S(1)} async-done(((f32[8,1,64]{2,1,0:T(1,128)}), f32[8,1,64]{2,1,0:T(1,128)S(1)}, u32[]{:S(2)}, u32[]{:S(2)}) %all-to-all-start.3) | async-done | bytes 2080 | tf_op jit(solution)/shard_map/all_to_all | solution.py:161
  171.5 1.8 multiply_convert_fusion
  173.2 14.2 %copy.57 = bf16[256,8,2,1664]{3,1,2,0:T(8,128)(2,1)} copy(bf16[256,8,2,1664]{3,2,1,0:T(2,128)(2,1)} %bitcast.139) | data formatting | bytes 27262976
  187.5 27.6 %all-gather.2.cloned.1.call-done = bf16[1024,2048]{1,0:T(8,128)(2,1)} async-done(((bf16[64,2048]{1,0:T(8,128)(2,1)}), bf16[1024,2048]{1,0:T(8,128)(2,1)}) %all-gather.2.cloned.1.call-update) | async-done | bytes 4194320 | tf_op jit(solution)/shard_map/all_gather | solution.py:173
  215.1 19.7 %convolution_convert_fusion = bf16[1024,3328]{1,0:T(8,128)(2,1)S(1)} fusion(bf16[1024,2048]{1,0:T(8,128)(2,1)} %all-gather.2.cloned.1.call-done, bf16[2048,3328]{1,0:T(8,128)(2,1)} %bitcast.140), kind=kOutput, calls=%fused_computation.7 | convolution fusion | flops 13962051584 | bytes 24641536 | tf_op jit(solution)/shard_map/dot_general | solution.py:175
  234.8 85.5 %all_to_all.27 = bf16[8,128,3328]{2,1,0:T(8,128)(2,1)S(1)} all-to-all(bf16[8,128,3328]{2,1,0:T(8,128)(2,1)S(1)} %bitcast.142), channel_id=1, replica_groups=mesh['replica'=8,'tensor'=16] {'replica'}, dimensions={0} | all-to-all | bytes 13631488 | tf_op jit(solution)/shard_map/all_to_all | solution.py:176
  320.3 1.0 convert_reduce_fusion
  321.3 1.0 fusion.24
  (55 shorter events, 6.9 us)
Async XLA Ops:
  6.5 88.4 %copy-start = (bf16[512,2048]{1,0:T(8,128)(2,1)S(1)}, bf16[512,2048]{1,0:T(8,128)(2,1)}, u32[]{:S(2)}) copy-start(bf16[512,2048]{1,0:T(8,128)(2,1)} %param.18) | copy-start | bytes 6291460
  14.4 44.2 %copy-start.4 = (s32[64]{0:T(128)S(1)}, s32[64]{0:T(128)}, u32[]{:S(2)}) copy-start(s32[64]{0:T(128)} %param.16) | copy-start | bytes 772
  14.4 44.3 %copy-start.2 = (bf16[128,512]{1,0:T(8,128)(2,1)S(1)}, bf16[128,512]{1,0:T(8,128)(2,1)}, u32[]{:S(2)}) copy-start(bf16[128,512]{1,0:T(8,128)(2,1)} %param.11) | copy-start | bytes 393220
  16.0 41.3 %all-to-all-start = ((bf16[128,1,32,256]{3,2,1,0:T(8,128)(2,1)}), bf16[128,1,32,256]{3,2,1,0:T(8,128)(2,1)}, u32[]{:S(2)}, u32[]{:S(2)}) async-start(bf16[128,1,32,256]{3,2,1,0:T(8,128)(2,1)} %bitcast.141), calls=%async_computation | async-start | bytes 4194304 | tf_op jit(solution)/shard_map/all_to_all | solution.py:56
  57.2 9.8 %collective-permute-start = (bf16[128,1,32,256]{3,2,1,0:T(8,128)(2,1)}, bf16[128,1,32,256]{3,2,1,0:T(8,128)(2,1)}, u32[]{:S(2)}, u32[]{:S(2)}) collective-permute-start(bf16[128,1,32,256]{3,2,1,0:T(8,128)(2,1)} %all-to-all-done), channel_id=1, source_target_pairs={{0,1},{1,0},{2,3},{3,2},{4,5},{5,4},{6,7},{7,6},{8,9},{9,8},{10,11... | collective-permute-start | bytes 6291464 | tf_op jit(solution)/shard_map/ppermute | solution.py:59
  99.3 57.7 %all-to-all-start.2 = ((bf16[16,64,2048]{2,1,0:T(8,128)(2,1)}), bf16[16,64,2048]{2,1,0:T(8,128)(2,1)}, u32[]{:S(2)}, u32[]{:S(2)}) async-start(bf16[16,64,2048]{2,1,0:T(8,128)(2,1)} %bitcast.146), calls=%async_computation.2 | async-start | bytes 8388608 | tf_op jit(solution)/shard_map/all_to_all | solution.py:148
  104.3 60.9 %copy-start.3 = (bf16[2048]{0:T(1024)(128)(2,1)S(1)}, bf16[2048]{0:T(1024)(128)(2,1)}, u32[]{:S(2)}) copy-start(bf16[2048]{0:T(1024)(128)(2,1)} %param.20) | copy-start | bytes 12292
  161.7 9.7 %all-to-all-start.3 = ((f32[8,1,64]{2,1,0:T(1,128)}), f32[8,1,64]{2,1,0:T(1,128)S(1)}, u32[]{:S(2)}, u32[]{:S(2)}) async-start(f32[8,1,64]{2,1,0:T(1,128)} %broadcast_in_dim.123), calls=%async_computation.3 | async-start | bytes 8192 | tf_op jit(solution)/shard_map/all_to_all | solution.py:161
  165.0 50.0 %all-gather.2.cloned.1.call-start = ((), (), s32[]{:S(2)}) async-start(), calls=%async_computation.5 | async-start | bytes 4456448 | tf_op jit(solution)/shard_map/all_gather | solution.py:173
  234.8 87.5 %copy-start.1 = (bf16[512,2048]{1,0:T(8,128)(2,1)S(1)}, bf16[512,2048]{1,0:T(8,128)(2,1)}, u32[]{:S(2)}) copy-start(bf16[512,2048]{1,0:T(8,128)(2,1)} %param.18) | copy-start | bytes 6291460
Sparse Core Ops, SparseCore 0:
  173.4 41.6 all-gather.1
